TPU v7x, 768 devices: a whole 4x8x12 slice. The times are simulated.
768 devices in a mesh: seq: 96 (over z, y), head: 8 (over x, core).
Axes of the slice: x: 4, y: 8, z: 12, core: 2. Of those that a mesh axis runs over, the one named last changes fastest.
Arguments:
- queries: bfloat16 [12288, 8192], P('seq', 'head'), may hold values from -6 to 6
- key_rows: bfloat16 [12288, 8192], P('seq', 'head'), may hold values from -6 to 6
- value_rows: bfloat16 [12288, 8192], P('seq', 'head'), may hold values from -64 to 64
- out_grad: bfloat16 [12288, 8192], P('seq', 'head'), may hold values from -6 to 6
- norm_gain: float32 [8192], P('head'), may hold values from 0.1 to 1.9
- dial_start: int32 [12288], P('seq'), may hold values from 0 to 12287, as said below
- dial_end: int32 [12288], P('seq'), may hold values from 1 to 12288
Outputs:
- normed: bfloat16 [12288, 8192], P('seq', 'head')
- query_grad: bfloat16 [12288, 8192], P('seq', 'head')
- key_grad: bfloat16 [12288, 8192], P('seq', 'head')
- value_grad: bfloat16 [12288, 8192], P('seq', 'head')
Inputs may be any that keep to these rules, and one draw needn't show every extreme that they name: Tokens of one dialogue are consecutive: dial_start gives the first token of a token's dialogue and dial_end one past its last; every dialogue holds 1 to 512 tokens and one holds exactly 512; the last token forms a dialogue of its own.
All inputs are finite; a program needn't handle non-finite values.
Results may differ from a plain program's by a relative error of at most 0.007.
Values sent between devices are 32-bit elements; how exact they have to be, the bound alone decides.
A program may use at most 128 MiB of HBM per device.

v0:
```python
import jax
import jax.numpy as jnp
from jax import lax
from jax.sharding import PartitionSpec as P

HEADS = 64
HD = 128
SPAN = 4


EPSILON = 1e-06


def from_behind(x, axis, by):
    count = lax.axis_size(axis)
    pairs = [(i, i + by) for i in range(count) if 0 <= i + by < count]
    return lax.ppermute(x, axis, pairs)


def join_states(earlier_part, later_part):
    return (
        later_part[0] + (1.0 - later_part[1]) * earlier_part[0],
        jnp.maximum(earlier_part[1], later_part[1]),
    )


def split_state(state):
    upper = state.astype(jnp.bfloat16)
    lower = (state - upper.astype(jnp.float32)).astype(jnp.bfloat16)
    return (upper, lower)


def state_product(form, rows, state):
    upper, lower = split_state(state)
    first = jnp.einsum(form, rows, upper, preferred_element_type=jnp.float32)
    return first + jnp.einsum(form, rows, lower, preferred_element_type=jnp.float32)


def shards(queries, key_rows, value_rows, out_grad, norm_gain, dial_start, dial_end):
    token_count = queries.shape[0]
    head_count = queries.shape[1] // HD
    score_scale = HD ** (-0.5)
    width_all = HEADS * HD
    block_begin = lax.axis_index("seq") * token_count
    local_pos = jnp.arange(token_count, dtype=jnp.int32)
    position = block_begin + local_pos
    query_h = queries.reshape(token_count, head_count, HD)
    key_h = key_rows.reshape(token_count, head_count, HD)
    value_h = value_rows.reshape(token_count, head_count, HD)
    distances = [1] + [1 << power for power in range((SPAN - 1).bit_length())]
    last_start = dial_start[token_count - 1]
    keep_last = position >= last_start
    element = jnp.einsum(
        "shd,she->hde",
        jnp.where(keep_last[:, None, None], key_h, jnp.zeros((), jnp.bfloat16)),
        value_h,
        preferred_element_type=jnp.float32,
    )
    reset_flag = (last_start >= block_begin).astype(jnp.float32)
    current = (element, reset_flag)
    for turn_index, distance in enumerate(distances):
        arrived = from_behind((current[0], current[1]), "seq", distance)
        current = arrived if turn_index == 0 else join_states(arrived, current)
    carried = current[0]
    inside = (position[None, :] >= dial_start[:, None]) & (local_pos[None, :] <= local_pos[:, None])
    scores = jnp.einsum("thd,shd->hts", query_h, key_h, preferred_element_type=jnp.float32)
    weights = jnp.where(inside[None], score_scale * scores, 0.0).astype(jnp.bfloat16)
    local_mix = jnp.einsum("hts,she->the", weights, value_h, preferred_element_type=jnp.float32)
    across = score_scale * state_product("thd,hde->the", query_h, carried)
    from_before = (dial_start < block_begin).astype(jnp.float32)[:, None, None]
    attended = (local_mix + from_before * across).reshape(token_count, head_count * HD)
    grad_wide = out_grad.astype(jnp.float32)
    square_sum, cross_sum = lax.psum(
        (jnp.sum(attended * attended, axis=1), jnp.sum(norm_gain * grad_wide * attended, axis=1)),
        "head",
    )
    inv_rms = lax.rsqrt(square_sum / width_all + EPSILON)
    normed = (attended * inv_rms[:, None] * norm_gain).astype(jnp.bfloat16)
    grad_attn = (
        inv_rms[:, None] * norm_gain * grad_wide
        - attended * (inv_rms * inv_rms * inv_rms * cross_sum / width_all)[:, None]
    )
    grad_weight = grad_attn.astype(jnp.bfloat16).reshape(token_count, head_count, HD)
    first_end = dial_end[0]
    keep_first = position < first_end
    back_element = jnp.einsum(
        "thd,the->hde",
        jnp.where(keep_first[:, None, None], query_h, jnp.zeros((), jnp.bfloat16)),
        grad_weight,
        preferred_element_type=jnp.float32,
    )
    back_reset = (first_end <= block_begin + token_count).astype(jnp.float32)
    current = (back_element, back_reset)
    for turn_index, distance in enumerate(distances):
        arrived = from_behind((current[0], current[1]), "seq", -distance)
        current = arrived if turn_index == 0 else join_states(arrived, current)
    returned = current[0]
    grad_scores = jnp.einsum(
        "the,she->hts", grad_weight, value_h, preferred_element_type=jnp.float32
    )
    grad_mix = jnp.where(inside[None], score_scale * grad_scores, 0.0).astype(jnp.bfloat16)
    to_after = (dial_end > block_begin + token_count).astype(jnp.float32)[:, None, None]
    query_grad = jnp.einsum(
        "hts,shd->thd", grad_mix, key_h, preferred_element_type=jnp.float32
    ) + from_before * score_scale * state_product("the,hde->thd", grad_weight, carried)
    key_grad = jnp.einsum(
        "hts,thd->shd", grad_mix, query_h, preferred_element_type=jnp.float32
    ) + to_after * score_scale * state_product("she,hde->shd", value_h, returned)
    value_grad = jnp.einsum(
        "hts,the->she", weights, grad_weight, preferred_element_type=jnp.float32
    ) + to_after * score_scale * state_product("shd,hde->she", key_h, returned)
    flat_shape = (token_count, head_count * HD)
    return (
        normed,
        query_grad.reshape(flat_shape).astype(jnp.bfloat16),
        key_grad.reshape(flat_shape).astype(jnp.bfloat16),
        value_grad.reshape(flat_shape).astype(jnp.bfloat16),
    )


def solution(mesh):
    placed = (
        P("seq", "head"),
        P("seq", "head"),
        P("seq", "head"),
        P("seq", "head"),
        P("head"),
        P("seq"),
        P("seq"),
    )
    return jax.shard_map(
        shards,
        mesh=mesh,
        in_specs=placed,
        out_specs=(P("seq", "head"), P("seq", "head"), P("seq", "head"), P("seq", "head")),
        check_vma=False,
    )
```

profile of v0, /device:TPU:248, one launch (start us, length us, event | category | flops | bytes accessed | tf_op | source)
XLA Modules:
  0.0 150.6 jit_solution(10471406803976047535)
XLA Ops:
  0.6 0.0 copy-start
  0.7 0.0 copy-start.5
  0.7 0.7 copy-done.5
  1.4 0.6 slice.6
  1.9 1.0 copy.49
  2.9 0.2 copy.14
  3.2 0.7 broadcast_compare_fusion.1
  3.8 0.0 copy-done
  3.8 0.2 fusion.27
  4.1 4.7 %collective-permute-start = (f32[8,128,128]{2,1,0:T(8,128)S(1)}, f32[8,128,128]{2,1,0:T(8,128)S(1)}, u32[]{:S(2)}, u32[]{:S(2)}) collective-permute-start(f32[8,128,128]{2,1,0:T(8,128)S(1)} %fusion.27), channel_id=1, source_target_pairs={{0,8},{8,16},{16,24},{24,32},{32,40},{40,48},{48,56},{56,64},{64,7... | collective-permute-start | bytes 1572872 | tf_op jit(solution)/shard_map/ppermute | solution.py:17
  8.8 11.2 %collective-permute-done = f32[8,128,128]{2,1,0:T(8,128)S(1)} collective-permute-done((f32[8,128,128]{2,1,0:T(8,128)S(1)}, f32[8,128,128]{2,1,0:T(8,128)S(1)}, u32[]{:S(2)}, u32[]{:S(2)}) %collective-permute-start) | collective-permute-done | bytes 524320 | tf_op jit(solution)/shard_map/ppermute | solution.py:17
  19.9 7.7 %collective-permute-start.2 = (f32[8,128,128]{2,1,0:T(8,128)S(1)}, f32[8,128,128]{2,1,0:T(8,128)S(1)}, u32[]{:S(2)}, u32[]{:S(2)}) collective-permute-start(f32[8,128,128]{2,1,0:T(8,128)S(1)} %collective-permute-done), channel_id=1, source_target_pairs={{0,8},{8,16},{16,24},{24,32},{32,40},{40,48},{48,56},{56,64},{64,7... | collective-permute-start | bytes 1572872 | tf_op jit(solution)/shard_map/ppermute | solution.py:17
  28.3 9.7 %collective-permute-start.1 = (f32[]{:T(128)}, f32[]{:T(128)}, u32[]{:S(2)}, u32[]{:S(2)}) collective-permute-start(f32[]{:T(128)} %convert_element_type.69), channel_id=1, source_target_pairs={{0,8},{8,16},{16,24},{24,32},{32,40},{40,48},{48,56},{56,64},{64,7... | collective-permute-start | bytes 20 | tf_op jit(solution)/shard_map/ppermute | solution.py:17
  38.6 0.0 copy-start.3
  38.6 0.0 collective-permute-done.2
  38.6 0.1 multiply_add_fusion.3
  38.7 4.1 %collective-permute-start.4 = (f32[8,128,128]{2,1,0:T(8,128)S(1)}, f32[8,128,128]{2,1,0:T(8,128)S(1)}, u32[]{:S(2)}, u32[]{:S(2)}) collective-permute-start(f32[8,128,128]{2,1,0:T(8,128)S(1)} %multiply_add_fusion.3), channel_id=1, source_target_pairs={{0,16},{8,24},{16,32},{24,40},{32,48},{40,56},{48,64},{56,72},{64,... | collective-permute-start | bytes 1572872 | tf_op jit(solution)/shard_map/ppermute | solution.py:17
  42.8 0.0 copy-start.6
  42.8 0.6 copy-done.6
  43.5 0.0 copy-done.3
  43.5 0.0 copy-start.1
  43.5 0.2 copy.45
  43.7 0.1 fusion.50
  43.8 0.7 copy-done.1
  44.4 0.3 fusion.14
  44.8 5.5 %collective-permute-start.3 = (f32[]{:T(128)}, f32[]{:T(128)}, u32[]{:S(2)}, u32[]{:S(2)}) collective-permute-start(f32[]{:T(128)} %collective-permute-done.1), channel_id=1, source_target_pairs={{0,8},{8,16},{16,24},{24,32},{32,40},{40,48},{48,56},{56,64},{64,7... | collective-permute-start | bytes 20 | tf_op jit(solution)/shard_map/ppermute | solution.py:17
  50.3 6.7 %collective-permute-done.3 = f32[]{:T(128)} collective-permute-done((f32[]{:T(128)}, f32[]{:T(128)}, u32[]{:S(2)}, u32[]{:S(2)}) %collective-permute-start.3) | collective-permute-done | bytes 36 | tf_op jit(solution)/shard_map/ppermute | solution.py:17
  58.2 7.2 %collective-permute-done.4 = f32[8,128,128]{2,1,0:T(8,128)S(1)} collective-permute-done((f32[8,128,128]{2,1,0:T(8,128)S(1)}, f32[8,128,128]{2,1,0:T(8,128)S(1)}, u32[]{:S(2)}, u32[]{:S(2)}) %collective-permute-start.4) | collective-permute-done | bytes 524320 | tf_op jit(solution)/shard_map/ppermute | solution.py:17
  65.5 0.1 subtract_convert_fusion.1
  65.6 0.3 fusion.57
  65.9 0.3 fusion.11
  66.2 0.3 multiply_reduce_fusion
  66.5 0.0 copy-start.4
  66.5 0.2 copy.20
  66.7 0.7 copy-done.2
  67.5 0.2 fusion.21
  67.6 12.4 %all-reduce = (f32[128]{0:T(128)S(1)}, f32[128]{0:T(128)S(1)}) all-reduce(f32[128]{0:T(128)S(1)} %get-tuple-element.18, f32[128]{0:T(128)S(1)} %fusion.21), channel_id=1, replica_groups=mesh['seq'=96,'head'=8] {'head'}, use_global_device_ids=true, to_apply=%region_1.2 | all-reduce | flops 256 | bytes 2048 | tf_op jit(solution)/shard_map/psum | solution.py:73
  80.1 0.9 fusion.19
  81.0 0.2 copy.46
  81.1 1.1 fusion.33
  82.2 3.7 %collective-permute-start.5 = (f32[8,128,128]{2,1,0:T(8,128)}, f32[8,128,128]{2,1,0:T(8,128)S(1)}, u32[]{:S(2)}, u32[]{:S(2)}) collective-permute-start(f32[8,128,128]{2,1,0:T(8,128)} %fusion.33), channel_id=1, source_target_pairs={{8,0},{16,8},{24,16},{32,24},{40,32},{48,40},{56,48},{64,56},{72,6... | collective-permute-start | bytes 1572872 | tf_op jit(solution)/shard_map/ppermute | solution.py:17
  85.9 11.5 %collective-permute-start.6 = (f32[]{:T(128)}, f32[]{:T(128)}, u32[]{:S(2)}, u32[]{:S(2)}) collective-permute-start(f32[]{:T(128)} %convert_element_type.79), channel_id=1, source_target_pairs={{8,0},{16,8},{24,16},{32,24},{40,32},{48,40},{56,48},{64,56},{72,6... | collective-permute-start | bytes 20 | tf_op jit(solution)/shard_map/ppermute | solution.py:17
  97.4 3.9 %collective-permute-done.5 = f32[8,128,128]{2,1,0:T(8,128)S(1)} collective-permute-done((f32[8,128,128]{2,1,0:T(8,128)}, f32[8,128,128]{2,1,0:T(8,128)S(1)}, u32[]{:S(2)}, u32[]{:S(2)}) %collective-permute-start.5) | collective-permute-done | bytes 524320 | tf_op jit(solution)/shard_map/ppermute | solution.py:17
  101.3 1.9 %collective-permute-start.7 = (f32[8,128,128]{2,1,0:T(8,128)S(1)}, f32[8,128,128]{2,1,0:T(8,128)}, u32[]{:S(2)}, u32[]{:S(2)}) collective-permute-start(f32[8,128,128]{2,1,0:T(8,128)S(1)} %collective-permute-done.5), channel_id=1, source_target_pairs={{8,0},{16,8},{24,16},{32,24},{40,32},{48,40},{56,48},{64,56},{72,6... | collective-permute-start | bytes 1572872 | tf_op jit(solution)/shard_map/ppermute | solution.py:17
  103.8 1.9 %collective-permute-start.8 = (f32[]{:T(128)}, f32[]{:T(128)}, u32[]{:S(2)}, u32[]{:S(2)}) collective-permute-start(f32[]{:T(128)} %collective-permute-done.6), channel_id=1, source_target_pairs={{8,0},{16,8},{24,16},{32,24},{40,32},{48,40},{56,48},{64,56},{72,6... | collective-permute-start | bytes 20 | tf_op jit(solution)/shard_map/ppermute | solution.py:17
  105.8 13.7 %collective-permute-done.8 = f32[]{:T(128)} collective-permute-done((f32[]{:T(128)}, f32[]{:T(128)}, u32[]{:S(2)}, u32[]{:S(2)}) %collective-permute-start.8) | collective-permute-done | bytes 36 | tf_op jit(solution)/shard_map/ppermute | solution.py:17
  120.7 0.2 fusion.58
  120.9 0.2 fusion.8
  121.1 0.0 collective-permute-done.7
  121.1 1.1 multiply_add_fusion.1
  122.2 1.9 %collective-permute-start.9 = (f32[8,128,128]{2,1,0:T(8,128)S(1)}, f32[8,128,128]{2,1,0:T(8,128)S(1)}, u32[]{:S(2)}, u32[]{:S(2)}) collective-permute-start(f32[8,128,128]{2,1,0:T(8,128)S(1)} %multiply_add_fusion.1), channel_id=1, source_target_pairs={{16,0},{24,8},{32,16},{40,24},{48,32},{56,40},{64,48},{72,56},{80,... | collective-permute-start | bytes 1572872 | tf_op jit(solution)/shard_map/ppermute | solution.py:17
  124.1 0.3 fusion.15
  124.5 0.3 fusion.17
  124.8 0.9 copy.38
  125.6 0.2 fusion.59
  125.9 21.4 %collective-permute-done.9 = f32[8,128,128]{2,1,0:T(8,128)S(1)} collective-permute-done((f32[8,128,128]{2,1,0:T(8,128)S(1)}, f32[8,128,128]{2,1,0:T(8,128)S(1)}, u32[]{:S(2)}, u32[]{:S(2)}) %collective-permute-start.9) | collective-permute-done | bytes 524320 | tf_op jit(solution)/shard_map/ppermute | solution.py:17
  147.3 0.1 subtract_convert_fusion
  147.4 0.3 fusion.29
  147.8 0.3 fusion.23
  148.1 0.3 fusion.13
  148.4 0.9 copy.40
  149.2 0.3 fusion.6
  149.6 0.2 fusion.16
  149.8 0.9 copy.39
  (9 shorter events, 0.1 us)
Async XLA Ops:
  0.6 3.2 %copy-start = (bf16[128,1024]{1,0:T(8,128)(2,1)S(1)}, bf16[128,1024]{1,0:T(8,128)(2,1)}, u32[]{:S(2)}) copy-start(bf16[128,1024]{1,0:T(8,128)(2,1)} %param.9) | copy-start | bytes 786436
  0.7 0.7 copy-start.5
  4.1 15.9 %collective-permute-start = (f32[8,128,128]{2,1,0:T(8,128)S(1)}, f32[8,128,128]{2,1,0:T(8,128)S(1)}, u32[]{:S(2)}, u32[]{:S(2)}) collective-permute-start(f32[8,128,128]{2,1,0:T(8,128)S(1)} %fusion.27), channel_id=1, source_target_pairs={{0,8},{8,16},{16,24},{24,32},{32,40},{40,48},{48,56},{56,64},{64,7... | collective-permute-start | bytes 1572872 | tf_op jit(solution)/shard_map/ppermute | solution.py:17
  19.9 18.7 %collective-permute-start.2 = (f32[8,128,128]{2,1,0:T(8,128)S(1)}, f32[8,128,128]{2,1,0:T(8,128)S(1)}, u32[]{:S(2)}, u32[]{:S(2)}) collective-permute-start(f32[8,128,128]{2,1,0:T(8,128)S(1)} %collective-permute-done), channel_id=1, source_target_pairs={{0,8},{8,16},{16,24},{24,32},{32,40},{40,48},{48,56},{56,64},{64,7... | collective-permute-start | bytes 1572872 | tf_op jit(solution)/shard_map/ppermute | solution.py:17
  28.3 9.7 %collective-permute-start.1 = (f32[]{:T(128)}, f32[]{:T(128)}, u32[]{:S(2)}, u32[]{:S(2)}) collective-permute-start(f32[]{:T(128)} %convert_element_type.69), channel_id=1, source_target_pairs={{0,8},{8,16},{16,24},{24,32},{32,40},{40,48},{48,56},{56,64},{64,7... | collective-permute-start | bytes 20 | tf_op jit(solution)/shard_map/ppermute | solution.py:17
  38.6 4.9 %copy-start.3 = (bf16[128,1024]{1,0:T(8,128)(2,1)S(1)}, bf16[128,1024]{1,0:T(8,128)(2,1)}, u32[]{:S(2)}) copy-start(bf16[128,1024]{1,0:T(8,128)(2,1)} %param.7) | copy-start | bytes 786436
  38.7 26.8 %collective-permute-start.4 = (f32[8,128,128]{2,1,0:T(8,128)S(1)}, f32[8,128,128]{2,1,0:T(8,128)S(1)}, u32[]{:S(2)}, u32[]{:S(2)}) collective-permute-start(f32[8,128,128]{2,1,0:T(8,128)S(1)} %multiply_add_fusion.3), channel_id=1, source_target_pairs={{0,16},{8,24},{16,32},{24,40},{32,48},{40,56},{48,64},{56,72},{64,... | collective-permute-start | bytes 1572872 | tf_op jit(solution)/shard_map/ppermute | solution.py:17
  42.8 0.7 copy-start.6
  43.5 1.0 copy-start.1
  44.8 12.2 %collective-permute-start.3 = (f32[]{:T(128)}, f32[]{:T(128)}, u32[]{:S(2)}, u32[]{:S(2)}) collective-permute-start(f32[]{:T(128)} %collective-permute-done.1), channel_id=1, source_target_pairs={{0,8},{8,16},{16,24},{24,32},{32,40},{40,48},{48,56},{56,64},{64,7... | collective-permute-start | bytes 20 | tf_op jit(solution)/shard_map/ppermute | solution.py:17
  66.5 1.0 copy-start.2
  66.5 1.0 copy-start.4
  82.2 19.1 %collective-permute-start.5 = (f32[8,128,128]{2,1,0:T(8,128)}, f32[8,128,128]{2,1,0:T(8,128)S(1)}, u32[]{:S(2)}, u32[]{:S(2)}) collective-permute-start(f32[8,128,128]{2,1,0:T(8,128)} %fusion.33), channel_id=1, source_target_pairs={{8,0},{16,8},{24,16},{32,24},{40,32},{48,40},{56,48},{64,56},{72,6... | collective-permute-start | bytes 1572872 | tf_op jit(solution)/shard_map/ppermute | solution.py:17
  85.9 17.3 %collective-permute-start.6 = (f32[]{:T(128)}, f32[]{:T(128)}, u32[]{:S(2)}, u32[]{:S(2)}) collective-permute-start(f32[]{:T(128)} %convert_element_type.79), channel_id=1, source_target_pairs={{8,0},{16,8},{24,16},{32,24},{40,32},{48,40},{56,48},{64,56},{72,6... | collective-permute-start | bytes 20 | tf_op jit(solution)/shard_map/ppermute | solution.py:17
  101.3 19.8 %collective-permute-start.7 = (f32[8,128,128]{2,1,0:T(8,128)S(1)}, f32[8,128,128]{2,1,0:T(8,128)}, u32[]{:S(2)}, u32[]{:S(2)}) collective-permute-start(f32[8,128,128]{2,1,0:T(8,128)S(1)} %collective-permute-done.5), channel_id=1, source_target_pairs={{8,0},{16,8},{24,16},{32,24},{40,32},{48,40},{56,48},{64,56},{72,6... | collective-permute-start | bytes 1572872 | tf_op jit(solution)/shard_map/ppermute | solution.py:17
  103.8 15.6 %collective-permute-start.8 = (f32[]{:T(128)}, f32[]{:T(128)}, u32[]{:S(2)}, u32[]{:S(2)}) collective-permute-start(f32[]{:T(128)} %collective-permute-done.6), channel_id=1, source_target_pairs={{8,0},{16,8},{24,16},{32,24},{40,32},{48,40},{56,48},{64,56},{72,6... | collective-permute-start | bytes 20 | tf_op jit(solution)/shard_map/ppermute | solution.py:17
  122.2 25.1 %collective-permute-start.9 = (f32[8,128,128]{2,1,0:T(8,128)S(1)}, f32[8,128,128]{2,1,0:T(8,128)S(1)}, u32[]{:S(2)}, u32[]{:S(2)}) collective-permute-start(f32[8,128,128]{2,1,0:T(8,128)S(1)} %multiply_add_fusion.1), channel_id=1, source_target_pairs={{16,0},{24,8},{32,16},{40,24},{48,32},{56,40},{64,48},{72,56},{80,... | collective-permute-start | bytes 1572872 | tf_op jit(solution)/shard_map/ppermute | solution.py:17
where the time goes:
time: 151 us
  waiting for transfers between devices  64.1 us (42%)
  starting transfers between devices  52.5 us (35%)
  blocking collectives  12.4 us (8%)
  local copies, waits for them, and re-layouts  7.65 us (5%)
  matrix products  5.33 us (4%)
  between operations  5.26 us (3%)
  other arithmetic  3.28 us (2%)
    ppermute x10, waiting for transfers between devices, from_behind(): return lax.ppermute(x, axis, pairs)  64.1 us
    ppermute x10, starting transfers between devices, from_behind(): return lax.ppermute(x, axis, pairs)  52.5 us
    psum x1, blocking collectives, shards(): lax.psum((jnp.sum(attended * attended, axis=1), jnp.sum(norm_gain * grad_...  12.4 us
    unnamed x18, local copies, waits for them, and re-layouts  6.31 us
  transfers between devices with their start and end apart: 10, of which 6 were waited for; matrix products, arithmetic and copies ran while one was open for 2% of the time, Pallas kernels for 0%

commit v1 on v0

--- a/solution.py
+++ b/solution.py
@@ -15,6 +15,15 @@
     count = lax.axis_size(axis)
     pairs = [(i, i + by) for i in range(count) if 0 <= i + by < count]
     return lax.ppermute(x, axis, pairs)
+
+
+def scan_window(element, reach, step):
+    nearest = from_behind(element, "seq", step)
+    second = from_behind(nearest, "seq", step)
+    pair = nearest + (reach >= 2).astype(jnp.float32) * second
+    far_pair = from_behind(pair, "seq", 2 * step)
+    total = pair + (reach >= 3).astype(jnp.float32) * far_pair
+    return (reach >= 1).astype(jnp.float32) * total
 
 
 def join_states(earlier_part, later_part):
@@ -47,7 +56,6 @@
     query_h = queries.reshape(token_count, head_count, HD)
     key_h = key_rows.reshape(token_count, head_count, HD)
     value_h = value_rows.reshape(token_count, head_count, HD)
-    distances = [1] + [1 << power for power in range((SPAN - 1).bit_length())]
     last_start = dial_start[token_count - 1]
     keep_last = position >= last_start
     element = jnp.einsum(
@@ -56,12 +64,9 @@
         value_h,
         preferred_element_type=jnp.float32,
     )
-    reset_flag = (last_start >= block_begin).astype(jnp.float32)
-    current = (element, reset_flag)
-    for turn_index, distance in enumerate(distances):
-        arrived = from_behind((current[0], current[1]), "seq", distance)
-        current = arrived if turn_index == 0 else join_states(arrived, current)
-    carried = current[0]
+    block_index = lax.axis_index("seq")
+    reach_back = block_index - dial_start[0] // token_count
+    carried = scan_window(element, reach_back, 1)
     inside = (position[None, :] >= dial_start[:, None]) & (local_pos[None, :] <= local_pos[:, None])
     scores = jnp.einsum("thd,shd->hts", query_h, key_h, preferred_element_type=jnp.float32)
     weights = jnp.where(inside[None], score_scale * scores, 0.0).astype(jnp.bfloat16)
@@ -89,12 +94,8 @@
         grad_weight,
         preferred_element_type=jnp.float32,
     )
-    back_reset = (first_end <= block_begin + token_count).astype(jnp.float32)
-    current = (back_element, back_reset)
-    for turn_index, distance in enumerate(distances):
-        arrived = from_behind((current[0], current[1]), "seq", -distance)
-        current = arrived if turn_index == 0 else join_states(arrived, current)
-    returned = current[0]
+    reach_ahead = (dial_end[token_count - 1] + token_count - 1) // token_count - 1 - block_index
+    returned = scan_window(back_element, reach_ahead, -1)
     grad_scores = jnp.einsum(
         "the,she->hts", grad_weight, value_h, preferred_element_type=jnp.float32
     )

time: 151 us -> 149 us (0.987)
  starting transfers between devices: 52.5 us -> 22.3 us
  waiting for transfers between devices: 64.1 us -> 92.4 us
  other arithmetic: 3.28 us -> 5.11 us
    ppermute x10 -> x6, starting transfers between devices: 52.5 us -> 22.3 us  [from_behind(): return lax.ppermute(x, axis, pairs)]
    ppermute x10 -> x6, waiting for transfers between devices: 64.1 us -> 92.4 us  [from_behind(): return lax.ppermute(x, axis, pairs)]
    unnamed x18 -> x20, local copies, waits for them, and re-layouts: 6.31 us -> 6.08 us
  transfers between devices with their start and end apart: 10 -> 6, of which waited for: 6 -> 6; matrix products, arithmetic and copies ran while one was open for 2% -> 3% of each run, Pallas kernels for 0% -> 0%
where the time goes in v1:
time: 149 us
  waiting for transfers between devices  92.4 us (62%)
  starting transfers between devices  22.3 us (15%)
  blocking collectives  12.4 us (8%)
  local copies, waits for them, and re-layouts  8 us (5%)
  other arithmetic  5.11 us (3%)
  matrix products  4.53 us (3%)
  between operations  4.21 us (3%)
    ppermute x6, waiting for transfers between devices, from_behind(): return lax.ppermute(x, axis, pairs)  92.4 us
    ppermute x6, starting transfers between devices, from_behind(): return lax.ppermute(x, axis, pairs)  22.3 us
    psum x1, blocking collectives, shards(): lax.psum((jnp.sum(attended * attended, axis=1), jnp.sum(norm_gain * grad_...  12.4 us
    unnamed x20, local copies, waits for them, and re-layouts  6.08 us
  transfers between devices with their start and end apart: 6, of which 6 were waited for; matrix products, arithmetic and copies ran while one was open for 3% of the time, Pallas kernels for 0%

profile of v1, /device:TPU:248, one launch (start us, length us, event | category | flops | bytes accessed | tf_op | source)
XLA Modules:
  0.0 149.0 jit_solution(5555925062345213861)
XLA Ops:
  0.6 0.0 copy-start
  0.6 1.0 copy.49
  1.7 0.0 copy-start.6
  1.7 0.2 copy.14
  1.9 0.4 copy-done.6
  2.4 0.6 fusion.58
  2.9 0.7 broadcast_compare_fusion.1
  3.6 0.0 copy-done
  3.6 0.2 fusion.27
  3.8 4.7 %collective-permute-start = (f32[8,128,128]{2,1,0:T(8,128)S(1)}, f32[8,128,128]{2,1,0:T(8,128)S(1)}, u32[]{:S(2)}, u32[]{:S(2)}) collective-permute-start(f32[8,128,128]{2,1,0:T(8,128)S(1)} %fusion.27), channel_id=1, source_target_pairs={{0,8},{8,16},{16,24},{24,32},{32,40},{40,48},{48,56},{56,64},{64,7... | collective-permute-start | bytes 1572872 | tf_op jit(solution)/shard_map/ppermute | solution.py:17
  8.5 11.2 %collective-permute-done = f32[8,128,128]{2,1,0:T(8,128)S(1)} collective-permute-done((f32[8,128,128]{2,1,0:T(8,128)S(1)}, f32[8,128,128]{2,1,0:T(8,128)S(1)}, u32[]{:S(2)}, u32[]{:S(2)}) %collective-permute-start) | collective-permute-done | bytes 524320 | tf_op jit(solution)/shard_map/ppermute | solution.py:17
  19.7 7.7 %collective-permute-start.1 = (f32[8,128,128]{2,1,0:T(8,128)S(1)}, f32[8,128,128]{2,1,0:T(8,128)S(1)}, u32[]{:S(2)}, u32[]{:S(2)}) collective-permute-start(f32[8,128,128]{2,1,0:T(8,128)S(1)} %collective-permute-done), channel_id=1, source_target_pairs={{0,8},{8,16},{16,24},{24,32},{32,40},{40,48},{48,56},{56,64},{64,7... | collective-permute-start | bytes 1572872 | tf_op jit(solution)/shard_map/ppermute | solution.py:17
  30.0 0.0 copy-start.7
  30.0 0.6 copy-done.7
  30.7 0.6 fusion.57
  31.2 0.0 copy-start.4
  31.2 6.4 %collective-permute-done.1 = f32[8,128,128]{2,1,0:T(8,128)S(1)} collective-permute-done((f32[8,128,128]{2,1,0:T(8,128)S(1)}, f32[8,128,128]{2,1,0:T(8,128)S(1)}, u32[]{:S(2)}, u32[]{:S(2)}) %collective-permute-start.1) | collective-permute-done | bytes 524320 | tf_op jit(solution)/shard_map/ppermute | solution.py:17
  37.7 0.1 multiply_add_fusion.1
  37.7 4.1 %collective-permute-start.2 = (f32[8,128,128]{2,1,0:T(8,128)S(1)}, f32[8,128,128]{2,1,0:T(8,128)S(1)}, u32[]{:S(2)}, u32[]{:S(2)}) collective-permute-start(f32[8,128,128]{2,1,0:T(8,128)S(1)} %multiply_add_fusion.1), channel_id=1, source_target_pairs={{0,16},{8,24},{16,32},{24,40},{32,48},{40,56},{48,64},{56,72},{64,... | collective-permute-start | bytes 1572872 | tf_op jit(solution)/shard_map/ppermute | solution.py:17
  41.9 0.7 broadcast_compare_fusion
  42.5 0.0 copy-done.4
  42.5 0.0 copy-start.1
  42.6 0.2 copy.45
  42.7 0.1 fusion.50
  42.8 0.7 copy-done.1
  43.5 0.3 fusion.14
  43.8 20.7 %collective-permute-done.2 = f32[8,128,128]{2,1,0:T(8,128)S(1)} collective-permute-done((f32[8,128,128]{2,1,0:T(8,128)S(1)}, f32[8,128,128]{2,1,0:T(8,128)S(1)}, u32[]{:S(2)}, u32[]{:S(2)}) %collective-permute-start.2) | collective-permute-done | bytes 524320 | tf_op jit(solution)/shard_map/ppermute | solution.py:17
  64.5 0.1 subtract_convert_fusion.1
  64.7 0.3 fusion.59
  65.0 0.3 fusion.11
  65.3 0.4 multiply_reduce_fusion
  65.6 0.0 copy-start.2
  65.6 0.0 copy-start.5
  65.6 0.2 copy.20
  65.8 0.7 copy-done.2
  66.6 0.0 copy-done.5
  66.6 0.2 fusion.21
  66.7 12.4 %all-reduce = (f32[128]{0:T(128)S(1)}, f32[128]{0:T(128)S(1)}) all-reduce(f32[128]{0:T(128)S(1)} %get-tuple-element.22, f32[128]{0:T(128)S(1)} %fusion.21), channel_id=1, replica_groups=mesh['seq'=96,'head'=8] {'head'}, use_global_device_ids=true, to_apply=%region_1.2 | all-reduce | flops 256 | bytes 2048 | tf_op jit(solution)/shard_map/psum | solution.py:78
  79.2 0.9 fusion.19
  80.1 0.2 copy.46
  80.2 0.3 fusion.33
  80.6 1.9 %collective-permute-start.3 = (f32[8,128,128]{2,1,0:T(8,128)S(1)}, f32[8,128,128]{2,1,0:T(8,128)S(1)}, u32[]{:S(2)}, u32[]{:S(2)}) collective-permute-start(f32[8,128,128]{2,1,0:T(8,128)S(1)} %fusion.33), channel_id=1, source_target_pairs={{8,0},{16,8},{24,16},{32,24},{40,32},{48,40},{56,48},{64,56},{72,6... | collective-permute-start | bytes 1572872 | tf_op jit(solution)/shard_map/ppermute | solution.py:17
  82.5 17.0 %collective-permute-done.3 = f32[8,128,128]{2,1,0:T(8,128)S(1)} collective-permute-done((f32[8,128,128]{2,1,0:T(8,128)S(1)}, f32[8,128,128]{2,1,0:T(8,128)S(1)}, u32[]{:S(2)}, u32[]{:S(2)}) %collective-permute-start.3) | collective-permute-done | bytes 524320 | tf_op jit(solution)/shard_map/ppermute | solution.py:17
  99.5 0.0 copy-start.3
  99.5 1.9 %collective-permute-start.4 = (f32[8,128,128]{2,1,0:T(8,128)S(1)}, f32[8,128,128]{2,1,0:T(8,128)}, u32[]{:S(2)}, u32[]{:S(2)}) collective-permute-start(f32[8,128,128]{2,1,0:T(8,128)S(1)} %collective-permute-done.3), channel_id=1, source_target_pairs={{8,0},{16,8},{24,16},{32,24},{40,32},{48,40},{56,48},{64,56},{72,6... | collective-permute-start | bytes 1572872 | tf_op jit(solution)/shard_map/ppermute | solution.py:17
  102.1 0.2 fusion.60
  102.3 0.0 copy-done.3
  102.3 0.2 fusion.8
  102.5 15.1 %collective-permute-done.4 = f32[8,128,128]{2,1,0:T(8,128)} collective-permute-done((f32[8,128,128]{2,1,0:T(8,128)S(1)}, f32[8,128,128]{2,1,0:T(8,128)}, u32[]{:S(2)}, u32[]{:S(2)}) %collective-permute-start.4) | collective-permute-done | bytes 524320 | tf_op jit(solution)/shard_map/ppermute | solution.py:17
  117.6 1.3 multiply_add_fusion
  118.8 1.9 %collective-permute-start.5 = (f32[8,128,128]{2,1,0:T(8,128)S(1)}, f32[8,128,128]{2,1,0:T(8,128)}, u32[]{:S(2)}, u32[]{:S(2)}) collective-permute-start(f32[8,128,128]{2,1,0:T(8,128)S(1)} %multiply_add_fusion), channel_id=1, source_target_pairs={{16,0},{24,8},{32,16},{40,24},{48,32},{56,40},{64,48},{72,56},{80,... | collective-permute-start | bytes 1572872 | tf_op jit(solution)/shard_map/ppermute | solution.py:17
  120.8 0.3 fusion.15
  121.1 0.3 fusion.17
  121.4 0.9 copy.38
  122.3 0.2 fusion.61
  122.5 22.1 %collective-permute-done.5 = f32[8,128,128]{2,1,0:T(8,128)} collective-permute-done((f32[8,128,128]{2,1,0:T(8,128)S(1)}, f32[8,128,128]{2,1,0:T(8,128)}, u32[]{:S(2)}, u32[]{:S(2)}) %collective-permute-start.5) | collective-permute-done | bytes 524320 | tf_op jit(solution)/shard_map/ppermute | solution.py:17
  144.6 1.2 subtract_convert_fusion
  145.8 0.3 fusion.23
  146.0 0.3 fusion.29
  146.4 0.3 fusion.6
  146.7 0.2 fusion.16
  146.9 0.9 copy.39
  147.8 0.3 fusion.13
  148.1 0.9 copy.40
  (4 shorter events, 0.0 us)
Async XLA Ops:
  0.6 3.0 %copy-start = (bf16[128,1024]{1,0:T(8,128)(2,1)S(1)}, bf16[128,1024]{1,0:T(8,128)(2,1)}, u32[]{:S(2)}) copy-start(bf16[128,1024]{1,0:T(8,128)(2,1)} %param.9) | copy-start | bytes 786436
  1.7 0.7 copy-start.6
  3.8 15.9 %collective-permute-start = (f32[8,128,128]{2,1,0:T(8,128)S(1)}, f32[8,128,128]{2,1,0:T(8,128)S(1)}, u32[]{:S(2)}, u32[]{:S(2)}) collective-permute-start(f32[8,128,128]{2,1,0:T(8,128)S(1)} %fusion.27), channel_id=1, source_target_pairs={{0,8},{8,16},{16,24},{24,32},{32,40},{40,48},{48,56},{56,64},{64,7... | collective-permute-start | bytes 1572872 | tf_op jit(solution)/shard_map/ppermute | solution.py:17
  19.7 18.0 %collective-permute-start.1 = (f32[8,128,128]{2,1,0:T(8,128)S(1)}, f32[8,128,128]{2,1,0:T(8,128)S(1)}, u32[]{:S(2)}, u32[]{:S(2)}) collective-permute-start(f32[8,128,128]{2,1,0:T(8,128)S(1)} %collective-permute-done), channel_id=1, source_target_pairs={{0,8},{8,16},{16,24},{24,32},{32,40},{40,48},{48,56},{56,64},{64,7... | collective-permute-start | bytes 1572872 | tf_op jit(solution)/shard_map/ppermute | solution.py:17
  30.0 0.7 copy-start.7
  31.2 11.3 %copy-start.4 = (bf16[128,1024]{1,0:T(8,128)(2,1)S(1)}, bf16[128,1024]{1,0:T(8,128)(2,1)}, u32[]{:S(2)}) copy-start(bf16[128,1024]{1,0:T(8,128)(2,1)} %param.7) | copy-start | bytes 786436
  37.7 26.8 %collective-permute-start.2 = (f32[8,128,128]{2,1,0:T(8,128)S(1)}, f32[8,128,128]{2,1,0:T(8,128)S(1)}, u32[]{:S(2)}, u32[]{:S(2)}) collective-permute-start(f32[8,128,128]{2,1,0:T(8,128)S(1)} %multiply_add_fusion.1), channel_id=1, source_target_pairs={{0,16},{8,24},{16,32},{24,40},{32,48},{40,56},{48,64},{56,72},{64,... | collective-permute-start | bytes 1572872 | tf_op jit(solution)/shard_map/ppermute | solution.py:17
  42.5 1.0 copy-start.1
  65.6 1.0 copy-start.2
  65.6 1.0 copy-start.5
  80.6 18.9 %collective-permute-start.3 = (f32[8,128,128]{2,1,0:T(8,128)S(1)}, f32[8,128,128]{2,1,0:T(8,128)S(1)}, u32[]{:S(2)}, u32[]{:S(2)}) collective-permute-start(f32[8,128,128]{2,1,0:T(8,128)S(1)} %fusion.33), channel_id=1, source_target_pairs={{8,0},{16,8},{24,16},{32,24},{40,32},{48,40},{56,48},{64,56},{72,6... | collective-permute-start | bytes 1572872 | tf_op jit(solution)/shard_map/ppermute | solution.py:17
  99.5 2.8 %copy-start.3 = (f32[8,128,128]{2,1,0:T(8,128)}, f32[8,128,128]{2,1,0:T(8,128)S(1)}, u32[]{:S(2)}) copy-start(f32[8,128,128]{2,1,0:T(8,128)S(1)} %collective-permute-done.3) | copy-start | bytes 1572868
  99.5 18.1 %collective-permute-start.4 = (f32[8,128,128]{2,1,0:T(8,128)S(1)}, f32[8,128,128]{2,1,0:T(8,128)}, u32[]{:S(2)}, u32[]{:S(2)}) collective-permute-start(f32[8,128,128]{2,1,0:T(8,128)S(1)} %collective-permute-done.3), channel_id=1, source_target_pairs={{8,0},{16,8},{24,16},{32,24},{40,32},{48,40},{56,48},{64,56},{72,6... | collective-permute-start | bytes 1572872 | tf_op jit(solution)/shard_map/ppermute | solution.py:17
  118.8 25.7 %collective-permute-start.5 = (f32[8,128,128]{2,1,0:T(8,128)S(1)}, f32[8,128,128]{2,1,0:T(8,128)}, u32[]{:S(2)}, u32[]{:S(2)}) collective-permute-start(f32[8,128,128]{2,1,0:T(8,128)S(1)} %multiply_add_fusion), channel_id=1, source_target_pairs={{16,0},{24,8},{32,16},{40,24},{48,32},{56,40},{64,48},{72,56},{80,... | collective-permute-start | bytes 1572872 | tf_op jit(solution)/shard_map/ppermute | solution.py:17

commit v2 on v1

--- a/solution.py
+++ b/solution.py
@@ -1,6 +1,10 @@
+import functools
+
 import jax
 import jax.numpy as jnp
 from jax import lax
+from jax.experimental import pallas as pl
+from jax.experimental.pallas import tpu as pltpu
 from jax.sharding import PartitionSpec as P
 
 HEADS = 64
@@ -17,13 +21,77 @@
     return lax.ppermute(x, axis, pairs)
 
 
-def scan_window(element, reach, step):
-    nearest = from_behind(element, "seq", step)
-    second = from_behind(nearest, "seq", step)
-    pair = nearest + (reach >= 2).astype(jnp.float32) * second
-    far_pair = from_behind(pair, "seq", 2 * step)
-    total = pair + (reach >= 3).astype(jnp.float32) * far_pair
-    return (reach >= 1).astype(jnp.float32) * total
+def window_kernel(count, step, masks_ref, element_ref, out_ref, slots, send_sems, recv_sems):
+    me = lax.axis_index("seq")
+    head = lax.axis_index("head")
+
+    def inside_axis(offset):
+        return (me + offset >= 0) & (me + offset < count)
+
+    def peer(offset):
+        return (me + offset, head)
+
+    barrier = pltpu.get_barrier_semaphore()
+    offsets = (step, 2 * step, -step, -2 * step)
+    for offset in offsets:
+        ring_peer = (lax.rem(me + offset + count, count), head)
+        pl.semaphore_signal(barrier, inc=1, device_id=ring_peer, device_id_type=pl.DeviceIdType.MESH)
+    pl.semaphore_wait(barrier, len(offsets))
+
+    def transfer(round_index, source, landing, distance):
+        copy = pltpu.make_async_remote_copy(
+            src_ref=source,
+            dst_ref=slots.at[landing],
+            send_sem=send_sems.at[round_index],
+            recv_sem=recv_sems.at[round_index],
+            device_id=peer(distance),
+            device_id_type=pl.DeviceIdType.MESH,
+        )
+
+        @pl.when(inside_axis(distance))
+        def _():
+            copy.start()
+
+        @pl.when(inside_axis(-distance))
+        def _():
+            copy.wait_recv()
+
+        @pl.when(jnp.logical_not(inside_axis(-distance)))
+        def _():
+            slots[landing] = jnp.zeros(slots.shape[1:], jnp.float32)
+
+        return copy
+
+    def finish(copy, distance):
+        @pl.when(inside_axis(distance))
+        def _():
+            copy.wait_send()
+
+    first = transfer(0, element_ref, 0, step)
+    second = transfer(1, slots.at[0], 1, step)
+    slots[2] = slots[0] + masks_ref[1] * slots[1]
+    third = transfer(2, slots.at[2], 3, 2 * step)
+    out_ref[...] = masks_ref[0] * (slots[2] + masks_ref[2] * slots[3])
+    finish(first, step)
+    finish(second, step)
+    finish(third, 2 * step)
+
+
+def scan_window(element, reach, step, ident):
+    count = lax.axis_size("seq")
+    masks = jnp.stack([reach >= 1, reach >= 2, reach >= 3]).astype(jnp.float32)
+    return pl.pallas_call(
+        functools.partial(window_kernel, count, step),
+        out_shape=jax.ShapeDtypeStruct(element.shape, jnp.float32),
+        in_specs=[pl.BlockSpec(memory_space=pltpu.SMEM), pl.BlockSpec(memory_space=pltpu.VMEM)],
+        out_specs=pl.BlockSpec(memory_space=pltpu.VMEM),
+        scratch_shapes=[
+            pltpu.VMEM((4,) + element.shape, jnp.float32),
+            pltpu.SemaphoreType.DMA((3,)),
+            pltpu.SemaphoreType.DMA((3,)),
+        ],
+        compiler_params=pltpu.CompilerParams(collective_id=ident, has_side_effects=True),
+    )(masks, element)
 
 
 def join_states(earlier_part, later_part):
@@ -66,7 +134,7 @@
     )
     block_index = lax.axis_index("seq")
     reach_back = block_index - dial_start[0] // token_count
-    carried = scan_window(element, reach_back, 1)
+    carried = scan_window(element, reach_back, 1, 0)
     inside = (position[None, :] >= dial_start[:, None]) & (local_pos[None, :] <= local_pos[:, None])
     scores = jnp.einsum("thd,shd->hts", query_h, key_h, preferred_element_type=jnp.float32)
     weights = jnp.where(inside[None], score_scale * scores, 0.0).astype(jnp.bfloat16)
@@ -95,7 +163,7 @@
         preferred_element_type=jnp.float32,
     )
     reach_ahead = (dial_end[token_count - 1] + token_count - 1) // token_count - 1 - block_index
-    returned = scan_window(back_element, reach_ahead, -1)
+    returned = scan_window(back_element, reach_ahead, -1, 1)
     grad_scores = jnp.einsum(
         "the,she->hts", grad_weight, value_h, preferred_element_type=jnp.float32
     )

time: 149 us -> 168 us (1.13)
  the two profiles are of different devices: /device:TPU:248 before, /device:TPU:24 now
where the time goes in v2:
time: 168 us; the launch traced here: 167 us
  Pallas kernels  130 us (77%)
  blocking collectives  14.2 us (8%)
  matrix products  8.34 us (5%)
  local copies, waits for them, and re-layouts  7.38 us (4%)
  between operations  4.14 us (2%)
  other arithmetic  3.73 us (2%)
    pallas_call x2, Pallas kernels, scan_window(): pl.pallas_call(functools.partial(window_kernel, count, step), out_shape=j...  130 us
    psum x1, blocking collectives, shards(): lax.psum((jnp.sum(attended * attended, axis=1), jnp.sum(norm_gain * grad_...  14.2 us
    unnamed x20, local copies, waits for them, and re-layouts  4.43 us

profile of v2, /device:TPU:24, one launch (start us, length us, event | category | flops | bytes accessed | tf_op | source)
XLA Modules:
  0.0 167.3 jit_solution(12443929727050379445)
XLA Ops:
  0.6 0.0 copy-start
  0.6 0.0 copy-start.3
  0.7 1.2 copy.45
  1.8 0.0 copy-start.6
  1.9 0.6 copy-done.6
  2.5 0.6 fusion.60
  5.7 0.7 add_convert_fusion.masks_ref
  6.4 0.0 copy-done.3
  6.4 0.0 copy-start.7
  6.4 0.2 copy.14
  6.6 0.4 copy-done.7
  7.1 0.6 fusion.59
  7.7 1.3 broadcast_compare_fusion
  9.0 0.0 copy-done
  9.0 1.0 fusion.27.element_ref
  10.0 65.1 %shard_map.102 = f32[8,128,128]{2,1,0:T(8,128)} custom-call(f32[3]{0:T(128)} %add_convert_fusion.masks_ref, f32[8,128,128]{2,1,0:T(8,128)} %fusion.27.element_ref), custom_call_target="tpu_custom_call" | custom-call | tf_op jit(solution)/shard_map/pallas_call | solution.py:83
  75.1 0.0 copy-start.2
  75.1 1.4 fusion.55
  76.5 0.0 copy-done.2
  76.5 0.3 fusion.11
  76.8 0.1 fusion.48
  76.9 0.3 fusion.14
  77.3 0.4 multiply_reduce_fusion
  77.6 0.0 copy-start.4
  77.6 0.0 copy-start.5
  77.6 0.2 copy.20
  77.8 0.7 copy-done.4
  78.6 0.0 copy-done.5
  78.6 0.2 fusion.21
  78.7 14.2 %all-reduce = (f32[128]{0:T(128)S(1)}, f32[128]{0:T(128)S(1)}) all-reduce(f32[128]{0:T(128)S(1)} %get-tuple-element.18, f32[128]{0:T(128)S(1)} %fusion.21), channel_id=1, replica_groups=mesh['seq'=96,'head'=8] {'head'}, use_global_device_ids=true, to_apply=%region_1.2 | all-reduce | flops 256 | bytes 2048 | tf_op jit(solution)/shard_map/psum | solution.py:146
  92.9 0.9 fusion.19
  93.8 0.2 copy.46
  94.0 0.2 fusion.53
  94.2 0.2 fusion.8
  94.4 0.3 fusion.15
  94.8 0.3 fusion.17
  95.1 0.9 copy.38
  96.6 0.6 add_convert_fusion.1.masks_ref
  97.2 1.1 fusion.33.element_ref
  98.3 64.4 %shard_map.103 = f32[8,128,128]{2,1,0:T(8,128)} custom-call(f32[3]{0:T(128)} %add_convert_fusion.1.masks_ref, f32[8,128,128]{2,1,0:T(8,128)} %fusion.33.element_ref), custom_call_target="tpu_custom_call" | custom-call | tf_op jit(solution)/shard_map/pallas_call | solution.py:83
  162.7 0.0 copy-start.1
  162.7 1.4 fusion.24
  164.1 0.0 copy-done.1
  164.2 0.3 fusion.6
  164.5 0.2 fusion.16
  164.7 0.9 copy.39
  165.6 0.2 fusion.61
  165.8 0.3 fusion.30
  166.1 0.3 fusion.13
  166.4 0.9 copy.40
  (5 shorter events, 0.1 us)
Async XLA Ops:
  0.6 8.3 %copy-start = (bf16[128,1024]{1,0:T(8,128)(2,1)S(1)}, bf16[128,1024]{1,0:T(8,128)(2,1)}, u32[]{:S(2)}) copy-start(bf16[128,1024]{1,0:T(8,128)(2,1)} %param.9) | copy-start | bytes 786436
  0.6 5.7 %copy-start.3 = (bf16[128,1024]{1,0:T(8,128)(2,1)S(1)}, bf16[128,1024]{1,0:T(8,128)(2,1)}, u32[]{:S(2)}) copy-start(bf16[128,1024]{1,0:T(8,128)(2,1)} %param.8) | copy-start | bytes 786436
  1.8 0.7 copy-start.6
  6.4 0.7 copy-start.7
  75.1 1.4 copy-start.2
  77.6 1.0 copy-start.4
  77.6 1.0 copy-start.5
  162.7 1.4 copy-start.1

commit v3 on v1

--- a/solution.py
+++ b/solution.py
@@ -1,6 +1,10 @@
+import functools
+
 import jax
 import jax.numpy as jnp
 from jax import lax
+from jax.experimental import pallas as pl
+from jax.experimental.pallas import tpu as pltpu
 from jax.sharding import PartitionSpec as P
 
 HEADS = 64
@@ -24,6 +28,66 @@
     far_pair = from_behind(pair, "seq", 2 * step)
     total = pair + (reach >= 3).astype(jnp.float32) * far_pair
     return (reach >= 1).astype(jnp.float32) * total
+
+
+def head_sum_kernel(count, parts_ref, out_ref, slots, send_sems, recv_sems):
+    me = lax.axis_index("head")
+    row = lax.axis_index("seq")
+    barrier = pltpu.get_barrier_semaphore()
+    for shift in range(1, count):
+        peer = (row, lax.rem(me + shift, count))
+        pl.semaphore_signal(barrier, inc=1, device_id=peer, device_id_type=pl.DeviceIdType.MESH)
+    pl.semaphore_wait(barrier, count - 1)
+    copies = []
+    for shift in range(1, count):
+        copy = pltpu.make_async_remote_copy(
+            src_ref=parts_ref,
+            dst_ref=slots.at[me],
+            send_sem=send_sems.at[shift],
+            recv_sem=recv_sems.at[me],
+            device_id=(row, lax.rem(me + shift, count)),
+            device_id_type=pl.DeviceIdType.MESH,
+        )
+        copy.start()
+        copies.append(copy)
+    slots[me] = parts_ref[...]
+    for shift in range(1, count):
+        source = lax.rem(me + count - shift, count)
+        pltpu.make_async_remote_copy(
+            src_ref=parts_ref,
+            dst_ref=slots.at[source],
+            send_sem=send_sems.at[shift],
+            recv_sem=recv_sems.at[source],
+            device_id=(row, source),
+            device_id_type=pl.DeviceIdType.MESH,
+        ).wait_recv()
+    total = slots[0]
+    for index in range(1, count):
+        total = total + slots[index]
+    out_ref[...] = total
+    for copy in copies:
+        copy.wait_send()
+
+
+def head_sum(square_sum, cross_sum):
+    count = lax.axis_size("head")
+    rows = square_sum.shape[0]
+    parts = jnp.concatenate(
+        [square_sum[None], cross_sum[None], jnp.zeros((6, rows), jnp.float32)], axis=0
+    )
+    total = pl.pallas_call(
+        functools.partial(head_sum_kernel, count),
+        out_shape=jax.ShapeDtypeStruct(parts.shape, jnp.float32),
+        in_specs=[pl.BlockSpec(memory_space=pltpu.VMEM)],
+        out_specs=pl.BlockSpec(memory_space=pltpu.VMEM),
+        scratch_shapes=[
+            pltpu.VMEM((count,) + parts.shape, jnp.float32),
+            pltpu.SemaphoreType.DMA((count,)),
+            pltpu.SemaphoreType.DMA((count,)),
+        ],
+        compiler_params=pltpu.CompilerParams(collective_id=2, has_side_effects=True),
+    )(parts)
+    return total[0], total[1]
 
 
 def join_states(earlier_part, later_part):
@@ -75,9 +139,8 @@
     from_before = (dial_start < block_begin).astype(jnp.float32)[:, None, None]
     attended = (local_mix + from_before * across).reshape(token_count, head_count * HD)
     grad_wide = out_grad.astype(jnp.float32)
-    square_sum, cross_sum = lax.psum(
-        (jnp.sum(attended * attended, axis=1), jnp.sum(norm_gain * grad_wide * attended, axis=1)),
-        "head",
+    square_sum, cross_sum = head_sum(
+        jnp.sum(attended * attended, axis=1), jnp.sum(norm_gain * grad_wide * attended, axis=1)
     )
     inv_rms = lax.rsqrt(square_sum / width_all + EPSILON)
     normed = (attended * inv_rms[:, None] * norm_gain).astype(jnp.bfloat16)

time: 149 us -> 148 us (level)
  blocking collectives: 12.4 us -> 0 us
  Pallas kernels: 0 us -> 8.03 us
  other arithmetic: 5.11 us -> 7.23 us
    psum x1 -> x0, blocking collectives: 12.4 us -> none  [shards(): lax.psum((jnp.sum(attended * attended, axis=1), jnp.sum(norm_gain * grad_...]
    pallas_call x0 -> x1, Pallas kernels: none -> 8.03 us  [head_sum(): pl.pallas_call(functools.partial(head_sum_kernel, count), out_shape=jax.S...]
where the time goes in v3:
time: 148 us; the launch traced here: 147 us
  waiting for transfers between devices  92.7 us (63%)
  starting transfers between devices  22.3 us (15%)
  Pallas kernels  8.03 us (5%)
  local copies, waits for them, and re-layouts  8 us (5%)
  other arithmetic  7.23 us (5%)
  matrix products  4.55 us (3%)
  between operations  4.22 us (3%)
    ppermute x6, waiting for transfers between devices, from_behind(): return lax.ppermute(x, axis, pairs)  92.7 us
    ppermute x6, starting transfers between devices, from_behind(): return lax.ppermute(x, axis, pairs)  22.3 us
    pallas_call x1, Pallas kernels, head_sum(): pl.pallas_call(functools.partial(head_sum_kernel, count), out_shape=jax.S...  8.03 us
    unnamed x20, local copies, waits for them, and re-layouts  6 us
  transfers between devices with their start and end apart: 6, of which 6 were waited for; matrix products, arithmetic and copies ran while one was open for 3% of the time, Pallas kernels for 0%

profile of v3, /device:TPU:248, one launch (start us, length us, event | category | flops | bytes accessed | tf_op | source)
XLA Modules:
  0.0 147.0 jit_solution(3460876469785371943)
XLA Ops:
  0.6 0.0 copy-start
  0.6 1.0 copy.49
  1.7 0.0 copy-start.6
  1.7 0.2 copy.14
  1.9 0.4 copy-done.6
  2.4 0.6 fusion.58
  2.9 0.7 broadcast_compare_fusion.1
  3.6 0.0 copy-done
  3.6 0.2 fusion.27
  3.8 4.7 %collective-permute-start = (f32[8,128,128]{2,1,0:T(8,128)S(1)}, f32[8,128,128]{2,1,0:T(8,128)S(1)}, u32[]{:S(2)}, u32[]{:S(2)}) collective-permute-start(f32[8,128,128]{2,1,0:T(8,128)S(1)} %fusion.27), channel_id=1, source_target_pairs={{0,8},{8,16},{16,24},{24,32},{32,40},{40,48},{48,56},{56,64},{64,7... | collective-permute-start | bytes 1572872 | tf_op jit(solution)/shard_map/ppermute | solution.py:21
  8.5 11.2 %collective-permute-done = f32[8,128,128]{2,1,0:T(8,128)S(1)} collective-permute-done((f32[8,128,128]{2,1,0:T(8,128)S(1)}, f32[8,128,128]{2,1,0:T(8,128)S(1)}, u32[]{:S(2)}, u32[]{:S(2)}) %collective-permute-start) | collective-permute-done | bytes 524320 | tf_op jit(solution)/shard_map/ppermute | solution.py:21
  19.7 7.7 %collective-permute-start.1 = (f32[8,128,128]{2,1,0:T(8,128)S(1)}, f32[8,128,128]{2,1,0:T(8,128)S(1)}, u32[]{:S(2)}, u32[]{:S(2)}) collective-permute-start(f32[8,128,128]{2,1,0:T(8,128)S(1)} %collective-permute-done), channel_id=1, source_target_pairs={{0,8},{8,16},{16,24},{24,32},{32,40},{40,48},{48,56},{56,64},{64,7... | collective-permute-start | bytes 1572872 | tf_op jit(solution)/shard_map/ppermute | solution.py:21
  30.0 0.0 copy-start.7
  30.0 0.6 copy-done.7
  30.7 0.6 fusion.57
  31.2 6.4 %collective-permute-done.1 = f32[8,128,128]{2,1,0:T(8,128)S(1)} collective-permute-done((f32[8,128,128]{2,1,0:T(8,128)S(1)}, f32[8,128,128]{2,1,0:T(8,128)S(1)}, u32[]{:S(2)}, u32[]{:S(2)}) %collective-permute-start.1) | collective-permute-done | bytes 524320 | tf_op jit(solution)/shard_map/ppermute | solution.py:21
  37.7 0.1 multiply_add_fusion.1
  37.7 4.1 %collective-permute-start.2 = (f32[8,128,128]{2,1,0:T(8,128)S(1)}, f32[8,128,128]{2,1,0:T(8,128)S(1)}, u32[]{:S(2)}, u32[]{:S(2)}) collective-permute-start(f32[8,128,128]{2,1,0:T(8,128)S(1)} %multiply_add_fusion.1), channel_id=1, source_target_pairs={{0,16},{8,24},{16,32},{24,40},{32,48},{40,56},{48,64},{56,72},{64,... | collective-permute-start | bytes 1572872 | tf_op jit(solution)/shard_map/ppermute | solution.py:21
  41.9 0.7 broadcast_compare_fusion
  42.5 0.0 copy-done.4
  42.6 0.0 copy-start.1
  42.6 0.2 copy.45
  42.8 0.1 pad.2.clone
  42.8 0.1 fusion.50
  42.9 0.6 copy-done.1
  43.5 0.3 fusion.14
  43.8 20.7 %collective-permute-done.2 = f32[8,128,128]{2,1,0:T(8,128)S(1)} collective-permute-done((f32[8,128,128]{2,1,0:T(8,128)S(1)}, f32[8,128,128]{2,1,0:T(8,128)S(1)}, u32[]{:S(2)}, u32[]{:S(2)}) %collective-permute-start.2) | collective-permute-done | bytes 524320 | tf_op jit(solution)/shard_map/ppermute | solution.py:21
  64.6 0.1 subtract_convert_fusion.1
  64.7 0.3 fusion.59
  65.0 0.3 fusion.11
  65.3 0.4 multiply_reduce_fusion
  65.6 0.0 copy-start.5
  65.7 0.2 copy.21
  65.9 0.7 copy-done.2
  66.6 0.2 fusion.19
  66.7 0.7 maximum_maximum_fusion.parts_ref
  67.4 8.0 %shard_map.102 = f32[8,128]{1,0:T(8,128)} custom-call(f32[8,128]{1,0:T(8,128)} %maximum_maximum_fusion.parts_ref), custom_call_target="tpu_custom_call" | custom-call | tf_op jit(solution)/shard_map/pallas_call | solution.py:78
  75.4 0.8 fusion.52
  76.2 0.7 rsqrt_bitcast_fusion
  76.9 0.9 fusion.21
  77.8 0.2 copy.46
  78.0 0.3 fusion.33
  78.3 1.9 %collective-permute-start.3 = (f32[8,128,128]{2,1,0:T(8,128)S(1)}, f32[8,128,128]{2,1,0:T(8,128)S(1)}, u32[]{:S(2)}, u32[]{:S(2)}) collective-permute-start(f32[8,128,128]{2,1,0:T(8,128)S(1)} %fusion.33), channel_id=1, source_target_pairs={{8,0},{16,8},{24,16},{32,24},{40,32},{48,40},{56,48},{64,56},{72,6... | collective-permute-start | bytes 1572872 | tf_op jit(solution)/shard_map/ppermute | solution.py:21
  80.2 17.2 %collective-permute-done.3 = f32[8,128,128]{2,1,0:T(8,128)S(1)} collective-permute-done((f32[8,128,128]{2,1,0:T(8,128)S(1)}, f32[8,128,128]{2,1,0:T(8,128)S(1)}, u32[]{:S(2)}, u32[]{:S(2)}) %collective-permute-start.3) | collective-permute-done | bytes 524320 | tf_op jit(solution)/shard_map/ppermute | solution.py:21
  97.4 1.9 %collective-permute-start.4 = (f32[8,128,128]{2,1,0:T(8,128)S(1)}, f32[8,128,128]{2,1,0:T(8,128)}, u32[]{:S(2)}, u32[]{:S(2)}) collective-permute-start(f32[8,128,128]{2,1,0:T(8,128)S(1)} %collective-permute-done.3), channel_id=1, source_target_pairs={{8,0},{16,8},{24,16},{32,24},{40,32},{48,40},{56,48},{64,56},{72,6... | collective-permute-start | bytes 1572872 | tf_op jit(solution)/shard_map/ppermute | solution.py:21
  100.1 0.2 fusion.60
  100.3 0.0 copy-done.3
  100.3 0.2 fusion.8
  100.5 15.3 %collective-permute-done.4 = f32[8,128,128]{2,1,0:T(8,128)} collective-permute-done((f32[8,128,128]{2,1,0:T(8,128)S(1)}, f32[8,128,128]{2,1,0:T(8,128)}, u32[]{:S(2)}, u32[]{:S(2)}) %collective-permute-start.4) | collective-permute-done | bytes 524320 | tf_op jit(solution)/shard_map/ppermute | solution.py:21
  115.9 1.3 multiply_add_fusion
  117.1 1.9 %collective-permute-start.5 = (f32[8,128,128]{2,1,0:T(8,128)S(1)}, f32[8,128,128]{2,1,0:T(8,128)}, u32[]{:S(2)}, u32[]{:S(2)}) collective-permute-start(f32[8,128,128]{2,1,0:T(8,128)S(1)} %multiply_add_fusion), channel_id=1, source_target_pairs={{16,0},{24,8},{32,16},{40,24},{48,32},{56,40},{64,48},{72,56},{80,... | collective-permute-start | bytes 1572872 | tf_op jit(solution)/shard_map/ppermute | solution.py:21
  119.0 0.3 fusion.15
  119.4 0.3 fusion.17
  119.7 0.9 copy.38
  120.5 0.2 fusion.61
  120.8 21.8 %collective-permute-done.5 = f32[8,128,128]{2,1,0:T(8,128)} collective-permute-done((f32[8,128,128]{2,1,0:T(8,128)S(1)}, f32[8,128,128]{2,1,0:T(8,128)}, u32[]{:S(2)}, u32[]{:S(2)}) %collective-permute-start.5) | collective-permute-done | bytes 524320 | tf_op jit(solution)/shard_map/ppermute | solution.py:21
  142.6 1.2 subtract_convert_fusion
  143.8 0.3 fusion.23
  144.1 0.3 fusion.29
  144.4 0.3 fusion.6
  144.7 0.2 fusion.16
  145.0 0.9 copy.39
  145.8 0.3 fusion.13
  146.2 0.9 copy.40
  (8 shorter events, 0.0 us)
Async XLA Ops:
  0.6 3.0 %copy-start = (bf16[128,1024]{1,0:T(8,128)(2,1)S(1)}, bf16[128,1024]{1,0:T(8,128)(2,1)}, u32[]{:S(2)}) copy-start(bf16[128,1024]{1,0:T(8,128)(2,1)} %param.9) | copy-start | bytes 786436
  1.7 0.7 copy-start.6
  3.8 15.9 %collective-permute-start = (f32[8,128,128]{2,1,0:T(8,128)S(1)}, f32[8,128,128]{2,1,0:T(8,128)S(1)}, u32[]{:S(2)}, u32[]{:S(2)}) collective-permute-start(f32[8,128,128]{2,1,0:T(8,128)S(1)} %fusion.27), channel_id=1, source_target_pairs={{0,8},{8,16},{16,24},{24,32},{32,40},{40,48},{48,56},{56,64},{64,7... | collective-permute-start | bytes 1572872 | tf_op jit(solution)/shard_map/ppermute | solution.py:21
  19.7 18.0 %collective-permute-start.1 = (f32[8,128,128]{2,1,0:T(8,128)S(1)}, f32[8,128,128]{2,1,0:T(8,128)S(1)}, u32[]{:S(2)}, u32[]{:S(2)}) collective-permute-start(f32[8,128,128]{2,1,0:T(8,128)S(1)} %collective-permute-done), channel_id=1, source_target_pairs={{0,8},{8,16},{16,24},{24,32},{32,40},{40,48},{48,56},{56,64},{64,7... | collective-permute-start | bytes 1572872 | tf_op jit(solution)/shard_map/ppermute | solution.py:21
  30.0 0.7 copy-start.7
  31.2 11.3 %copy-start.4 = (bf16[128,1024]{1,0:T(8,128)(2,1)S(1)}, bf16[128,1024]{1,0:T(8,128)(2,1)}, u32[]{:S(2)}) copy-start(bf16[128,1024]{1,0:T(8,128)(2,1)} %param.7) | copy-start | bytes 786436
  37.7 26.8 %collective-permute-start.2 = (f32[8,128,128]{2,1,0:T(8,128)S(1)}, f32[8,128,128]{2,1,0:T(8,128)S(1)}, u32[]{:S(2)}, u32[]{:S(2)}) collective-permute-start(f32[8,128,128]{2,1,0:T(8,128)S(1)} %multiply_add_fusion.1), channel_id=1, source_target_pairs={{0,16},{8,24},{16,32},{24,40},{32,48},{40,56},{48,64},{56,72},{64,... | collective-permute-start | bytes 1572872 | tf_op jit(solution)/shard_map/ppermute | solution.py:21
  42.6 1.0 copy-start.1
  65.6 1.0 copy-start.2
  65.6 1.0 copy-start.5
  78.3 19.1 %collective-permute-start.3 = (f32[8,128,128]{2,1,0:T(8,128)S(1)}, f32[8,128,128]{2,1,0:T(8,128)S(1)}, u32[]{:S(2)}, u32[]{:S(2)}) collective-permute-start(f32[8,128,128]{2,1,0:T(8,128)S(1)} %fusion.33), channel_id=1, source_target_pairs={{8,0},{16,8},{24,16},{32,24},{40,32},{48,40},{56,48},{64,56},{72,6... | collective-permute-start | bytes 1572872 | tf_op jit(solution)/shard_map/ppermute | solution.py:21
  97.4 2.8 %copy-start.3 = (f32[8,128,128]{2,1,0:T(8,128)}, f32[8,128,128]{2,1,0:T(8,128)S(1)}, u32[]{:S(2)}) copy-start(f32[8,128,128]{2,1,0:T(8,128)S(1)} %collective-permute-done.3) | copy-start | bytes 1572868
  97.4 18.4 %collective-permute-start.4 = (f32[8,128,128]{2,1,0:T(8,128)S(1)}, f32[8,128,128]{2,1,0:T(8,128)}, u32[]{:S(2)}, u32[]{:S(2)}) collective-permute-start(f32[8,128,128]{2,1,0:T(8,128)S(1)} %collective-permute-done.3), channel_id=1, source_target_pairs={{8,0},{16,8},{24,16},{32,24},{40,32},{48,40},{56,48},{64,56},{72,6... | collective-permute-start | bytes 1572872 | tf_op jit(solution)/shard_map/ppermute | solution.py:21
  117.1 25.5 %collective-permute-start.5 = (f32[8,128,128]{2,1,0:T(8,128)S(1)}, f32[8,128,128]{2,1,0:T(8,128)}, u32[]{:S(2)}, u32[]{:S(2)}) collective-permute-start(f32[8,128,128]{2,1,0:T(8,128)S(1)} %multiply_add_fusion), channel_id=1, source_target_pairs={{16,0},{24,8},{32,16},{40,24},{48,32},{56,40},{64,48},{72,56},{80,... | collective-permute-start | bytes 1572872 | tf_op jit(solution)/shard_map/ppermute | solution.py:21

commit v4 on v3

--- a/solution.py
+++ b/solution.py
@@ -21,14 +21,87 @@
     return lax.ppermute(x, axis, pairs)
 
 
-def scan_window(element, reach, step):
-    nearest = from_behind(element, "seq", step)
-    second = from_behind(nearest, "seq", step)
-    pair = nearest + (reach >= 2).astype(jnp.float32) * second
-    far_pair = from_behind(pair, "seq", 2 * step)
-    total = pair + (reach >= 3).astype(jnp.float32) * far_pair
-    return (reach >= 1).astype(jnp.float32) * total
-
+def window_kernel(count, step, masks_ref, element_ref, out_ref, slots, send_sems, recv_sems):
+    me = lax.axis_index("seq")
+    head = lax.axis_index("head")
+    heads = element_ref.shape[0]
+
+    def inside_axis(offset):
+        return (me + offset >= 0) & (me + offset < count)
+
+    barrier = pltpu.get_barrier_semaphore()
+    offsets = (step, 2 * step, -step, -2 * step)
+    for offset in offsets:
+        ring_peer = (lax.rem(me + offset + count, count), head)
+        pl.semaphore_signal(barrier, inc=1, device_id=ring_peer, device_id_type=pl.DeviceIdType.MESH)
+    pl.semaphore_wait(barrier, len(offsets))
+
+    def describe(round_index, source, landing, part, distance):
+        return pltpu.make_async_remote_copy(
+            src_ref=source,
+            dst_ref=slots.at[landing, part],
+            send_sem=send_sems.at[round_index, part],
+            recv_sem=recv_sems.at[round_index, part],
+            device_id=(me + distance, head),
+            device_id_type=pl.DeviceIdType.MESH,
+        )
+
+    def send(copy, distance):
+        @pl.when(inside_axis(distance))
+        def _():
+            copy.start()
+
+    def land(copy, landing, part, distance):
+        @pl.when(inside_axis(-distance))
+        def _():
+            copy.wait_recv()
+
+        @pl.when(jnp.logical_not(inside_axis(-distance)))
+        def _():
+            slots[landing, part] = jnp.zeros(slots.shape[2:], jnp.float32)
+
+    rounds = [[], [], []]
+    for part in range(heads):
+        copy = describe(0, element_ref.at[part], 0, part, step)
+        send(copy, step)
+        rounds[0].append(copy)
+    for part in range(heads):
+        land(rounds[0][part], 0, part, step)
+        copy = describe(1, slots.at[0, part], 1, part, step)
+        send(copy, step)
+        rounds[1].append(copy)
+    for part in range(heads):
+        land(rounds[1][part], 1, part, step)
+        slots[2, part] = slots[0, part] + masks_ref[1] * slots[1, part]
+        copy = describe(2, slots.at[2, part], 3, part, 2 * step)
+        send(copy, 2 * step)
+        rounds[2].append(copy)
+    for part in range(heads):
+        land(rounds[2][part], 3, part, 2 * step)
+        out_ref[part] = masks_ref[0] * (slots[2, part] + masks_ref[2] * slots[3, part])
+    for round_index, distance in enumerate((step, step, 2 * step)):
+        for copy in rounds[round_index]:
+            @pl.when(inside_axis(distance))
+            def _():
+                copy.wait_send()
+
+
+def scan_window(element, reach, step, ident):
+    count = lax.axis_size("seq")
+    heads = element.shape[0]
+    masks = jnp.stack([reach >= 1, reach >= 2, reach >= 3]).astype(jnp.float32)
+    return pl.pallas_call(
+        functools.partial(window_kernel, count, step),
+        out_shape=jax.ShapeDtypeStruct(element.shape, jnp.float32),
+        in_specs=[pl.BlockSpec(memory_space=pltpu.SMEM), pl.BlockSpec(memory_space=pltpu.VMEM)],
+        out_specs=pl.BlockSpec(memory_space=pltpu.VMEM),
+        scratch_shapes=[
+            pltpu.VMEM((4,) + element.shape, jnp.float32),
+            pltpu.SemaphoreType.DMA((3, heads)),
+            pltpu.SemaphoreType.DMA((3, heads)),
+        ],
+        compiler_params=pltpu.CompilerParams(collective_id=ident, has_side_effects=True),
+    )(masks, element)
 
 def head_sum_kernel(count, parts_ref, out_ref, slots, send_sems, recv_sems):
     me = lax.axis_index("head")
@@ -130,7 +203,7 @@
     )
     block_index = lax.axis_index("seq")
     reach_back = block_index - dial_start[0] // token_count
-    carried = scan_window(element, reach_back, 1)
+    carried = scan_window(element, reach_back, 1, 0)
     inside = (position[None, :] >= dial_start[:, None]) & (local_pos[None, :] <= local_pos[:, None])
     scores = jnp.einsum("thd,shd->hts", query_h, key_h, preferred_element_type=jnp.float32)
     weights = jnp.where(inside[None], score_scale * scores, 0.0).astype(jnp.bfloat16)
@@ -158,7 +231,7 @@
         preferred_element_type=jnp.float32,
     )
     reach_ahead = (dial_end[token_count - 1] + token_count - 1) // token_count - 1 - block_index
-    returned = scan_window(back_element, reach_ahead, -1)
+    returned = scan_window(back_element, reach_ahead, -1, 1)
     grad_scores = jnp.einsum(
         "the,she->hts", grad_weight, value_h, preferred_element_type=jnp.float32
     )

time: 148 us -> 156 us (1.054)
  the two profiles are of different devices: /device:TPU:248 before, /device:TPU:24 now
where the time goes in v4:
time: 156 us; the launch traced here: 155 us
  Pallas kernels  129 us (83%)
  matrix products  8.35 us (5%)
  local copies, waits for them, and re-layouts  7.49 us (5%)
  other arithmetic  5.82 us (4%)
  between operations  4.14 us (3%)
    pallas_call x2, Pallas kernels, scan_window(): pl.pallas_call(functools.partial(window_kernel, count, step), out_shape=j...  121 us
    pallas_call x1, Pallas kernels, head_sum(): pl.pallas_call(functools.partial(head_sum_kernel, count), out_shape=jax.S...  8.03 us
    unnamed x20, local copies, waits for them, and re-layouts  4.43 us
    dot_general x4, matrix products, state_product(): first = jnp.einsum(form, rows, upper, preferred_element_type=jnp.float32)  3.33 us

profile of v4, /device:TPU:24, one launch (start us, length us, event | category | flops | bytes accessed | tf_op | source)
XLA Modules:
  0.0 155.1 jit_solution(5139856848150880801)
XLA Ops:
  0.6 0.0 copy-start
  0.6 0.0 copy-start.3
  0.7 1.2 copy.45
  1.8 0.0 copy-start.6
  1.9 0.6 copy-done.6
  2.5 0.6 fusion.60
  5.7 0.6 add_convert_fusion.masks_ref
  6.3 0.0 copy-done.3
  6.4 0.0 copy-start.7
  6.4 0.2 copy.14
  6.6 0.4 copy-done.7
  7.0 0.6 fusion.59
  7.7 1.3 broadcast_compare_fusion
  9.0 0.0 copy-done
  9.0 1.0 fusion.27.element_ref
  10.0 64.3 %shard_map.102 = f32[8,128,128]{2,1,0:T(8,128)} custom-call(f32[3]{0:T(128)} %add_convert_fusion.masks_ref, f32[8,128,128]{2,1,0:T(8,128)} %fusion.27.element_ref), custom_call_target="tpu_custom_call" | custom-call | tf_op jit(solution)/shard_map/pallas_call | solution.py:93
  74.3 0.0 copy-start.2
  74.3 1.4 fusion.55
  75.7 0.0 copy-done.2
  75.7 0.3 fusion.11
  76.0 0.1 fusion.48
  76.1 0.3 fusion.14
  76.4 0.4 multiply_reduce_fusion
  76.8 0.0 copy-start.4
  76.8 0.0 copy-start.5
  76.8 0.2 copy.21
  77.0 0.7 copy-done.4
  77.8 0.0 copy-done.5
  77.8 0.2 fusion.19
  77.9 0.1 pad.5.clone
  78.0 0.7 maximum_maximum_fusion.parts_ref
  78.7 8.0 %shard_map.103 = f32[8,128]{1,0:T(8,128)} custom-call(f32[8,128]{1,0:T(8,128)} %maximum_maximum_fusion.parts_ref), custom_call_target="tpu_custom_call" | custom-call | tf_op jit(solution)/shard_map/pallas_call | solution.py:151
  86.7 0.8 fusion.50
  87.5 0.7 rsqrt_bitcast_fusion
  88.1 0.9 fusion.21
  89.0 0.2 copy.46
  89.2 0.2 fusion.53
  89.4 0.2 fusion.8
  89.7 0.3 fusion.15
  90.0 0.3 fusion.17
  90.3 0.9 copy.38
  91.8 0.7 add_convert_fusion.1.masks_ref
  92.5 1.1 fusion.33.element_ref
  93.6 57.0 %shard_map.104 = f32[8,128,128]{2,1,0:T(8,128)} custom-call(f32[3]{0:T(128)} %add_convert_fusion.1.masks_ref, f32[8,128,128]{2,1,0:T(8,128)} %fusion.33.element_ref), custom_call_target="tpu_custom_call" | custom-call | tf_op jit(solution)/shard_map/pallas_call | solution.py:93
  150.5 0.0 copy-start.1
  150.5 1.4 fusion.24
  151.9 0.0 copy-done.1
  151.9 0.3 fusion.6
  152.3 0.2 fusion.16
  152.5 0.9 copy.39
  153.3 0.2 fusion.61
  153.6 0.3 fusion.30
  153.9 0.3 fusion.13
  154.2 0.9 copy.40
  (5 shorter events, 0.1 us)
Async XLA Ops:
  0.6 8.3 %copy-start = (bf16[128,1024]{1,0:T(8,128)(2,1)S(1)}, bf16[128,1024]{1,0:T(8,128)(2,1)}, u32[]{:S(2)}) copy-start(bf16[128,1024]{1,0:T(8,128)(2,1)} %param.9) | copy-start | bytes 786436
  0.6 5.7 %copy-start.3 = (bf16[128,1024]{1,0:T(8,128)(2,1)S(1)}, bf16[128,1024]{1,0:T(8,128)(2,1)}, u32[]{:S(2)}) copy-start(bf16[128,1024]{1,0:T(8,128)(2,1)} %param.8) | copy-start | bytes 786436
  1.8 0.7 copy-start.6
  6.4 0.7 copy-start.7
  74.3 1.4 copy-start.2
  76.8 1.0 copy-start.4
  76.8 1.0 copy-start.5
  150.5 1.4 copy-start.1

commit v5 on v3

--- a/solution.py
+++ b/solution.py
@@ -21,7 +21,7 @@
     return lax.ppermute(x, axis, pairs)
 
 
-def scan_window(element, reach, step):
+def scan_window_permutes(element, reach, step):
     nearest = from_behind(element, "seq", step)
     second = from_behind(nearest, "seq", step)
     pair = nearest + (reach >= 2).astype(jnp.float32) * second
@@ -29,6 +29,117 @@
     total = pair + (reach >= 3).astype(jnp.float32) * far_pair
     return (reach >= 1).astype(jnp.float32) * total
 
+
+def chain_kernel(count, step, flag_ref, element_ref, out_ref, link_slot, state_slot, sent_slot, send_sems, recv_sems):
+    me = lax.axis_index("seq")
+    head = lax.axis_index("head")
+    heads = element_ref.shape[0]
+    rank = lax.rem(me, 4)
+    pos = rank if step == 1 else 3 - rank
+    ahead_exists = (me + step >= 0) & (me + step < count)
+    behind_exists = (me - step >= 0) & (me - step < count)
+
+    barrier = pltpu.get_barrier_semaphore()
+    for offset in (1, -1):
+        ring_peer = (lax.rem(me + offset + count, count), head)
+        pl.semaphore_signal(barrier, inc=1, device_id=ring_peer, device_id_type=pl.DeviceIdType.MESH)
+    pl.semaphore_wait(barrier, 2)
+
+    def describe(kind, part, source, landing):
+        return pltpu.make_async_remote_copy(
+            src_ref=source,
+            dst_ref=landing.at[part],
+            send_sem=send_sems.at[kind, part],
+            recv_sem=recv_sems.at[kind, part],
+            device_id=(me + step, head),
+            device_id_type=pl.DeviceIdType.MESH,
+        )
+
+    flag = flag_ref[0]
+    sends = []
+    for part in range(heads):
+        @pl.when(pos >= 1)
+        def _():
+            describe(0, part, link_slot.at[part], link_slot).wait_recv()
+            link_slot[part] = element_ref[part] + flag * link_slot[part]
+
+        @pl.when(pos == 0)
+        def _():
+            link_slot[part] = element_ref[part]
+
+        into_link = describe(0, part, link_slot.at[part], link_slot)
+        into_state = pltpu.make_async_remote_copy(
+            src_ref=link_slot.at[part],
+            dst_ref=state_slot.at[part],
+            send_sem=send_sems.at[0, part],
+            recv_sem=recv_sems.at[1, part],
+            device_id=(me + step, head),
+            device_id_type=pl.DeviceIdType.MESH,
+        )
+
+        @pl.when(pos <= 2)
+        def _():
+            into_link.start()
+
+        @pl.when((pos == 3) & ahead_exists)
+        def _():
+            into_state.start()
+
+        sends.append((into_link, into_state))
+    state_sends = []
+    for part in range(heads):
+        @pl.when(behind_exists)
+        def _():
+            describe(1, part, state_slot.at[part], state_slot).wait_recv()
+
+        @pl.when(jnp.logical_not(behind_exists))
+        def _():
+            state_slot[part] = jnp.zeros(state_slot.shape[1:], jnp.float32)
+
+        out_ref[part] = state_slot[part]
+        copy = describe(1, part, sent_slot.at[part], state_slot)
+
+        @pl.when(pos <= 2)
+        def _():
+            sent_slot[part] = element_ref[part] + flag * state_slot[part]
+            copy.start()
+
+        state_sends.append(copy)
+    for part in range(heads):
+        into_link, into_state = sends[part]
+
+        @pl.when(pos <= 2)
+        def _():
+            into_link.wait_send()
+
+        @pl.when((pos == 3) & ahead_exists)
+        def _():
+            into_state.wait_send()
+
+        @pl.when(pos <= 2)
+        def _():
+            state_sends[part].wait_send()
+
+
+def scan_window(element, flag, reach, step, ident):
+    count = lax.axis_size("seq")
+    if count % 4:
+        return scan_window_permutes(element, reach, step)
+    heads = element.shape[0]
+    return pl.pallas_call(
+        functools.partial(chain_kernel, count, step),
+        out_shape=jax.ShapeDtypeStruct(element.shape, jnp.float32),
+        in_specs=[pl.BlockSpec(memory_space=pltpu.SMEM), pl.BlockSpec(memory_space=pltpu.VMEM)],
+        out_specs=pl.BlockSpec(memory_space=pltpu.VMEM),
+        scratch_shapes=[
+            pltpu.VMEM(element.shape, jnp.float32),
+            pltpu.VMEM(element.shape, jnp.float32),
+            pltpu.VMEM(element.shape, jnp.float32),
+            pltpu.SemaphoreType.DMA((2, heads)),
+            pltpu.SemaphoreType.DMA((2, heads)),
+        ],
+        compiler_params=pltpu.CompilerParams(collective_id=ident, has_side_effects=True),
+    )(flag.astype(jnp.float32).reshape(1), element)
 
 def head_sum_kernel(count, parts_ref, out_ref, slots, send_sems, recv_sems):
     me = lax.axis_index("head")
@@ -130,7 +241,7 @@
     )
     block_index = lax.axis_index("seq")
     reach_back = block_index - dial_start[0] // token_count
-    carried = scan_window(element, reach_back, 1)
+    carried = scan_window(element, last_start < block_begin, reach_back, 1, 0)
     inside = (position[None, :] >= dial_start[:, None]) & (local_pos[None, :] <= local_pos[:, None])
     scores = jnp.einsum("thd,shd->hts", query_h, key_h, preferred_element_type=jnp.float32)
     weights = jnp.where(inside[None], score_scale * scores, 0.0).astype(jnp.bfloat16)
@@ -158,7 +269,7 @@
         preferred_element_type=jnp.float32,
     )
     reach_ahead = (dial_end[token_count - 1] + token_count - 1) // token_count - 1 - block_index
-    returned = scan_window(back_element, reach_ahead, -1)
+    returned = scan_window(back_element, first_end > block_begin + token_count, reach_ahead, -1, 1)
     grad_scores = jnp.einsum(
         "the,she->hts", grad_weight, value_h, preferred_element_type=jnp.float32
     )

time: 148 us -> 119 us (0.80)
  the two profiles are of different devices: /device:TPU:248 before, /device:TPU:4 now
where the time goes in v5:
time: 119 us
  Pallas kernels  97.8 us (82%)
  matrix products  8.32 us (7%)
  local copies, waits for them, and re-layouts  7.09 us (6%)
  other arithmetic  3.97 us (3%)
  between operations  1.57 us (1%)
    pallas_call x2, Pallas kernels, scan_window(): pl.pallas_call(functools.partial(chain_kernel, count, step), out_shape=ja...  90.5 us
    pallas_call x1, Pallas kernels, head_sum(): pl.pallas_call(functools.partial(head_sum_kernel, count), out_shape=jax.S...  7.35 us
    unnamed x20, local copies, waits for them, and re-layouts  4.67 us
    dot_general x4, matrix products, state_product(): first = jnp.einsum(form, rows, upper, preferred_element_type=jnp.float32)  3.33 us

profile of v5, /device:TPU:4, one launch (start us, length us, event | category | flops | bytes accessed | tf_op | source)
XLA Modules:
  0.0 118.8 jit_solution(17695270280593962144)
XLA Ops:
  0.6 0.0 copy-start
  0.6 0.0 copy-start.3
  0.7 1.2 copy.45
  1.8 0.0 copy-start.6
  1.8 0.6 copy-done.6
  2.5 0.6 slice.12
  3.7 0.0 copy-done.3
  3.8 0.2 copy.14
  4.0 0.0 copy-start.7
  4.0 0.6 copy-done.7
  4.7 0.7 broadcast_compare_fusion
  5.4 0.0 copy-done
  5.4 1.0 fusion.27.element_ref
  6.4 40.8 %shard_map.102 = f32[8,128,128]{2,1,0:T(8,128)} custom-call(f32[1]{0:T(128)} %bitcast.2.flag_ref, f32[8,128,128]{2,1,0:T(8,128)} %fusion.27.element_ref), custom_call_target="tpu_custom_call" | custom-call | tf_op jit(solution)/shard_map/pallas_call | solution.py:129
  47.2 0.0 copy-start.2
  47.2 1.4 %fusion.55 = f32[8,128,128]{2,1,0:T(8,128)S(1)} fusion(bf16[128,8,128]{0,2,1:T(8,128)(2,1)S(1)} %bitcast.107, f32[8,128,128]{2,1,0:T(8,128)} %shard_map.102), kind=kOutput, calls=%fused_computation.79 | convolution fusion | flops 33685504 | bytes 1310720 | tf_op jit(solution)/shard_map/thd,hde->the/dot_general | solution.py:219
  48.6 0.0 copy-done.2
  48.7 0.3 fusion.11
  49.0 0.1 fusion.48
  49.0 0.3 fusion.14
  49.4 0.4 multiply_reduce_fusion
  49.7 0.0 copy-start.4
  49.7 0.0 copy-start.5
  49.8 0.2 copy.21
  50.0 0.7 copy-done.4
  50.7 0.0 copy-done.5
  50.7 0.2 fusion.19
  50.8 0.1 pad.2.clone
  50.9 0.7 maximum_maximum_fusion.parts_ref
  51.6 7.3 %shard_map.103 = f32[8,128]{1,0:T(8,128)} custom-call(f32[8,128]{1,0:T(8,128)} %maximum_maximum_fusion.parts_ref), custom_call_target="tpu_custom_call" | custom-call | tf_op jit(solution)/shard_map/pallas_call | solution.py:189
  58.9 0.8 fusion.50
  59.7 0.7 rsqrt_bitcast_fusion
  60.4 0.9 fusion.21
  61.3 0.2 copy.46
  61.5 0.2 fusion.53
  61.7 0.2 fusion.8
  61.9 0.3 fusion.15
  62.3 0.3 fusion.17
  62.6 0.9 copy.38
  63.5 1.1 fusion.33.element_ref
  64.6 49.7 %shard_map.104 = f32[8,128,128]{2,1,0:T(8,128)} custom-call(f32[1]{0:T(128)} %bitcast.14.flag_ref, f32[8,128,128]{2,1,0:T(8,128)} %fusion.33.element_ref), custom_call_target="tpu_custom_call" | custom-call | tf_op jit(solution)/shard_map/pallas_call | solution.py:129
  114.2 0.0 copy-start.1
  114.2 1.4 %fusion.24 = f32[8,128,128]{2,1,0:T(8,128)S(1)} fusion(f32[8,128,128]{2,1,0:T(8,128)} %shard_map.104, bf16[128,1024]{1,0:T(8,128)(2,1)S(1)} %copy-done), kind=kOutput, calls=%fused_computation.39 | convolution fusion | flops 33685504 | bytes 1310720 | tf_op jit(solution)/shard_map/she,hde->shd/dot_general | solution.py:219
  115.7 0.0 copy-done.1
  115.7 0.3 fusion.6
  116.0 0.2 fusion.16
  116.2 0.9 copy.39
  117.0 0.2 fusion.59
  117.3 0.3 fusion.30
  117.6 0.3 fusion.13
  117.9 0.9 copy.40
  (5 shorter events, 0.1 us)
Async XLA Ops:
  0.6 4.8 %copy-start = (bf16[128,1024]{1,0:T(8,128)(2,1)S(1)}, bf16[128,1024]{1,0:T(8,128)(2,1)}, u32[]{:S(2)}) copy-start(bf16[128,1024]{1,0:T(8,128)(2,1)} %param.9) | copy-start | bytes 786436
  0.6 3.1 %copy-start.3 = (bf16[128,1024]{1,0:T(8,128)(2,1)S(1)}, bf16[128,1024]{1,0:T(8,128)(2,1)}, u32[]{:S(2)}) copy-start(bf16[128,1024]{1,0:T(8,128)(2,1)} %param.8) | copy-start | bytes 786436
  1.8 0.7 copy-start.6
  4.0 0.7 copy-start.7
  47.2 1.4 %copy-start.2 = (f32[8,128,128]{2,1,0:T(8,128)S(1)}, f32[8,128,128]{2,1,0:T(8,128)}, u32[]{:S(2)}) copy-start(f32[8,128,128]{2,1,0:T(8,128)} %shard_map.102) | copy-start | bytes 1572868
  49.7 1.0 copy-start.4
  49.7 1.0 copy-start.5
  114.2 1.4 %copy-start.1 = (f32[8,128,128]{2,1,0:T(8,128)S(1)}, f32[8,128,128]{2,1,0:T(8,128)}, u32[]{:S(2)}) copy-start(f32[8,128,128]{2,1,0:T(8,128)} %shard_map.104) | copy-start | bytes 1572868

commit v6 on v5

--- a/solution.py
+++ b/solution.py
@@ -30,7 +30,11 @@
     return (reach >= 1).astype(jnp.float32) * total
 
 
-def chain_kernel(count, step, flag_ref, element_ref, out_ref, link_slot, state_slot, sent_slot, send_sems, recv_sems):
+def chain_kernel(count, step, side_work, extra_in, flag_ref, element_ref, *refs):
+    side_in = refs[:extra_in]
+    out_ref = refs[extra_in]
+    link_slot, state_slot, sent_slot, send_sems, recv_sems = refs[-5:]
+    side_out = refs[extra_in + 1:-5]
     me = lax.axis_index("seq")
     head = lax.axis_index("head")
     heads = element_ref.shape[0]
@@ -86,6 +90,7 @@
             into_state.start()
 
         sends.append((into_link, into_state))
+    side_work(side_in, side_out)
     state_sends = []
     for part in range(heads):
         @pl.when(behind_exists)
@@ -121,16 +126,50 @@
             state_sends[part].wait_send()
 
 
-def scan_window(element, flag, reach, step, ident):
+def forward_local(scale, side_in, side_out):
+    query_ref, key_ref, value_ref, inside_ref = side_in
+    (mix_ref,) = side_out
+    inside = inside_ref[...] > 0.5
+    for part in range(query_ref.shape[1] // HD):
+        cols = pl.ds(part * HD, HD)
+        scores = lax.dot_general(
+            query_ref[:, cols], key_ref[:, cols], (((1,), (1,)), ((), ())),
+            preferred_element_type=jnp.float32,
+        )
+        weights = jnp.where(inside, scale * scores, 0.0).astype(jnp.bfloat16)
+        mix_ref[:, cols] = jnp.dot(weights, value_ref[:, cols], preferred_element_type=jnp.float32)
+
+
+def backward_local(scale, side_in, side_out):
+    query_ref, key_ref, value_ref, grad_ref, inside_ref = side_in
+    query_out, key_out, value_out = side_out
+    inside = inside_ref[...] > 0.5
+    contract_last = (((1,), (1,)), ((), ()))
+    for part in range(query_ref.shape[1] // HD):
+        cols = pl.ds(part * HD, HD)
+        query_h = query_ref[:, cols]
+        key_h = key_ref[:, cols]
+        grad_h = grad_ref[:, cols]
+        scores = lax.dot_general(query_h, key_h, contract_last, preferred_element_type=jnp.float32)
+        scaled = jnp.where(inside, scale * scores, 0.0)
+        grad_scores = lax.dot_general(
+            grad_h, value_ref[:, cols], contract_last, preferred_element_type=jnp.float32
+        )
+        mixed = jnp.where(inside, scale * grad_scores, 0.0)
+        query_out[:, cols] = jnp.dot(mixed.astype(jnp.bfloat16), key_h, preferred_element_type=jnp.float32)
+        key_out[:, cols] = jnp.dot(mixed.T.astype(jnp.bfloat16), query_h, preferred_element_type=jnp.float32)
+        value_out[:, cols] = jnp.dot(scaled.T.astype(jnp.bfloat16), grad_h, preferred_element_type=jnp.float32)
+
+
+def scan_window(element, flag, step, ident, side_work, side_inputs, side_shapes):
     count = lax.axis_size("seq")
-    if count % 4:
-        return scan_window_permutes(element, reach, step)
     heads = element.shape[0]
+    vmem = pl.BlockSpec(memory_space=pltpu.VMEM)
     return pl.pallas_call(
-        functools.partial(chain_kernel, count, step),
-        out_shape=jax.ShapeDtypeStruct(element.shape, jnp.float32),
-        in_specs=[pl.BlockSpec(memory_space=pltpu.SMEM), pl.BlockSpec(memory_space=pltpu.VMEM)],
-        out_specs=pl.BlockSpec(memory_space=pltpu.VMEM),
+        functools.partial(chain_kernel, count, step, side_work, len(side_inputs)),
+        out_shape=(jax.ShapeDtypeStruct(element.shape, jnp.float32),) + tuple(side_shapes),
+        in_specs=[pl.BlockSpec(memory_space=pltpu.SMEM)] + [vmem] * (1 + len(side_inputs)),
+        out_specs=(vmem,) * (1 + len(side_shapes)),
         scratch_shapes=[
             pltpu.VMEM(element.shape, jnp.float32),
             pltpu.VMEM(element.shape, jnp.float32),
@@ -139,7 +178,7 @@
             pltpu.SemaphoreType.DMA((2, heads)),
         ],
         compiler_params=pltpu.CompilerParams(collective_id=ident, has_side_effects=True),
-    )(flag.astype(jnp.float32).reshape(1), element)
+    )(flag.astype(jnp.float32).reshape(1), element, *side_inputs)
 
 def head_sum_kernel(count, parts_ref, out_ref, slots, send_sems, recv_sems):
     me = lax.axis_index("head")
@@ -239,13 +278,16 @@
         value_h,
         preferred_element_type=jnp.float32,
     )
-    block_index = lax.axis_index("seq")
-    reach_back = block_index - dial_start[0] // token_count
-    carried = scan_window(element, last_start < block_begin, reach_back, 1, 0)
     inside = (position[None, :] >= dial_start[:, None]) & (local_pos[None, :] <= local_pos[:, None])
-    scores = jnp.einsum("thd,shd->hts", query_h, key_h, preferred_element_type=jnp.float32)
-    weights = jnp.where(inside[None], score_scale * scores, 0.0).astype(jnp.bfloat16)
-    local_mix = jnp.einsum("hts,she->the", weights, value_h, preferred_element_type=jnp.float32)
+    inside_wide = inside.astype(jnp.float32)
+    flat_shape = (token_count, head_count * HD)
+    wide_shape = jax.ShapeDtypeStruct(flat_shape, jnp.float32)
+    carried, local_flat = scan_window(
+        element, last_start < block_begin, 1, 0,
+        functools.partial(forward_local, score_scale),
+        (queries, key_rows, value_rows, inside_wide), (wide_shape,),
+    )
+    local_mix = local_flat.reshape(token_count, head_count, HD)
     across = score_scale * state_product("thd,hde->the", query_h, carried)
     from_before = (dial_start < block_begin).astype(jnp.float32)[:, None, None]
     attended = (local_mix + from_before * across).reshape(token_count, head_count * HD)
@@ -268,23 +310,16 @@
         grad_weight,
         preferred_element_type=jnp.float32,
     )
-    reach_ahead = (dial_end[token_count - 1] + token_count - 1) // token_count - 1 - block_index
-    returned = scan_window(back_element, first_end > block_begin + token_count, reach_ahead, -1, 1)
-    grad_scores = jnp.einsum(
-        "the,she->hts", grad_weight, value_h, preferred_element_type=jnp.float32
-    )
-    grad_mix = jnp.where(inside[None], score_scale * grad_scores, 0.0).astype(jnp.bfloat16)
+    returned, query_local, key_local, value_local = scan_window(
+        back_element, first_end > block_begin + token_count, -1, 1,
+        functools.partial(backward_local, score_scale),
+        (queries, key_rows, value_rows, grad_weight.reshape(flat_shape), inside_wide),
+        (wide_shape,) * 3,
+    )
     to_after = (dial_end > block_begin + token_count).astype(jnp.float32)[:, None, None]
-    query_grad = jnp.einsum(
-        "hts,shd->thd", grad_mix, key_h, preferred_element_type=jnp.float32
-    ) + from_before * score_scale * state_product("the,hde->thd", grad_weight, carried)
-    key_grad = jnp.einsum(
-        "hts,thd->shd", grad_mix, query_h, preferred_element_type=jnp.float32
-    ) + to_after * score_scale * state_product("she,hde->shd", value_h, returned)
-    value_grad = jnp.einsum(
-        "hts,the->she", weights, grad_weight, preferred_element_type=jnp.float32
-    ) + to_after * score_scale * state_product("shd,hde->she", key_h, returned)
-    flat_shape = (token_count, head_count * HD)
+    query_grad = query_local.reshape(token_count, head_count, HD) + from_before * score_scale * state_product("the,hde->thd", grad_weight, carried)
+    key_grad = key_local.reshape(token_count, head_count, HD) + to_after * score_scale * state_product("she,hde->shd", value_h, returned)
+    value_grad = value_local.reshape(token_count, head_count, HD) + to_after * score_scale * state_product("shd,hde->she", key_h, returned)
     return (
         normed,
         query_grad.reshape(flat_shape).astype(jnp.bfloat16),

time: 119 us -> 123 us (1.034)
  local copies, waits for them, and re-layouts: 7.09 us -> 12.5 us
  matrix products: 8.32 us -> 4.46 us
  Pallas kernels: 97.8 us -> 99.4 us
    reshape x1 -> x4, local copies, waits for them, and re-layouts: 0.17 us -> 2.92 us  [the longest x1 1.27 us: shards(): local_mix = local_flat.reshape(token_count, head_count, HD)]
    dot_general x4, matrix products: 3.33 us -> 1.14 us  [state_product(): first = jnp.einsum(form, rows, upper, preferred_element_type=jnp.float32)]
    unnamed x20 -> x29, local copies, waits for them, and re-layouts: 4.67 us -> 6.74 us
    dot_general x6 -> x0, matrix products: 1.75 us -> none  [the longest x1 0.35 us: shards(): jnp.einsum('hts,she->the', weights, value_h, preferred_element_type=jnp.f...]
    pallas_call x2, Pallas kernels: 90.5 us -> 92.1 us  [scan_window(): pl.pallas_call(functools.partial(chain_kernel, count, step, side_work, le...]
where the time goes in v6:
time: 123 us
  Pallas kernels  99.4 us (81%)
  local copies, waits for them, and re-layouts  12.5 us (10%)
  other arithmetic  4.58 us (4%)
  matrix products  4.46 us (4%)
  between operations  1.57 us (1%)
    pallas_call x2, Pallas kernels, scan_window(): pl.pallas_call(functools.partial(chain_kernel, count, step, side_work, le...  92.1 us
    pallas_call x1, Pallas kernels, head_sum(): pl.pallas_call(functools.partial(head_sum_kernel, count), out_shape=jax.S...  7.34 us
    unnamed x29, local copies, waits for them, and re-layouts  6.74 us

profile of v6, /device:TPU:4, one launch (start us, length us, event | category | flops | bytes accessed | tf_op | source)
XLA Modules:
  0.0 122.6 jit_solution(9053031038158568440)
XLA Ops:
  0.6 1.2 %slice.12 = s32[1]{0:T(128)} slice(s32[128]{0:T(128)} %param.12), slice={[127:128]} | slice | bytes 8 | tf_op jit(solution)/shard_map/slice | solution.py:273
  2.5 0.0 copy-start.2
  2.5 1.2 copy.44
  3.7 0.0 copy-start.12
  3.7 0.6 copy-done.12
  4.4 0.7 broadcast_compare_fusion
  5.1 0.0 copy-done.2
  5.1 1.0 fusion.27.element_ref
  6.1 0.0 copy-start.11
  6.1 0.6 copy-done.11
  6.7 0.7 fusion.42.refs_3_.refs_4_
  7.5 41.2 %shard_map.102 = (f32[8,128,128]{2,1,0:T(8,128)}, f32[128,1024]{1,0:T(8,128)}) custom-call(f32[1]{0:T(128)} %bitcast.1.flag_ref, f32[8,128,128]{2,1,0:T(8,128)} %fusion.27.element_ref, bf16[128,1024]{1,0:T(8,128)(2,1)} %refs_0_.3, bf16[128,1024]{1,0:T(8,128)(2,1)} %refs_1_.3, bf16[128,1024]{1,0:T(8,128)(2,1)} %refs_2_.3, f32[128,128]{1,0:T(8,128)} %fusion.42.refs_3_.refs_4_), custom_call_target="tpu_custom_call" | custom-call | tf_op jit(solution)/shard_map/pallas_call | solution.py:168
  48.7 0.0 copy-start.6
  48.7 1.3 %copy.39 = f32[128,1024]{0,1:T(8,128)S(1)} copy(f32[128,1024]{1,0:T(8,128)} %get-tuple-element.10) | data formatting | bytes 1048576 | tf_op jit(solution)/shard_map/reshape | solution.py:290
  50.0 0.0 copy-start.1
  50.0 0.0 copy-done.6
  50.0 0.2 copy.45
  50.2 0.8 copy-done.1
  51.1 0.3 fusion.49
  51.3 0.4 multiply_reduce_fusion
  51.7 0.0 copy-start.7
  51.7 0.0 copy-start.10
  51.7 0.2 copy.40
  51.9 0.7 copy-done.7
  52.6 0.0 copy-done.10
  52.6 0.2 fusion.16
  52.8 0.1 pad.2.clone
  52.9 0.7 maximum_maximum_fusion.parts_ref
  53.5 7.3 %shard_map.103 = f32[8,128]{1,0:T(8,128)} custom-call(f32[8,128]{1,0:T(8,128)} %maximum_maximum_fusion.parts_ref), custom_call_target="tpu_custom_call" | custom-call | tf_op jit(solution)/shard_map/pallas_call | solution.py:228
  60.9 0.8 fusion.44
  61.7 0.7 rsqrt_bitcast_fusion
  62.3 0.9 fusion.18
  63.2 0.0 copy-start.4
  63.3 1.0 fusion.22.element_ref
  64.3 0.0 copy-done.4
  64.3 50.9 %shard_map.104 = (f32[8,128,128]{2,1,0:T(8,128)}, f32[128,1024]{1,0:T(8,128)}, f32[128,1024]{1,0:T(8,128)}, f32[128,1024]{1,0:T(8,128)}) custom-call(f32[1]{0:T(128)} %bitcast.9.flag_ref, f32[8,128,128]{2,1,0:T(8,128)} %fusion.22.element_ref, bf16[128,1024]{1,0:T(8,128)(2,1)} %refs_0_.3, bf16[128,1024]{1,0:T(8,128)(2,1)} %refs_1_.3, ...), custom_call_target="tpu_custom_call" | custom-call | tf_op jit(solution)/shard_map/pallas_call | solution.py:168
  115.2 0.0 copy-start.5
  115.2 1.3 %copy.41 = f32[128,1024]{0,1:T(8,128)S(1)} copy(f32[128,1024]{1,0:T(8,128)} %get-tuple-element.12) | data formatting | bytes 1048576 | tf_op jit(solution)/shard_map/reshape | solution.py:320
  116.5 0.0 copy-done.5
  116.5 0.3 fusion.20
  116.8 0.3 fusion.12
  117.1 0.0 copy-start.9
  117.1 0.9 copy.32
  118.0 0.2 copy-done.9
  118.2 0.0 copy-start
  118.2 0.0 copy-start.3
  118.2 0.2 copy.42
  118.4 0.8 copy-done
  119.2 0.1 copy-done.3
  119.3 0.3 fusion.25
  119.6 0.3 fusion.13
  119.9 0.0 copy-start.8
  119.9 0.9 copy.33
  120.7 0.2 copy-done.8
  120.9 0.2 copy.43
  121.1 0.3 fusion.45
  121.4 0.3 fusion.14
  121.7 0.9 copy.34
  (4 shorter events, 0.0 us)
Async XLA Ops:
  2.5 2.5 %copy-start.2 = (bf16[128,1024]{1,0:T(8,128)(2,1)S(1)}, bf16[128,1024]{1,0:T(8,128)(2,1)}, u32[]{:S(2)}) copy-start(bf16[128,1024]{1,0:T(8,128)(2,1)} %refs_2_.3) | copy-start | bytes 786436
  3.7 0.7 copy-start.12
  6.1 0.7 copy-start.11
  48.7 1.3 %copy-start.6 = (bf16[128,1024]{1,0:T(8,128)(2,1)S(1)}, bf16[128,1024]{1,0:T(8,128)(2,1)}, u32[]{:S(2)}) copy-start(bf16[128,1024]{1,0:T(8,128)(2,1)} %refs_0_.3) | copy-start | bytes 786436
  50.0 1.0 copy-start.1
  51.7 1.0 copy-start.7
  51.7 1.0 copy-start.10
  63.2 1.1 copy-start.4
  115.2 1.3 %copy-start.5 = (bf16[128,1024]{1,0:T(8,128)(2,1)S(1)}, bf16[128,1024]{1,0:T(8,128)(2,1)}, u32[]{:S(2)}) copy-start(bf16[128,1024]{1,0:T(8,128)(2,1)} %copy-done.4) | copy-start | bytes 786436
  117.1 1.0 copy-start.9
  118.2 1.0 copy-start
  118.2 1.1 copy-start.3
  119.9 1.0 copy-start.8

commit v7 on v5

--- a/solution.py
+++ b/solution.py
@@ -10,6 +10,7 @@
 HEADS = 64
 HD = 128
 SPAN = 4
+PIECES = 2
 
 
 EPSILON = 1e-06
@@ -125,6 +126,8 @@
     count = lax.axis_size("seq")
     if count % 4:
         return scan_window_permutes(element, reach, step)
+    shape = element.shape
+    element = element.reshape(shape[0] * PIECES, shape[1] // PIECES, shape[2])
     heads = element.shape[0]
     return pl.pallas_call(
         functools.partial(chain_kernel, count, step),
@@ -139,7 +142,7 @@
             pltpu.SemaphoreType.DMA((2, heads)),
         ],
         compiler_params=pltpu.CompilerParams(collective_id=ident, has_side_effects=True),
-    )(flag.astype(jnp.float32).reshape(1), element)
+    )(flag.astype(jnp.float32).reshape(1), element).reshape(shape)
 
 def head_sum_kernel(count, parts_ref, out_ref, slots, send_sems, recv_sems):
     me = lax.axis_index("head")

time: 119 us -> 116 us (0.975)
  Pallas kernels: 97.8 us -> 93.8 us
  matrix products: 8.32 us -> 6.12 us
  other arithmetic: 3.97 us -> 5.31 us
  local copies, waits for them, and re-layouts: 7.09 us -> 8.34 us
    pallas_call x2, Pallas kernels: 90.5 us -> 86.5 us  [scan_window(): pl.pallas_call(functools.partial(chain_kernel, count, step), out_shape=ja...]
    dot_general x4, matrix products: 3.33 us -> 1.11 us  [state_product(): first = jnp.einsum(form, rows, upper, preferred_element_type=jnp.float32)]
    convert_element_type x0 -> x1, other arithmetic: none -> 1.35 us  [split_state(): lower = (state - upper.astype(jnp.float32)).astype(jnp.bfloat16)]
    reshape x0 -> x1, local copies, waits for them, and re-layouts: none -> 1.24 us  [scan_window(): return pl.pallas_call(functools.partial(chain_kernel, count, step), out_s...]
    unnamed x20 -> x16, local copies, waits for them, and re-layouts: 4.67 us -> 4.69 us
where the time goes in v7:
time: 116 us; the launch traced here: 115 us
  Pallas kernels  93.8 us (81%)
  local copies, waits for them, and re-layouts  8.34 us (7%)
  matrix products  6.12 us (5%)
  other arithmetic  5.31 us (5%)
  between operations  1.58 us (1%)
    pallas_call x2, Pallas kernels, scan_window(): pl.pallas_call(functools.partial(chain_kernel, count, step), out_shape=ja...  86.5 us
    pallas_call x1, Pallas kernels, head_sum(): pl.pallas_call(functools.partial(head_sum_kernel, count), out_shape=jax.S...  7.35 us
    unnamed x16, local copies, waits for them, and re-layouts  4.69 us

profile of v7, /device:TPU:4, one launch (start us, length us, event | category | flops | bytes accessed | tf_op | source)
XLA Modules:
  0.0 115.2 jit_solution(2917079248401205420)
XLA Ops:
  0.6 0.0 copy-start
  0.7 0.0 copy-start.5
  0.7 0.7 copy-done.5
  1.4 0.6 slice.12
  2.6 0.0 copy-start.4
  2.6 0.6 copy-done.4
  3.3 0.7 broadcast_compare_fusion
  4.0 0.1 pad.2.clone
  4.1 0.1 fusion.49
  4.2 0.0 copy-start.1
  4.2 1.2 %copy.47 = bf16[128,1024]{0,1:T(8,128)(2,1)S(1)} copy(bf16[128,1024]{1,0:T(8,128)(2,1)} %param.7) | data formatting | bytes 524288 | tf_op jit(solution)/shard_map/reshape | solution.py:234
  5.4 0.0 copy-done.1
  5.4 0.3 fusion.14
  5.8 0.2 copy.14
  6.0 0.0 copy-done
  6.0 1.0 fusion.28
  7.0 41.1 %shard_map.102 = f32[16,64,128]{2,1,0:T(8,128)} custom-call(f32[1]{0:T(128)} %bitcast.2.flag_ref, f32[16,64,128]{2,1,0:T(8,128)} %bitcast.136), custom_call_target="tpu_custom_call" | custom-call | tf_op jit(solution)/shard_map/pallas_call | solution.py:132
  48.2 1.3 %fusion.22 = (bf16[8,128,128]{2,1,0:T(8,128)(2,1)S(1)}, bf16[8,128,128]{2,1,0:T(8,128)(2,1)S(1)}) fusion(f32[8,128,128]{2,1,0:T(8,128)} %bitcast.132), kind=kLoop, calls=%fused_computation.35 | loop fusion | flops 524288 | bytes 1048576 | tf_op jit(solution)/shard_map/convert_element_type | solution.py:216
  49.5 0.3 fusion.56
  49.8 0.3 fusion.11
  50.1 0.3 multiply_reduce_fusion
  50.4 0.0 copy-start.2
  50.4 0.0 copy-start.3
  50.5 0.2 copy.21
  50.7 0.7 copy-done.2
  51.4 0.0 copy-done.3
  51.4 0.2 fusion.19
  51.5 0.7 maximum_maximum_fusion.parts_ref
  52.2 7.3 %shard_map.103 = f32[8,128]{1,0:T(8,128)} custom-call(f32[8,128]{1,0:T(8,128)} %maximum_maximum_fusion.parts_ref), custom_call_target="tpu_custom_call" | custom-call | tf_op jit(solution)/shard_map/pallas_call | solution.py:192
  59.6 0.8 fusion.51
  60.3 0.7 rsqrt_bitcast_fusion
  61.0 0.9 fusion.21
  61.9 0.2 copy.48
  62.1 0.3 fusion.15
  62.4 0.2 fusion.57
  62.7 0.2 fusion.8
  62.9 0.3 fusion.17
  63.2 0.9 copy.40
  64.0 0.2 fusion.58
  64.3 1.1 fusion.34
  65.4 45.4 %shard_map.104 = f32[16,64,128]{2,1,0:T(8,128)} custom-call(f32[1]{0:T(128)} %bitcast.16.flag_ref, f32[16,64,128]{2,1,0:T(8,128)} %bitcast.135), custom_call_target="tpu_custom_call" | custom-call | tf_op jit(solution)/shard_map/pallas_call | solution.py:132
  110.7 1.2 %copy.31 = f32[8,128,128]{1,2,0:T(8,128)S(1)} copy(f32[8,128,128]{2,1,0:T(8,128)} %bitcast.134) | data formatting | bytes 1048576 | tf_op jit(solution)/shard_map/reshape | solution.py:145
  112.0 0.3 fusion.31
  112.3 0.3 fusion.13
  112.6 0.9 copy.42
  113.4 0.3 fusion.25
  113.8 0.3 fusion.6
  114.1 0.2 fusion.16
  114.3 0.8 copy.41
  (5 shorter events, 0.1 us)
Async XLA Ops:
  0.6 5.4 %copy-start = (bf16[128,1024]{1,0:T(8,128)(2,1)S(1)}, bf16[128,1024]{1,0:T(8,128)(2,1)}, u32[]{:S(2)}) copy-start(bf16[128,1024]{1,0:T(8,128)(2,1)} %param.9) | copy-start | bytes 786436
  0.7 0.7 copy-start.5
  2.6 0.7 copy-start.4
  4.2 1.2 %copy-start.1 = (bf16[128,1024]{1,0:T(8,128)(2,1)S(1)}, bf16[128,1024]{1,0:T(8,128)(2,1)}, u32[]{:S(2)}) copy-start(bf16[128,1024]{1,0:T(8,128)(2,1)} %param.8) | copy-start | bytes 786436
  50.4 1.0 copy-start.2
  50.4 1.0 copy-start.3

commit v8 on v7

--- a/solution.py
+++ b/solution.py
@@ -35,8 +35,7 @@
     me = lax.axis_index("seq")
     head = lax.axis_index("head")
     heads = element_ref.shape[0]
-    rank = lax.rem(me, 4)
-    pos = rank if step == 1 else 3 - rank
+    pos = lax.rem(me, 4) if step == 1 else 3 - lax.rem(me + 2, 4)
     ahead_exists = (me + step >= 0) & (me + step < count)
     behind_exists = (me - step >= 0) & (me - step < count)
 
@@ -59,12 +58,12 @@
     flag = flag_ref[0]
     sends = []
     for part in range(heads):
-        @pl.when(pos >= 1)
+        @pl.when((pos >= 1) & behind_exists)
         def _():
             describe(0, part, link_slot.at[part], link_slot).wait_recv()
             link_slot[part] = element_ref[part] + flag * link_slot[part]
 
-        @pl.when(pos == 0)
+        @pl.when((pos == 0) | jnp.logical_not(behind_exists))
         def _():
             link_slot[part] = element_ref[part]
 
@@ -78,7 +77,7 @@
             device_id_type=pl.DeviceIdType.MESH,
         )
 
-        @pl.when(pos <= 2)
+        @pl.when((pos <= 2) & ahead_exists)
         def _():
             into_link.start()
 
@@ -100,7 +99,7 @@
         out_ref[part] = state_slot[part]
         copy = describe(1, part, sent_slot.at[part], state_slot)
 
-        @pl.when(pos <= 2)
+        @pl.when((pos <= 2) & ahead_exists)
         def _():
             sent_slot[part] = element_ref[part] + flag * state_slot[part]
             copy.start()
@@ -109,7 +108,7 @@
     for part in range(heads):
         into_link, into_state = sends[part]
 
-        @pl.when(pos <= 2)
+        @pl.when((pos <= 2) & ahead_exists)
         def _():
             into_link.wait_send()
 
@@ -117,7 +116,7 @@
         def _():
             into_state.wait_send()
 
-        @pl.when(pos <= 2)
+        @pl.when((pos <= 2) & ahead_exists)
         def _():
             state_sends[part].wait_send()
 

time: 116 us -> 115 us (level)
  the two profiles are of different devices: /device:TPU:4 before, /device:TPU:16 now
where the time goes in v8:
time: 115 us
  Pallas kernels  93.5 us (81%)
  local copies, waits for them, and re-layouts  8.34 us (7%)
  matrix products  6.12 us (5%)
  other arithmetic  5.31 us (5%)
  between operations  1.58 us (1%)
    pallas_call x2, Pallas kernels, scan_window(): pl.pallas_call(functools.partial(chain_kernel, count, step), out_shape=ja...  85.4 us
    pallas_call x1, Pallas kernels, head_sum(): pl.pallas_call(functools.partial(head_sum_kernel, count), out_shape=jax.S...  8.03 us
    unnamed x16, local copies, waits for them, and re-layouts  4.7 us

profile of v8, /device:TPU:16, one launch (start us, length us, event | category | flops | bytes accessed | tf_op | source)
XLA Modules:
  0.0 114.8 jit_solution(14314527380559165273)
XLA Ops:
  0.6 0.0 copy-start
  0.7 0.0 copy-start.5
  0.7 0.7 copy-done.5
  1.4 0.6 slice.12
  2.6 0.0 copy-start.4
  2.6 0.6 copy-done.4
  3.3 0.7 broadcast_compare_fusion
  4.0 0.1 pad.2.clone
  4.1 0.1 fusion.49
  4.2 0.0 copy-start.1
  4.2 1.2 %copy.47 = bf16[128,1024]{0,1:T(8,128)(2,1)S(1)} copy(bf16[128,1024]{1,0:T(8,128)(2,1)} %param.7) | data formatting | bytes 524288 | tf_op jit(solution)/shard_map/reshape | solution.py:233
  5.4 0.0 copy-done.1
  5.4 0.3 fusion.14
  5.8 0.2 copy.14
  6.0 0.0 copy-done
  6.0 1.0 fusion.28
  7.0 46.0 %shard_map.102 = f32[16,64,128]{2,1,0:T(8,128)} custom-call(f32[1]{0:T(128)} %bitcast.2.flag_ref, f32[16,64,128]{2,1,0:T(8,128)} %bitcast.136), custom_call_target="tpu_custom_call" | custom-call | tf_op jit(solution)/shard_map/pallas_call | solution.py:131
  53.0 1.3 %fusion.22 = (bf16[8,128,128]{2,1,0:T(8,128)(2,1)S(1)}, bf16[8,128,128]{2,1,0:T(8,128)(2,1)S(1)}) fusion(f32[8,128,128]{2,1,0:T(8,128)} %bitcast.132), kind=kLoop, calls=%fused_computation.35 | loop fusion | flops 524288 | bytes 1048576 | tf_op jit(solution)/shard_map/convert_element_type | solution.py:215
  54.4 0.3 fusion.56
  54.7 0.3 fusion.11
  55.0 0.3 multiply_reduce_fusion
  55.3 0.0 copy-start.2
  55.3 0.0 copy-start.3
  55.3 0.2 copy.21
  55.5 0.7 copy-done.2
  56.3 0.0 copy-done.3
  56.3 0.2 fusion.19
  56.4 0.7 maximum_maximum_fusion.parts_ref
  57.1 8.0 %shard_map.103 = f32[8,128]{1,0:T(8,128)} custom-call(f32[8,128]{1,0:T(8,128)} %maximum_maximum_fusion.parts_ref), custom_call_target="tpu_custom_call" | custom-call | tf_op jit(solution)/shard_map/pallas_call | solution.py:191
  65.1 0.8 fusion.51
  65.9 0.7 rsqrt_bitcast_fusion
  66.6 0.9 fusion.21
  67.5 0.2 copy.48
  67.7 0.3 fusion.15
  68.0 0.2 fusion.57
  68.2 0.2 fusion.8
  68.5 0.3 fusion.17
  68.8 0.9 copy.40
  69.6 0.2 fusion.58
  69.8 1.1 fusion.34
  70.9 39.4 %shard_map.104 = f32[16,64,128]{2,1,0:T(8,128)} custom-call(f32[1]{0:T(128)} %bitcast.16.flag_ref, f32[16,64,128]{2,1,0:T(8,128)} %bitcast.135), custom_call_target="tpu_custom_call" | custom-call | tf_op jit(solution)/shard_map/pallas_call | solution.py:131
  110.4 1.2 %copy.31 = f32[8,128,128]{1,2,0:T(8,128)S(1)} copy(f32[8,128,128]{2,1,0:T(8,128)} %bitcast.134) | data formatting | bytes 1048576 | tf_op jit(solution)/shard_map/reshape | solution.py:144
  111.6 0.3 fusion.31
  111.9 0.3 fusion.13
  112.2 0.9 copy.42
  113.1 0.3 fusion.25
  113.4 0.3 fusion.6
  113.8 0.2 fusion.16
  114.0 0.8 copy.41
  (5 shorter events, 0.1 us)
Async XLA Ops:
  0.6 5.4 %copy-start = (bf16[128,1024]{1,0:T(8,128)(2,1)S(1)}, bf16[128,1024]{1,0:T(8,128)(2,1)}, u32[]{:S(2)}) copy-start(bf16[128,1024]{1,0:T(8,128)(2,1)} %param.9) | copy-start | bytes 786436
  0.7 0.7 copy-start.5
  2.6 0.7 copy-start.4
  4.2 1.2 %copy-start.1 = (bf16[128,1024]{1,0:T(8,128)(2,1)S(1)}, bf16[128,1024]{1,0:T(8,128)(2,1)}, u32[]{:S(2)}) copy-start(bf16[128,1024]{1,0:T(8,128)(2,1)} %param.8) | copy-start | bytes 786436
  55.3 1.0 copy-start.2
  55.3 1.0 copy-start.3

commit v9 on v8

--- a/solution.py
+++ b/solution.py
@@ -10,7 +10,7 @@
 HEADS = 64
 HD = 128
 SPAN = 4
-PIECES = 2
+PIECES = 4
 
 
 EPSILON = 1e-06

time: 115 us -> 114 us (level)
  Pallas kernels: 93.5 us -> 92.2 us
    pallas_call x2, Pallas kernels: 85.4 us -> 84.2 us  [scan_window(): pl.pallas_call(functools.partial(chain_kernel, count, step), out_shape=ja...]
where the time goes in v9:
time: 114 us
  Pallas kernels  92.2 us (81%)
  local copies, waits for them, and re-layouts  8.34 us (7%)
  matrix products  6.13 us (5%)
  other arithmetic  5.31 us (5%)
  between operations  1.58 us (1%)
    pallas_call x2, Pallas kernels, scan_window(): pl.pallas_call(functools.partial(chain_kernel, count, step), out_shape=ja...  84.2 us
    pallas_call x1, Pallas kernels, head_sum(): pl.pallas_call(functools.partial(head_sum_kernel, count), out_shape=jax.S...  8.03 us
    unnamed x16, local copies, waits for them, and re-layouts  4.69 us

profile of v9, /device:TPU:16, one launch (start us, length us, event | category | flops | bytes accessed | tf_op | source)
XLA Modules:
  0.0 113.6 jit_solution(4343737773214494656)
XLA Ops:
  0.6 0.0 copy-start
  0.7 0.0 copy-start.5
  0.7 0.7 copy-done.5
  1.4 0.6 slice.12
  2.6 0.0 copy-start.4
  2.6 0.6 copy-done.4
  3.3 0.7 broadcast_compare_fusion
  4.0 0.1 pad.2.clone
  4.1 0.1 fusion.49
  4.2 0.0 copy-start.1
  4.2 1.2 %copy.47 = bf16[128,1024]{0,1:T(8,128)(2,1)S(1)} copy(bf16[128,1024]{1,0:T(8,128)(2,1)} %param.7) | data formatting | bytes 524288 | tf_op jit(solution)/shard_map/reshape | solution.py:233
  5.4 0.0 copy-done.1
  5.4 0.3 fusion.14
  5.8 0.2 copy.14
  6.0 0.0 copy-done
  6.0 1.0 fusion.28
  7.0 46.2 %shard_map.102 = f32[32,32,128]{2,1,0:T(8,128)} custom-call(f32[1]{0:T(128)} %bitcast.2.flag_ref, f32[32,32,128]{2,1,0:T(8,128)} %bitcast.136), custom_call_target="tpu_custom_call" | custom-call | tf_op jit(solution)/shard_map/pallas_call | solution.py:131
  53.3 1.3 %fusion.22 = (bf16[8,128,128]{2,1,0:T(8,128)(2,1)S(1)}, bf16[8,128,128]{2,1,0:T(8,128)(2,1)S(1)}) fusion(f32[8,128,128]{2,1,0:T(8,128)} %bitcast.132), kind=kLoop, calls=%fused_computation.35 | loop fusion | flops 524288 | bytes 1048576 | tf_op jit(solution)/shard_map/convert_element_type | solution.py:215
  54.6 0.3 fusion.56
  54.9 0.3 fusion.11
  55.2 0.3 multiply_reduce_fusion
  55.5 0.0 copy-start.2
  55.5 0.0 copy-start.3
  55.5 0.2 copy.21
  55.8 0.7 copy-done.2
  56.5 0.0 copy-done.3
  56.5 0.2 fusion.19
  56.6 0.7 maximum_maximum_fusion.parts_ref
  57.3 8.0 %shard_map.103 = f32[8,128]{1,0:T(8,128)} custom-call(f32[8,128]{1,0:T(8,128)} %maximum_maximum_fusion.parts_ref), custom_call_target="tpu_custom_call" | custom-call | tf_op jit(solution)/shard_map/pallas_call | solution.py:191
  65.3 0.8 fusion.51
  66.1 0.7 rsqrt_bitcast_fusion
  66.8 0.9 fusion.21
  67.7 0.2 copy.48
  67.9 0.3 fusion.15
  68.2 0.2 fusion.57
  68.4 0.2 fusion.8
  68.7 0.3 fusion.17
  69.0 0.9 copy.40
  69.8 0.2 fusion.58
  70.0 1.1 fusion.34
  71.1 38.0 %shard_map.104 = f32[32,32,128]{2,1,0:T(8,128)} custom-call(f32[1]{0:T(128)} %bitcast.16.flag_ref, f32[32,32,128]{2,1,0:T(8,128)} %bitcast.135), custom_call_target="tpu_custom_call" | custom-call | tf_op jit(solution)/shard_map/pallas_call | solution.py:131
  109.1 1.2 %copy.31 = f32[8,128,128]{1,2,0:T(8,128)S(1)} copy(f32[8,128,128]{2,1,0:T(8,128)} %bitcast.134) | data formatting | bytes 1048576 | tf_op jit(solution)/shard_map/reshape | solution.py:144
  110.4 0.3 fusion.31
  110.7 0.3 fusion.13
  111.0 0.9 copy.42
  111.9 0.3 fusion.25
  112.2 0.3 fusion.6
  112.5 0.2 fusion.16
  112.7 0.8 copy.41
  (5 shorter events, 0.1 us)
Async XLA Ops:
  0.6 5.4 %copy-start = (bf16[128,1024]{1,0:T(8,128)(2,1)S(1)}, bf16[128,1024]{1,0:T(8,128)(2,1)}, u32[]{:S(2)}) copy-start(bf16[128,1024]{1,0:T(8,128)(2,1)} %param.9) | copy-start | bytes 786436
  0.7 0.7 copy-start.5
  2.6 0.7 copy-start.4
  4.2 1.2 %copy-start.1 = (bf16[128,1024]{1,0:T(8,128)(2,1)S(1)}, bf16[128,1024]{1,0:T(8,128)(2,1)}, u32[]{:S(2)}) copy-start(bf16[128,1024]{1,0:T(8,128)(2,1)} %param.8) | copy-start | bytes 786436
  55.5 1.0 copy-start.2
  55.5 1.0 copy-start.3

commit v10 on v9

--- a/solution.py
+++ b/solution.py
@@ -10,7 +10,7 @@
 HEADS = 64
 HD = 128
 SPAN = 4
-PIECES = 4
+PIECES = 8
 
 
 EPSILON = 1e-06

time: 114 us -> 115 us (level)
  Pallas kernels: 92.2 us -> 93.6 us
    pallas_call x2, Pallas kernels: 84.2 us -> 85.5 us  [scan_window(): pl.pallas_call(functools.partial(chain_kernel, count, step), out_shape=ja...]
where the time goes in v10:
time: 115 us
  Pallas kernels  93.6 us (81%)
  local copies, waits for them, and re-layouts  8.34 us (7%)
  matrix products  6.12 us (5%)
  other arithmetic  5.31 us (5%)
  between operations  1.58 us (1%)
    pallas_call x2, Pallas kernels, scan_window(): pl.pallas_call(functools.partial(chain_kernel, count, step), out_shape=ja...  85.5 us
    pallas_call x1, Pallas kernels, head_sum(): pl.pallas_call(functools.partial(head_sum_kernel, count), out_shape=jax.S...  8.03 us
    unnamed x16, local copies, waits for them, and re-layouts  4.69 us

profile of v10, /device:TPU:16, one launch (start us, length us, event | category | flops | bytes accessed | tf_op | source)
XLA Modules:
  0.0 114.9 jit_solution(10839890532366121841)
XLA Ops:
  0.6 0.0 copy-start
  0.7 0.0 copy-start.5
  0.7 0.7 copy-done.5
  1.4 0.6 slice.12
  2.6 0.0 copy-start.4
  2.6 0.6 copy-done.4
  3.3 0.7 broadcast_compare_fusion
  4.0 0.1 pad.2.clone
  4.1 0.1 fusion.49
  4.2 0.0 copy-start.1
  4.2 1.2 %copy.47 = bf16[128,1024]{0,1:T(8,128)(2,1)S(1)} copy(bf16[128,1024]{1,0:T(8,128)(2,1)} %param.7) | data formatting | bytes 524288 | tf_op jit(solution)/shard_map/reshape | solution.py:233
  5.4 0.0 copy-done.1
  5.4 0.3 fusion.14
  5.8 0.2 copy.14
  6.0 0.0 copy-done
  6.0 1.0 fusion.28
  7.0 47.2 %shard_map.102 = f32[64,16,128]{2,1,0:T(8,128)} custom-call(f32[1]{0:T(128)} %bitcast.2.flag_ref, f32[64,16,128]{2,1,0:T(8,128)} %bitcast.136), custom_call_target="tpu_custom_call" | custom-call | tf_op jit(solution)/shard_map/pallas_call | solution.py:131
  54.2 1.3 %fusion.22 = (bf16[8,128,128]{2,1,0:T(8,128)(2,1)S(1)}, bf16[8,128,128]{2,1,0:T(8,128)(2,1)S(1)}) fusion(f32[8,128,128]{2,1,0:T(8,128)} %bitcast.132), kind=kLoop, calls=%fused_computation.35 | loop fusion | flops 524288 | bytes 1048576 | tf_op jit(solution)/shard_map/convert_element_type | solution.py:215
  55.6 0.3 fusion.56
  55.9 0.3 fusion.11
  56.2 0.3 multiply_reduce_fusion
  56.5 0.0 copy-start.2
  56.5 0.0 copy-start.3
  56.5 0.2 copy.21
  56.7 0.7 copy-done.2
  57.5 0.0 copy-done.3
  57.5 0.2 fusion.19
  57.6 0.7 maximum_maximum_fusion.parts_ref
  58.3 8.0 %shard_map.103 = f32[8,128]{1,0:T(8,128)} custom-call(f32[8,128]{1,0:T(8,128)} %maximum_maximum_fusion.parts_ref), custom_call_target="tpu_custom_call" | custom-call | tf_op jit(solution)/shard_map/pallas_call | solution.py:191
  66.3 0.8 fusion.51
  67.1 0.7 rsqrt_bitcast_fusion
  67.8 0.9 fusion.21
  68.7 0.2 copy.48
  68.9 0.3 fusion.15
  69.2 0.2 fusion.57
  69.4 0.2 fusion.8
  69.6 0.3 fusion.17
  70.0 0.9 copy.40
  70.8 0.2 fusion.58
  71.0 1.1 fusion.34
  72.1 38.3 %shard_map.104 = f32[64,16,128]{2,1,0:T(8,128)} custom-call(f32[1]{0:T(128)} %bitcast.16.flag_ref, f32[64,16,128]{2,1,0:T(8,128)} %bitcast.135), custom_call_target="tpu_custom_call" | custom-call | tf_op jit(solution)/shard_map/pallas_call | solution.py:131
  110.5 1.2 %copy.31 = f32[8,128,128]{1,2,0:T(8,128)S(1)} copy(f32[8,128,128]{2,1,0:T(8,128)} %bitcast.134) | data formatting | bytes 1048576 | tf_op jit(solution)/shard_map/reshape | solution.py:144
  111.7 0.3 fusion.31
  112.0 0.3 fusion.13
  112.3 0.9 copy.42
  113.2 0.3 fusion.25
  113.5 0.3 fusion.6
  113.8 0.2 fusion.16
  114.1 0.8 copy.41
  (5 shorter events, 0.1 us)
Async XLA Ops:
  0.6 5.4 %copy-start = (bf16[128,1024]{1,0:T(8,128)(2,1)S(1)}, bf16[128,1024]{1,0:T(8,128)(2,1)}, u32[]{:S(2)}) copy-start(bf16[128,1024]{1,0:T(8,128)(2,1)} %param.9) | copy-start | bytes 786436
  0.7 0.7 copy-start.5
  2.6 0.7 copy-start.4
  4.2 1.2 %copy-start.1 = (bf16[128,1024]{1,0:T(8,128)(2,1)S(1)}, bf16[128,1024]{1,0:T(8,128)(2,1)}, u32[]{:S(2)}) copy-start(bf16[128,1024]{1,0:T(8,128)(2,1)} %param.8) | copy-start | bytes 786436
  56.5 1.0 copy-start.2
  56.5 1.0 copy-start.3

commit v11 on v9

--- a/solution.py
+++ b/solution.py
@@ -203,6 +203,64 @@
     return total[0], total[1]
 
 
+def gradient_kernel(scale, query_ref, key_ref, value_ref, grad_ref, inside_ref, before_ref, after_ref,
+                    carried_ref, returned_ref, query_out, key_out, value_out):
+    inside = inside_ref[...] > 0.5
+    before = before_ref[...]
+    after = after_ref[...]
+    contract_last = (((1,), (1,)), ((), ()))
+
+    def halves(state):
+        upper = state.astype(jnp.bfloat16)
+        return upper, (state - upper.astype(jnp.float32)).astype(jnp.bfloat16)
+
+    def across(rows, state, form):
+        upper, lower = halves(state)
+        if form == "nt":
+            first = lax.dot_general(rows, upper, contract_last, preferred_element_type=jnp.float32)
+            return first + lax.dot_general(rows, lower, contract_last, preferred_element_type=jnp.float32)
+        first = jnp.dot(rows, upper, preferred_element_type=jnp.float32)
+        return first + jnp.dot(rows, lower, preferred_element_type=jnp.float32)
+
+    for part in range(query_ref.shape[1] // HD):
+        cols = pl.ds(part * HD, HD)
+        query_h = query_ref[:, cols]
+        key_h = key_ref[:, cols]
+        value_h = value_ref[:, cols]
+        grad_h = grad_ref[:, cols]
+        scores = lax.dot_general(query_h, key_h, contract_last, preferred_element_type=jnp.float32)
+        scaled = jnp.where(inside, scale * scores, 0.0)
+        grad_scores = lax.dot_general(grad_h, value_h, contract_last, preferred_element_type=jnp.float32)
+        mixed = jnp.where(inside, scale * grad_scores, 0.0)
+        carried = carried_ref[part]
+        returned = returned_ref[part]
+        query_out[:, cols] = (
+            jnp.dot(mixed.astype(jnp.bfloat16), key_h, preferred_element_type=jnp.float32)
+            + before * scale * across(grad_h, carried, "nt")
+        ).astype(jnp.bfloat16)
+        key_out[:, cols] = (
+            jnp.dot(mixed.T.astype(jnp.bfloat16), query_h, preferred_element_type=jnp.float32)
+            + after * scale * across(value_h, returned, "nt")
+        ).astype(jnp.bfloat16)
+        value_out[:, cols] = (
+            jnp.dot(scaled.T.astype(jnp.bfloat16), grad_h, preferred_element_type=jnp.float32)
+            + after * scale * across(key_h, returned, "nn")
+        ).astype(jnp.bfloat16)
+
+
+def gradients(scale, queries, key_rows, value_rows, grad_flat, inside, before, after, carried, returned):
+    flat = jax.ShapeDtypeStruct(queries.shape, jnp.bfloat16)
+    vmem = pl.BlockSpec(memory_space=pltpu.VMEM)
+    rows = queries.shape[0]
+    wide = lambda mask: jnp.broadcast_to(mask.astype(jnp.float32)[:, None], (rows, HD))
+    return pl.pallas_call(
+        functools.partial(gradient_kernel, scale),
+        out_shape=(flat, flat, flat),
+        in_specs=[vmem] * 9,
+        out_specs=(vmem, vmem, vmem),
+    )(queries, key_rows, value_rows, grad_flat, inside.astype(jnp.float32), wide(before), wide(after), carried, returned)
+
+
 def join_states(earlier_part, later_part):
     return (
         later_part[0] + (1.0 - later_part[1]) * earlier_part[0],
@@ -272,27 +330,11 @@
     )
     reach_ahead = (dial_end[token_count - 1] + token_count - 1) // token_count - 1 - block_index
     returned = scan_window(back_element, first_end > block_begin + token_count, reach_ahead, -1, 1)
-    grad_scores = jnp.einsum(
-        "the,she->hts", grad_weight, value_h, preferred_element_type=jnp.float32
-    )
-    grad_mix = jnp.where(inside[None], score_scale * grad_scores, 0.0).astype(jnp.bfloat16)
-    to_after = (dial_end > block_begin + token_count).astype(jnp.float32)[:, None, None]
-    query_grad = jnp.einsum(
-        "hts,shd->thd", grad_mix, key_h, preferred_element_type=jnp.float32
-    ) + from_before * score_scale * state_product("the,hde->thd", grad_weight, carried)
-    key_grad = jnp.einsum(
-        "hts,thd->shd", grad_mix, query_h, preferred_element_type=jnp.float32
-    ) + to_after * score_scale * state_product("she,hde->shd", value_h, returned)
-    value_grad = jnp.einsum(
-        "hts,the->she", weights, grad_weight, preferred_element_type=jnp.float32
-    ) + to_after * score_scale * state_product("shd,hde->she", key_h, returned)
-    flat_shape = (token_count, head_count * HD)
-    return (
-        normed,
-        query_grad.reshape(flat_shape).astype(jnp.bfloat16),
-        key_grad.reshape(flat_shape).astype(jnp.bfloat16),
-        value_grad.reshape(flat_shape).astype(jnp.bfloat16),
-    )
+    query_grad, key_grad, value_grad = gradients(
+        score_scale, queries, key_rows, value_rows, grad_weight.reshape(queries.shape), inside,
+        dial_start < block_begin, dial_end > block_begin + token_count, carried, returned,
+    )
+    return (normed, query_grad, key_grad, value_grad)
 
 
 def solution(mesh):

time: 114 us -> 117 us (1.026)
  Pallas kernels: 92.2 us -> 97 us
  local copies, waits for them, and re-layouts: 8.34 us -> 5.62 us
  other arithmetic: 5.31 us -> 7.82 us
  matrix products: 6.13 us -> 4.22 us
    pallas_call x0 -> x1, Pallas kernels: none -> 4.81 us  [gradients(): pl.pallas_call(functools.partial(gradient_kernel, scale), out_shape=(flat...]
    unnamed x16 -> x14, local copies, waits for them, and re-layouts: 4.69 us -> 2.31 us
    convert_element_type x1 -> x3, other arithmetic: 1.35 us -> 3.34 us  [the longest x1 1.37 us: gradients(): inside.astype(jnp.float32)]
    broadcast_in_dim x0 -> x2, local copies, waits for them, and re-layouts: none -> 1.42 us  [gradients(): jnp.broadcast_to(mask.astype(jnp.float32)[:, None], (rows, HD))]
    dot_general x5 -> x0, matrix products: 1.41 us -> none  [the longest x1 0.34 us: shards(): jnp.einsum('the,she->hts', grad_weight, value_h, preferred_element_type=j...]
    reshape x2 -> x0, local copies, waits for them, and re-layouts: 1.4 us -> none  [the longest x1 1.24 us: scan_window(): return pl.pallas_call(functools.partial(chain_kernel, count, step), out_s...]
where the time goes in v11:
time: 117 us
  Pallas kernels  97 us (83%)
  other arithmetic  7.82 us (7%)
  local copies, waits for them, and re-layouts  5.62 us (5%)
  matrix products  4.22 us (4%)
  between operations  2.06 us (2%)
    pallas_call x2, Pallas kernels, scan_window(): pl.pallas_call(functools.partial(chain_kernel, count, step), out_shape=ja...  84.2 us
    pallas_call x1, Pallas kernels, head_sum(): pl.pallas_call(functools.partial(head_sum_kernel, count), out_shape=jax.S...  8.03 us
    pallas_call x1, Pallas kernels, gradients(): pl.pallas_call(functools.partial(gradient_kernel, scale), out_shape=(flat...  4.81 us

profile of v11, /device:TPU:16, one launch (start us, length us, event | category | flops | bytes accessed | tf_op | source)
XLA Modules:
  0.0 116.7 jit_solution(15751697564548949114)
XLA Ops:
  0.6 0.0 copy-start.3
  0.7 1.3 %slice.12 = s32[1]{0:T(128)} slice(s32[128]{0:T(128)} %param.12), slice={[127:128]} | slice | bytes 8 | tf_op jit(solution)/shard_map/slice | solution.py:294
  3.2 0.7 compare_convert_fusion
  3.9 0.7 broadcast_compare_fusion.1
  4.6 0.7 compare_select_fusion
  5.2 0.1 pad.2.clone
  5.3 1.3 %compare_convert_fusion.1 = (f32[128]{0:T(128)S(1)}, pred[128]{0:T(512)(128)(4,1)S(1)}) fusion(s32[128]{0:T(128)} %param.12, s32[]{:T(128)S(6)} %mul.96, s32[]{:T(128)} %bitcast.69), kind=kLoop, calls=%fused_computation.41 | loop fusion | flops 512 | bytes 1160 | tf_op jit(solution)/shard_map/convert_element_type | solution.py:310
  6.6 0.7 broadcast_in_dim.72.before_ref
  7.3 0.7 broadcast_in_dim.73.after_ref
  8.0 1.4 %fusion.36 = (f32[128,128]{1,0:T(8,128)}, pred[128,128]{1,0:T(8,128)(4,1)S(1)}) fusion(s32[128]{0:T(128)} %param.12, s32[128]{0:T(128)S(1)} %iota_add_fusion), kind=kLoop, calls=%fused_computation.54 | loop fusion | flops 65536 | bytes 82944 | tf_op jit(solution)/shard_map/convert_element_type | solution.py:261
  9.4 0.0 copy-done.3
  9.4 0.0 copy-start.4
  9.4 0.2 copy.25
  9.6 0.8 copy-done.4
  10.4 0.0 copy-start.1
  10.4 0.2 copy.23
  10.5 0.8 copy-done.1
  11.3 1.0 fusion.13
  12.3 46.2 %shard_map.102 = f32[32,32,128]{2,1,0:T(8,128)} custom-call(f32[1]{0:T(128)} %bitcast.3.flag_ref, f32[32,32,128]{2,1,0:T(8,128)} %bitcast.64), custom_call_target="tpu_custom_call" | custom-call | tf_op jit(solution)/shard_map/pallas_call | solution.py:131
  58.5 0.0 copy-start
  58.5 1.4 %fusion.25 = f32[8,128,128]{2,1,0:T(8,128)S(1)} fusion(bf16[128,8,128]{0,2,1:T(8,128)(2,1)S(1)} %bitcast.56, f32[8,128,128]{2,1,0:T(8,128)} %bitcast.53), kind=kOutput, calls=%fused_computation.33 | convolution fusion | flops 33685504 | bytes 1310720 | tf_op jit(solution)/shard_map/thd,hde->the/dot_general | solution.py:279
  59.9 0.0 copy-done
  59.9 0.3 fusion.2
  60.2 0.5 multiply_reduce_fusion
  60.7 0.0 copy-start.5
  60.8 0.0 copy-start.6
  60.8 0.2 copy.24
  61.0 0.7 copy-done.5
  61.7 0.0 copy-done.6
  61.7 0.2 fusion.6
  61.9 0.7 maximum_maximum_fusion.parts_ref
  62.5 8.0 %shard_map.103 = f32[8,128]{1,0:T(8,128)} custom-call(f32[8,128]{1,0:T(8,128)} %maximum_maximum_fusion.parts_ref), custom_call_target="tpu_custom_call" | custom-call | tf_op jit(solution)/shard_map/pallas_call | solution.py:191
  70.6 0.8 fusion.31
  71.3 0.7 rsqrt_bitcast_fusion
  72.0 0.9 fusion.8
  72.9 0.0 copy-start.2
  72.9 1.0 fusion.9
  73.9 0.0 copy-done.2
  73.9 38.0 %shard_map.104 = f32[32,32,128]{2,1,0:T(8,128)} custom-call(f32[1]{0:T(128)} %bitcast.13.flag_ref, f32[32,32,128]{2,1,0:T(8,128)} %bitcast.63), custom_call_target="tpu_custom_call" | custom-call | tf_op jit(solution)/shard_map/pallas_call | solution.py:131
  111.9 4.8 %shard_map.105 = (bf16[128,1024]{1,0:T(8,128)(2,1)}, bf16[128,1024]{1,0:T(8,128)(2,1)}, bf16[128,1024]{1,0:T(8,128)(2,1)}) custom-call(bf16[128,1024]{1,0:T(8,128)(2,1)} %query_ref.1, bf16[128,1024]{1,0:T(8,128)(2,1)} %key_ref.1, bf16[128,1024]{1,0:T(8,128)(2,1)} %value_ref.1, bf16[128,1024]{1,0:T(8,128)(2,1)} %copy-done.2, ...), custom_call_target="tpu_custom_call" | custom-call | tf_op jit(solution)/shard_map/pallas_call | solution.py:256
  (2 shorter events, 0.0 us)
Async XLA Ops:
  0.6 8.8 %copy-start.3 = (bf16[128,1024]{1,0:T(8,128)(2,1)S(1)}, bf16[128,1024]{1,0:T(8,128)(2,1)}, u32[]{:S(2)}) copy-start(bf16[128,1024]{1,0:T(8,128)(2,1)} %query_ref.1) | copy-start | bytes 786436
  9.4 1.0 copy-start.4
  10.4 0.9 copy-start.1
  58.5 1.4 %copy-start = (f32[32,32,128]{2,1,0:T(8,128)S(1)}, f32[32,32,128]{2,1,0:T(8,128)}, u32[]{:S(2)}) copy-start(f32[32,32,128]{2,1,0:T(8,128)} %shard_map.102) | copy-start | bytes 1572868
  60.7 1.0 copy-start.5
  60.8 1.0 copy-start.6
  72.9 1.0 copy-start.2

commit v12 on v11

--- a/solution.py
+++ b/solution.py
@@ -31,7 +31,11 @@
     return (reach >= 1).astype(jnp.float32) * total
 
 
-def chain_kernel(count, step, flag_ref, element_ref, out_ref, link_slot, state_slot, sent_slot, send_sems, recv_sems):
+def chain_kernel(count, step, side_work, extra_in, flag_ref, element_ref, *refs):
+    side_in = refs[:extra_in]
+    out_ref = refs[extra_in]
+    link_slot, state_slot, sent_slot, send_sems, recv_sems = refs[-5:]
+    side_out = refs[extra_in + 1:-5]
     me = lax.axis_index("seq")
     head = lax.axis_index("head")
     heads = element_ref.shape[0]
@@ -86,6 +90,7 @@
             into_state.start()
 
         sends.append((into_link, into_state))
+    side_work(side_in, side_out)
     state_sends = []
     for part in range(heads):
         @pl.when(behind_exists)
@@ -121,18 +126,42 @@
             state_sends[part].wait_send()
 
 
-def scan_window(element, flag, reach, step, ident):
+def no_side_work(side_in, side_out):
+    del side_in, side_out
+
+
+def backward_local(scale, side_in, side_out):
+    query_ref, key_ref, value_ref, grad_ref, inside_ref = side_in
+    query_out, key_out, value_out = side_out
+    inside = inside_ref[...] > 0.5
+    contract_last = (((1,), (1,)), ((), ()))
+    for part in range(query_ref.shape[1] // HD):
+        cols = pl.ds(part * HD, HD)
+        query_h = query_ref[:, cols]
+        key_h = key_ref[:, cols]
+        grad_h = grad_ref[:, cols]
+        scores = lax.dot_general(query_h, key_h, contract_last, preferred_element_type=jnp.float32)
+        scaled = jnp.where(inside, scale * scores, 0.0)
+        grad_scores = lax.dot_general(
+            grad_h, value_ref[:, cols], contract_last, preferred_element_type=jnp.float32
+        )
+        mixed = jnp.where(inside, scale * grad_scores, 0.0)
+        query_out[:, cols] = jnp.dot(mixed.astype(jnp.bfloat16), key_h, preferred_element_type=jnp.float32)
+        key_out[:, cols] = jnp.dot(mixed.T.astype(jnp.bfloat16), query_h, preferred_element_type=jnp.float32)
+        value_out[:, cols] = jnp.dot(scaled.T.astype(jnp.bfloat16), grad_h, preferred_element_type=jnp.float32)
+
+
+def scan_window(element, flag, step, ident, side_work=no_side_work, side_inputs=(), side_shapes=()):
     count = lax.axis_size("seq")
-    if count % 4:
-        return scan_window_permutes(element, reach, step)
     shape = element.shape
     element = element.reshape(shape[0] * PIECES, shape[1] // PIECES, shape[2])
     heads = element.shape[0]
-    return pl.pallas_call(
-        functools.partial(chain_kernel, count, step),
-        out_shape=jax.ShapeDtypeStruct(element.shape, jnp.float32),
-        in_specs=[pl.BlockSpec(memory_space=pltpu.SMEM), pl.BlockSpec(memory_space=pltpu.VMEM)],
-        out_specs=pl.BlockSpec(memory_space=pltpu.VMEM),
+    vmem = pl.BlockSpec(memory_space=pltpu.VMEM)
+    outs = pl.pallas_call(
+        functools.partial(chain_kernel, count, step, side_work, len(side_inputs)),
+        out_shape=(jax.ShapeDtypeStruct(element.shape, jnp.float32),) + tuple(side_shapes),
+        in_specs=[pl.BlockSpec(memory_space=pltpu.SMEM)] + [vmem] * (1 + len(side_inputs)),
+        out_specs=(vmem,) * (1 + len(side_shapes)),
         scratch_shapes=[
             pltpu.VMEM(element.shape, jnp.float32),
             pltpu.VMEM(element.shape, jnp.float32),
@@ -141,7 +170,8 @@
             pltpu.SemaphoreType.DMA((2, heads)),
         ],
         compiler_params=pltpu.CompilerParams(collective_id=ident, has_side_effects=True),
-    )(flag.astype(jnp.float32).reshape(1), element).reshape(shape)
+    )(flag.astype(jnp.float32).reshape(1), element, *side_inputs)
+    return (outs[0].reshape(shape),) + tuple(outs[1:])
 
 def head_sum_kernel(count, parts_ref, out_ref, slots, send_sems, recv_sems):
     me = lax.axis_index("head")
@@ -203,9 +233,9 @@
     return total[0], total[1]
 
 
-def gradient_kernel(scale, query_ref, key_ref, value_ref, grad_ref, inside_ref, before_ref, after_ref,
-                    carried_ref, returned_ref, query_out, key_out, value_out):
-    inside = inside_ref[...] > 0.5
+def gradient_kernel(scale, query_ref, key_ref, value_ref, grad_ref, before_ref, after_ref,
+                    carried_ref, returned_ref, query_local, key_local, value_local,
+                    query_out, key_out, value_out):
     before = before_ref[...]
     after = after_ref[...]
     contract_last = (((1,), (1,)), ((), ()))
@@ -224,31 +254,20 @@
 
     for part in range(query_ref.shape[1] // HD):
         cols = pl.ds(part * HD, HD)
-        query_h = query_ref[:, cols]
-        key_h = key_ref[:, cols]
-        value_h = value_ref[:, cols]
-        grad_h = grad_ref[:, cols]
-        scores = lax.dot_general(query_h, key_h, contract_last, preferred_element_type=jnp.float32)
-        scaled = jnp.where(inside, scale * scores, 0.0)
-        grad_scores = lax.dot_general(grad_h, value_h, contract_last, preferred_element_type=jnp.float32)
-        mixed = jnp.where(inside, scale * grad_scores, 0.0)
         carried = carried_ref[part]
         returned = returned_ref[part]
         query_out[:, cols] = (
-            jnp.dot(mixed.astype(jnp.bfloat16), key_h, preferred_element_type=jnp.float32)
-            + before * scale * across(grad_h, carried, "nt")
+            query_local[:, cols] + before * scale * across(grad_ref[:, cols], carried, "nt")
         ).astype(jnp.bfloat16)
         key_out[:, cols] = (
-            jnp.dot(mixed.T.astype(jnp.bfloat16), query_h, preferred_element_type=jnp.float32)
-            + after * scale * across(value_h, returned, "nt")
+            key_local[:, cols] + after * scale * across(value_ref[:, cols], returned, "nt")
         ).astype(jnp.bfloat16)
         value_out[:, cols] = (
-            jnp.dot(scaled.T.astype(jnp.bfloat16), grad_h, preferred_element_type=jnp.float32)
-            + after * scale * across(key_h, returned, "nn")
+            value_local[:, cols] + after * scale * across(key_ref[:, cols], returned, "nn")
         ).astype(jnp.bfloat16)
 
 
-def gradients(scale, queries, key_rows, value_rows, grad_flat, inside, before, after, carried, returned):
+def gradients(scale, queries, key_rows, value_rows, grad_flat, before, after, carried, returned, local):
     flat = jax.ShapeDtypeStruct(queries.shape, jnp.bfloat16)
     vmem = pl.BlockSpec(memory_space=pltpu.VMEM)
     rows = queries.shape[0]
@@ -256,10 +275,9 @@
     return pl.pallas_call(
         functools.partial(gradient_kernel, scale),
         out_shape=(flat, flat, flat),
-        in_specs=[vmem] * 9,
+        in_specs=[vmem] * 11,
         out_specs=(vmem, vmem, vmem),
-    )(queries, key_rows, value_rows, grad_flat, inside.astype(jnp.float32), wide(before), wide(after), carried, returned)
-
+    )(queries, key_rows, value_rows, grad_flat, wide(before), wide(after), carried, returned, *local)
 
 def join_states(earlier_part, later_part):
     return (
@@ -299,9 +317,7 @@
         value_h,
         preferred_element_type=jnp.float32,
     )
-    block_index = lax.axis_index("seq")
-    reach_back = block_index - dial_start[0] // token_count
-    carried = scan_window(element, last_start < block_begin, reach_back, 1, 0)
+    carried = scan_window(element, last_start < block_begin, 1, 0)[0]
     inside = (position[None, :] >= dial_start[:, None]) & (local_pos[None, :] <= local_pos[:, None])
     scores = jnp.einsum("thd,shd->hts", query_h, key_h, preferred_element_type=jnp.float32)
     weights = jnp.where(inside[None], score_scale * scores, 0.0).astype(jnp.bfloat16)
@@ -328,11 +344,17 @@
         grad_weight,
         preferred_element_type=jnp.float32,
     )
-    reach_ahead = (dial_end[token_count - 1] + token_count - 1) // token_count - 1 - block_index
-    returned = scan_window(back_element, first_end > block_begin + token_count, reach_ahead, -1, 1)
+    wide_shape = jax.ShapeDtypeStruct(queries.shape, jnp.float32)
+    grad_flat = grad_weight.reshape(queries.shape)
+    returned, *local = scan_window(
+        back_element, first_end > block_begin + token_count, -1, 1,
+        functools.partial(backward_local, score_scale),
+        (queries, key_rows, value_rows, grad_flat, inside.astype(jnp.float32)),
+        (wide_shape,) * 3,
+    )
     query_grad, key_grad, value_grad = gradients(
-        score_scale, queries, key_rows, value_rows, grad_weight.reshape(queries.shape), inside,
-        dial_start < block_begin, dial_end > block_begin + token_count, carried, returned,
+        score_scale, queries, key_rows, value_rows, grad_flat,
+        dial_start < block_begin, dial_end > block_begin + token_count, carried, returned, local,
     )
     return (normed, query_grad, key_grad, value_grad)
 

time: 117 us -> 117 us (level)
  no operation moved by 1% of the time
where the time goes in v12:
time: 117 us
  Pallas kernels  97.1 us (83%)
  other arithmetic  7.79 us (7%)
  local copies, waits for them, and re-layouts  5.59 us (5%)
  matrix products  4.21 us (4%)
  between operations  2.06 us (2%)
    pallas_call x2, Pallas kernels, scan_window(): pl.pallas_call(functools.partial(chain_kernel, count, step, side_work, le...  85.2 us
    pallas_call x1, Pallas kernels, head_sum(): pl.pallas_call(functools.partial(head_sum_kernel, count), out_shape=jax.S...  8.02 us
    pallas_call x1, Pallas kernels, gradients(): pl.pallas_call(functools.partial(gradient_kernel, scale), out_shape=(flat...  3.87 us

profile of v12, /device:TPU:16, one launch (start us, length us, event | category | flops | bytes accessed | tf_op | source)
XLA Modules:
  0.0 116.7 jit_solution(15896630140705361207)
XLA Ops:
  0.6 0.0 copy-start.3
  0.7 1.3 %slice.12 = s32[1]{0:T(128)} slice(s32[128]{0:T(128)} %param.12), slice={[127:128]} | slice | bytes 8 | tf_op jit(solution)/shard_map/slice | solution.py:312
  3.2 0.7 compare_convert_fusion
  3.9 0.7 broadcast_compare_fusion.1
  4.6 0.7 compare_select_fusion
  5.2 0.1 pad.2.clone
  5.3 1.3 %compare_convert_fusion.1 = (f32[128]{0:T(128)S(1)}, pred[128]{0:T(512)(128)(4,1)S(1)}) fusion(s32[128]{0:T(128)} %param.12, s32[]{:T(128)S(6)} %mul.96, s32[]{:T(128)} %bitcast.69), kind=kLoop, calls=%fused_computation.41 | loop fusion | flops 512 | bytes 1160 | tf_op jit(solution)/shard_map/convert_element_type | solution.py:326
  6.6 0.7 broadcast_in_dim.72.before_ref
  7.3 0.7 broadcast_in_dim.73.after_ref
  8.0 1.4 %fusion.36 = (f32[128,128]{1,0:T(8,128)}, pred[128,128]{1,0:T(8,128)(4,1)S(1)}) fusion(s32[128]{0:T(128)} %param.12, s32[128]{0:T(128)S(1)} %iota_add_fusion), kind=kLoop, calls=%fused_computation.54 | loop fusion | flops 65536 | bytes 82944 | tf_op jit(solution)/shard_map/convert_element_type | solution.py:352
  9.4 0.0 copy-done.3
  9.4 0.0 copy-start.4
  9.4 0.2 copy.25
  9.5 0.8 copy-done.4
  10.3 0.0 copy-start.1
  10.3 0.2 copy.23
  10.5 0.8 copy-done.1
  11.3 1.0 fusion.13
  12.3 46.2 %shard_map.102 = f32[32,32,128]{2,1,0:T(8,128)} custom-call(f32[1]{0:T(128)} %bitcast.3.flag_ref, f32[32,32,128]{2,1,0:T(8,128)} %bitcast.64), custom_call_target="tpu_custom_call" | custom-call | tf_op jit(solution)/shard_map/pallas_call | solution.py:160
  58.5 0.0 copy-start
  58.5 1.4 %fusion.25 = f32[8,128,128]{2,1,0:T(8,128)S(1)} fusion(bf16[128,8,128]{0,2,1:T(8,128)(2,1)S(1)} %bitcast.56, f32[8,128,128]{2,1,0:T(8,128)} %bitcast.53), kind=kOutput, calls=%fused_computation.33 | convolution fusion | flops 33685504 | bytes 1310720 | tf_op jit(solution)/shard_map/thd,hde->the/dot_general | solution.py:297
  59.9 0.0 copy-done
  59.9 0.3 fusion.2
  60.2 0.5 multiply_reduce_fusion
  60.7 0.0 copy-start.5
  60.7 0.0 copy-start.6
  60.7 0.2 copy.24
  60.9 0.7 copy-done.5
  61.7 0.0 copy-done.6
  61.7 0.2 fusion.6
  61.8 0.7 maximum_maximum_fusion.parts_ref
  62.5 8.0 %shard_map.103 = f32[8,128]{1,0:T(8,128)} custom-call(f32[8,128]{1,0:T(8,128)} %maximum_maximum_fusion.parts_ref), custom_call_target="tpu_custom_call" | custom-call | tf_op jit(solution)/shard_map/pallas_call | solution.py:221
  70.5 0.7 fusion.31
  71.3 0.7 rsqrt_bitcast_fusion
  71.9 0.9 fusion.8
  72.8 0.0 copy-start.2
  72.8 1.0 fusion.9
  73.9 0.0 copy-done.2
  73.9 39.0 %shard_map.104 = (f32[32,32,128]{2,1,0:T(8,128)}, f32[128,1024]{1,0:T(8,128)}, f32[128,1024]{1,0:T(8,128)}, f32[128,1024]{1,0:T(8,128)}) custom-call(f32[1]{0:T(128)} %bitcast.13.flag_ref, f32[32,32,128]{2,1,0:T(8,128)} %bitcast.62, bf16[128,1024]{1,0:T(8,128)(2,1)} %query_ref.1, bf16[128,1024]{1,0:T(8,128)(2,1)} %key_ref.1, bf16[128,1024]{1,0:T(8,128)(2,1)} %value_ref.1, ...), custom_call_target="tpu_custom_call" | custom-call | tf_op jit(solution)/shard_map/pallas_call | solution.py:160
  112.8 3.9 %shard_map.105 = (bf16[128,1024]{1,0:T(8,128)(2,1)}, bf16[128,1024]{1,0:T(8,128)(2,1)}, bf16[128,1024]{1,0:T(8,128)(2,1)}) custom-call(bf16[128,1024]{1,0:T(8,128)(2,1)} %query_ref.1, bf16[128,1024]{1,0:T(8,128)(2,1)} %key_ref.1, bf16[128,1024]{1,0:T(8,128)(2,1)} %value_ref.1, bf16[128,1024]{1,0:T(8,128)(2,1)} %copy-done.2, ...), custom_call_target="tpu_custom_call" | custom-call | tf_op jit(solution)/shard_map/pallas_call | solution.py:275
  (2 shorter events, 0.0 us)
Async XLA Ops:
  0.6 8.7 %copy-start.3 = (bf16[128,1024]{1,0:T(8,128)(2,1)S(1)}, bf16[128,1024]{1,0:T(8,128)(2,1)}, u32[]{:S(2)}) copy-start(bf16[128,1024]{1,0:T(8,128)(2,1)} %query_ref.1) | copy-start | bytes 786436
  9.4 1.0 copy-start.4
  10.3 0.9 copy-start.1
  58.5 1.4 %copy-start = (f32[32,32,128]{2,1,0:T(8,128)S(1)}, f32[32,32,128]{2,1,0:T(8,128)}, u32[]{:S(2)}) copy-start(f32[32,32,128]{2,1,0:T(8,128)} %shard_map.102) | copy-start | bytes 1572868
  60.7 1.0 copy-start.5
  60.7 1.0 copy-start.6
  72.8 1.0 copy-start.2

commit v13 on v12

--- a/solution.py
+++ b/solution.py
@@ -318,6 +318,7 @@
         preferred_element_type=jnp.float32,
     )
     carried = scan_window(element, last_start < block_begin, 1, 0)[0]
+    carried, query_h, key_h, value_h = lax.optimization_barrier((carried, query_h, key_h, value_h))
     inside = (position[None, :] >= dial_start[:, None]) & (local_pos[None, :] <= local_pos[:, None])
     scores = jnp.einsum("thd,shd->hts", query_h, key_h, preferred_element_type=jnp.float32)
     weights = jnp.where(inside[None], score_scale * scores, 0.0).astype(jnp.bfloat16)

time: 117 us -> 116 us (level)
  no operation moved by 1% of the time
where the time goes in v13:
time: 116 us
  Pallas kernels  97.2 us (84%)
  other arithmetic  7.79 us (7%)
  local copies, waits for them, and re-layouts  5.71 us (5%)
  matrix products  3.2 us (3%)
  between operations  2.08 us (2%)
    pallas_call x2, Pallas kernels, scan_window(): pl.pallas_call(functools.partial(chain_kernel, count, step, side_work, le...  85.3 us
    pallas_call x1, Pallas kernels, head_sum(): pl.pallas_call(functools.partial(head_sum_kernel, count), out_shape=jax.S...  8.02 us
    pallas_call x1, Pallas kernels, gradients(): pl.pallas_call(functools.partial(gradient_kernel, scale), out_shape=(flat...  3.87 us

profile of v13, /device:TPU:16, one launch (start us, length us, event | category | flops | bytes accessed | tf_op | source)
XLA Modules:
  0.0 116.0 jit_solution(3133036062757087251)
XLA Ops:
  0.6 0.0 copy-start.1
  0.7 1.3 %slice.12 = s32[1]{0:T(128)} slice(s32[128]{0:T(128)} %param.12), slice={[127:128]} | slice | bytes 8 | tf_op jit(solution)/shard_map/slice | solution.py:312
  3.2 0.7 compare_convert_fusion
  3.9 0.7 broadcast_compare_fusion.1
  4.6 0.7 compare_select_fusion
  5.2 0.1 pad.2.clone
  5.3 1.3 %compare_convert_fusion.1 = (f32[128]{0:T(128)S(1)}, pred[128]{0:T(512)(128)(4,1)S(1)}) fusion(s32[128]{0:T(128)} %param.12, s32[]{:T(128)S(6)} %mul.94, s32[]{:T(128)} %bitcast.65), kind=kLoop, calls=%fused_computation.41 | loop fusion | flops 512 | bytes 1160 | tf_op jit(solution)/shard_map/convert_element_type | solution.py:327
  6.6 0.7 broadcast_in_dim.72.before_ref
  7.3 0.7 broadcast_in_dim.73.after_ref
  8.0 1.4 %fusion.38 = (f32[128,128]{1,0:T(8,128)}, pred[128,128]{1,0:T(8,128)(4,1)S(1)}) fusion(s32[128]{0:T(128)} %param.12, s32[128]{0:T(128)S(1)} %iota_add_fusion), kind=kLoop, calls=%fused_computation.54 | loop fusion | flops 65536 | bytes 82944 | tf_op jit(solution)/shard_map/convert_element_type | solution.py:353
  9.4 0.0 copy-done.1
  9.4 0.0 copy-start.4
  9.4 0.9 copy-done.4
  10.4 0.2 copy.11
  10.6 1.0 fusion.13
  11.6 0.0 copy-start.3
  11.6 46.3 %shard_map.102 = f32[32,32,128]{2,1,0:T(8,128)} custom-call(f32[1]{0:T(128)} %bitcast.1.flag_ref, f32[32,32,128]{2,1,0:T(8,128)} %bitcast.58), custom_call_target="tpu_custom_call" | custom-call | tf_op jit(solution)/shard_map/pallas_call | solution.py:160
  58.0 0.0 copy-done.3
  58.0 0.2 copy.19
  58.3 0.0 copy-start
  58.3 0.5 fusion.4
  58.8 0.5 copy-done
  59.3 0.3 fusion.27
  59.6 0.4 fusion.9
  60.0 0.0 copy-start.5
  60.0 0.0 copy-start.6
  60.0 0.2 copy.24
  60.2 0.7 copy-done.5
  60.9 0.0 copy-done.6
  60.9 0.2 fusion.6
  61.1 0.7 maximum_maximum_fusion.parts_ref
  61.7 8.0 %shard_map.103 = f32[8,128]{1,0:T(8,128)} custom-call(f32[8,128]{1,0:T(8,128)} %maximum_maximum_fusion.parts_ref), custom_call_target="tpu_custom_call" | custom-call | tf_op jit(solution)/shard_map/pallas_call | solution.py:221
  69.8 0.7 fusion.33
  70.5 0.7 rsqrt_bitcast_fusion
  71.2 0.9 fusion.8
  72.1 0.0 copy-start.2
  72.1 1.0 fusion.10
  73.1 0.0 copy-done.2
  73.1 39.0 %shard_map.104 = (f32[32,32,128]{2,1,0:T(8,128)}, f32[128,1024]{1,0:T(8,128)}, f32[128,1024]{1,0:T(8,128)}, f32[128,1024]{1,0:T(8,128)}) custom-call(f32[1]{0:T(128)} %bitcast.12.flag_ref, f32[32,32,128]{2,1,0:T(8,128)} %bitcast.56, bf16[128,1024]{1,0:T(8,128)(2,1)} %query_ref.1, bf16[128,1024]{1,0:T(8,128)(2,1)} %key_ref.1, bf16[128,1024]{1,0:T(8,128)(2,1)} %value_ref.1, ...), custom_call_target="tpu_custom_call" | custom-call | tf_op jit(solution)/shard_map/pallas_call | solution.py:160
  112.1 3.9 %shard_map.105 = (bf16[128,1024]{1,0:T(8,128)(2,1)}, bf16[128,1024]{1,0:T(8,128)(2,1)}, bf16[128,1024]{1,0:T(8,128)(2,1)}) custom-call(bf16[128,1024]{1,0:T(8,128)(2,1)} %query_ref.1, bf16[128,1024]{1,0:T(8,128)(2,1)} %key_ref.1, bf16[128,1024]{1,0:T(8,128)(2,1)} %value_ref.1, bf16[128,1024]{1,0:T(8,128)(2,1)} %copy-done.2, ...), custom_call_target="tpu_custom_call" | custom-call | tf_op jit(solution)/shard_map/pallas_call | solution.py:275
  (5 shorter events, 0.1 us)
Async XLA Ops:
  0.6 8.7 %copy-start.1 = (bf16[128,1024]{1,0:T(8,128)(2,1)S(1)}, bf16[128,1024]{1,0:T(8,128)(2,1)}, u32[]{:S(2)}) copy-start(bf16[128,1024]{1,0:T(8,128)(2,1)} %value_ref.1) | copy-start | bytes 786436
  9.4 1.0 copy-start.4
  11.6 46.3 %copy-start.3 = (bf16[128,1024]{1,0:T(8,128)(2,1)S(1)}, bf16[128,1024]{1,0:T(8,128)(2,1)}, u32[]{:S(2)}) copy-start(bf16[128,1024]{1,0:T(8,128)(2,1)} %query_ref.1) | copy-start | bytes 786436
  58.3 1.0 copy-start
  60.0 1.0 copy-start.5
  60.0 1.0 copy-start.6
  72.1 1.0 copy-start.2

commit v14 on v13

--- a/solution.py
+++ b/solution.py
@@ -131,9 +131,13 @@
 
 
 def backward_local(scale, side_in, side_out):
-    query_ref, key_ref, value_ref, grad_ref, inside_ref = side_in
+    query_ref, key_ref, value_ref, grad_ref, starts_ref = side_in
     query_out, key_out, value_out = side_out
-    inside = inside_ref[...] > 0.5
+    rows = query_ref.shape[0]
+    row = lax.broadcasted_iota(jnp.int32, (rows, rows), 0)
+    col = lax.broadcasted_iota(jnp.int32, (rows, rows), 1)
+    begin = lax.axis_index("seq") * rows
+    inside = (begin + col >= starts_ref[...]) & (col <= row)
     contract_last = (((1,), (1,)), ((), ()))
     for part in range(query_ref.shape[1] // HD):
         cols = pl.ds(part * HD, HD)
@@ -236,8 +240,10 @@
 def gradient_kernel(scale, query_ref, key_ref, value_ref, grad_ref, before_ref, after_ref,
                     carried_ref, returned_ref, query_local, key_local, value_local,
                     query_out, key_out, value_out):
-    before = before_ref[...]
-    after = after_ref[...]
+    rows = query_ref.shape[0]
+    begin = lax.axis_index("seq") * rows
+    before = (before_ref[...] < begin).astype(jnp.float32)
+    after = (after_ref[...] > begin + rows).astype(jnp.float32)
     contract_last = (((1,), (1,)), ((), ()))
 
     def halves(state):
@@ -271,7 +277,7 @@
     flat = jax.ShapeDtypeStruct(queries.shape, jnp.bfloat16)
     vmem = pl.BlockSpec(memory_space=pltpu.VMEM)
     rows = queries.shape[0]
-    wide = lambda mask: jnp.broadcast_to(mask.astype(jnp.float32)[:, None], (rows, HD))
+    wide = lambda bounds: bounds.reshape(rows, 1)
     return pl.pallas_call(
         functools.partial(gradient_kernel, scale),
         out_shape=(flat, flat, flat),
@@ -350,12 +356,12 @@
     returned, *local = scan_window(
         back_element, first_end > block_begin + token_count, -1, 1,
         functools.partial(backward_local, score_scale),
-        (queries, key_rows, value_rows, grad_flat, inside.astype(jnp.float32)),
+        (queries, key_rows, value_rows, grad_flat, dial_start.reshape(token_count, 1)),
         (wide_shape,) * 3,
     )
     query_grad, key_grad, value_grad = gradients(
         score_scale, queries, key_rows, value_rows, grad_flat,
-        dial_start < block_begin, dial_end > block_begin + token_count, carried, returned, local,
+        dial_start, dial_end, carried, returned, local,
     )
     return (normed, query_grad, key_grad, value_grad)
 

time: 116 us -> 114 us (0.983)
  other arithmetic: 7.79 us -> 3.96 us
  local copies, waits for them, and re-layouts: 5.71 us -> 7.19 us
    convert_element_type x3 -> x0, other arithmetic: 3.34 us -> none  [the longest x1 1.37 us: shards(): inside.astype(jnp.float32)]
    unnamed x17 -> x21, local copies, waits for them, and re-layouts: 2.3 us -> 4.4 us
where the time goes in v14:
time: 114 us; the launch traced here: 113 us
  Pallas kernels  97.2 us (85%)
  local copies, waits for them, and re-layouts  7.19 us (6%)
  other arithmetic  3.96 us (3%)
  matrix products  3.2 us (3%)
  between operations  1.52 us (1%)
    pallas_call x2, Pallas kernels, scan_window(): pl.pallas_call(functools.partial(chain_kernel, count, step, side_work, le...  85.3 us
    pallas_call x1, Pallas kernels, head_sum(): pl.pallas_call(functools.partial(head_sum_kernel, count), out_shape=jax.S...  8.04 us
    unnamed x21, local copies, waits for them, and re-layouts  4.4 us
    pallas_call x1, Pallas kernels, gradients(): pl.pallas_call(functools.partial(gradient_kernel, scale), out_shape=(flat...  3.88 us

profile of v14, /device:TPU:16, one launch (start us, length us, event | category | flops | bytes accessed | tf_op | source)
XLA Modules:
  0.0 113.1 jit_solution(13189928736172180432)
XLA Ops:
  0.6 0.0 copy-start.7
  0.7 0.6 copy-done.7
  1.3 0.6 slice.12
  2.5 0.0 copy-start.8
  2.5 0.6 copy-done.8
  3.3 0.7 broadcast_compare_fusion
  4.0 0.1 pad.2.clone
  4.0 0.1 fusion.31
  4.1 0.7 copy.22.refs_4_.before_ref
  4.9 0.7 copy.23.after_ref
  5.6 0.0 copy-start.4
  5.6 1.0 copy.32
  6.6 0.0 copy-done.4
  6.7 0.0 copy-start.1
  6.7 0.2 copy.11
  7.0 0.7 copy-done.1
  7.7 1.0 fusion.13
  8.7 0.0 copy-start.3
  8.7 46.3 %shard_map.102 = f32[32,32,128]{2,1,0:T(8,128)} custom-call(f32[1]{0:T(128)} %bitcast.1.flag_ref, f32[32,32,128]{2,1,0:T(8,128)} %bitcast.60), custom_call_target="tpu_custom_call" | custom-call | tf_op jit(solution)/shard_map/pallas_call | solution.py:164
  55.0 0.0 copy-done.3
  55.1 0.2 copy.19
  55.3 0.0 copy-start
  55.3 0.5 fusion.4
  55.9 0.5 copy-done
  56.4 0.3 fusion.27
  56.7 0.4 fusion.9
  57.0 0.0 copy-start.5
  57.0 0.0 copy-start.6
  57.0 0.2 copy.27
  57.3 0.7 copy-done.5
  58.0 0.0 copy-done.6
  58.0 0.2 fusion.6
  58.1 0.7 maximum_maximum_fusion.parts_ref
  58.8 8.0 %shard_map.103 = f32[8,128]{1,0:T(8,128)} custom-call(f32[8,128]{1,0:T(8,128)} %maximum_maximum_fusion.parts_ref), custom_call_target="tpu_custom_call" | custom-call | tf_op jit(solution)/shard_map/pallas_call | solution.py:225
  66.8 0.8 fusion.33
  67.6 0.7 rsqrt_bitcast_fusion
  68.3 0.9 fusion.8
  69.2 0.0 copy-start.2
  69.2 1.0 fusion.10
  70.2 0.0 copy-done.2
  70.2 39.0 %shard_map.104 = (f32[32,32,128]{2,1,0:T(8,128)}, f32[128,1024]{1,0:T(8,128)}, f32[128,1024]{1,0:T(8,128)}, f32[128,1024]{1,0:T(8,128)}) custom-call(f32[1]{0:T(128)} %bitcast.14.flag_ref, f32[32,32,128]{2,1,0:T(8,128)} %bitcast.58, bf16[128,1024]{1,0:T(8,128)(2,1)} %query_ref.1, bf16[128,1024]{1,0:T(8,128)(2,1)} %key_ref.1, bf16[128,1024]{1,0:T(8,128)(2,1)} %value_ref.1, ...), custom_call_target="tpu_custom_call" | custom-call | tf_op jit(solution)/shard_map/pallas_call | solution.py:164
  109.2 3.9 %shard_map.105 = (bf16[128,1024]{1,0:T(8,128)(2,1)}, bf16[128,1024]{1,0:T(8,128)(2,1)}, bf16[128,1024]{1,0:T(8,128)(2,1)}) custom-call(bf16[128,1024]{1,0:T(8,128)(2,1)} %query_ref.1, bf16[128,1024]{1,0:T(8,128)(2,1)} %key_ref.1, bf16[128,1024]{1,0:T(8,128)(2,1)} %value_ref.1, bf16[128,1024]{1,0:T(8,128)(2,1)} %copy-done.2, ...), custom_call_target="tpu_custom_call" | custom-call | tf_op jit(solution)/shard_map/pallas_call | solution.py:281
  (5 shorter events, 0.1 us)
Async XLA Ops:
  0.6 0.7 copy-start.7
  2.5 0.7 copy-start.8
  5.6 1.0 copy-start.4
  6.7 1.0 copy-start.1
  8.7 46.4 %copy-start.3 = (bf16[128,1024]{1,0:T(8,128)(2,1)S(1)}, bf16[128,1024]{1,0:T(8,128)(2,1)}, u32[]{:S(2)}) copy-start(bf16[128,1024]{1,0:T(8,128)(2,1)} %query_ref.1) | copy-start | bytes 786436
  55.3 1.0 copy-start
  57.0 1.0 copy-start.5
  57.0 1.0 copy-start.6
  69.2 1.0 copy-start.2

commit v15 on v14

--- a/solution.py
+++ b/solution.py
@@ -137,7 +137,8 @@
     row = lax.broadcasted_iota(jnp.int32, (rows, rows), 0)
     col = lax.broadcasted_iota(jnp.int32, (rows, rows), 1)
     begin = lax.axis_index("seq") * rows
-    inside = (begin + col >= starts_ref[...]) & (col <= row)
+    starts = jnp.broadcast_to(starts_ref[...], (rows, rows)).T
+    inside = (begin + col >= starts) & (col <= row)
     contract_last = (((1,), (1,)), ((), ()))
     for part in range(query_ref.shape[1] // HD):
         cols = pl.ds(part * HD, HD)
@@ -242,8 +243,8 @@
                     query_out, key_out, value_out):
     rows = query_ref.shape[0]
     begin = lax.axis_index("seq") * rows
-    before = (before_ref[...] < begin).astype(jnp.float32)
-    after = (after_ref[...] > begin + rows).astype(jnp.float32)
+    before = (jnp.broadcast_to(before_ref[...], (rows, rows)).T < begin).astype(jnp.float32)
+    after = (jnp.broadcast_to(after_ref[...], (rows, rows)).T > begin + rows).astype(jnp.float32)
     contract_last = (((1,), (1,)), ((), ()))
 
     def halves(state):
@@ -277,7 +278,7 @@
     flat = jax.ShapeDtypeStruct(queries.shape, jnp.bfloat16)
     vmem = pl.BlockSpec(memory_space=pltpu.VMEM)
     rows = queries.shape[0]
-    wide = lambda bounds: bounds.reshape(rows, 1)
+    wide = lambda bounds: bounds.reshape(1, rows)
     return pl.pallas_call(
         functools.partial(gradient_kernel, scale),
         out_shape=(flat, flat, flat),
@@ -356,7 +357,7 @@
     returned, *local = scan_window(
         back_element, first_end > block_begin + token_count, -1, 1,
         functools.partial(backward_local, score_scale),
-        (queries, key_rows, value_rows, grad_flat, dial_start.reshape(token_count, 1)),
+        (queries, key_rows, value_rows, grad_flat, dial_start.reshape(1, token_count)),
         (wide_shape,) * 3,
     )
     query_grad, key_grad, value_grad = gradients(

time: 114 us -> 112 us (0.982)
  local copies, waits for them, and re-layouts: 7.19 us -> 5.72 us
where the time goes in v15:
time: 112 us
  Pallas kernels  97.2 us (87%)
  local copies, waits for them, and re-layouts  5.72 us (5%)
  other arithmetic  3.96 us (4%)
  matrix products  3.19 us (3%)
  between operations  1.53 us (1%)
    pallas_call x2, Pallas kernels, scan_window(): pl.pallas_call(functools.partial(chain_kernel, count, step, side_work, le...  85.3 us
    pallas_call x1, Pallas kernels, head_sum(): pl.pallas_call(functools.partial(head_sum_kernel, count), out_shape=jax.S...  8.04 us
    unnamed x21, local copies, waits for them, and re-layouts  4.41 us
    pallas_call x1, Pallas kernels, gradients(): pl.pallas_call(functools.partial(gradient_kernel, scale), out_shape=(flat...  3.86 us

profile of v15, /device:TPU:16, one launch (start us, length us, event | category | flops | bytes accessed | tf_op | source)
XLA Modules:
  0.0 111.6 jit_solution(15587753417830278144)
XLA Ops:
  0.6 0.0 copy-start.7
  0.7 0.6 copy-done.7
  1.3 0.6 slice.12
  2.5 0.0 copy-start.8
  2.5 0.6 copy-done.8
  3.3 0.7 broadcast_compare_fusion
  4.0 0.1 pad.2.clone
  4.0 0.1 fusion.31
  4.1 0.0 copy-start.4
  4.1 1.0 copy.29
  5.2 0.0 copy-done.4
  5.2 0.0 copy-start.1
  5.3 0.2 copy.11
  5.5 0.7 copy-done.1
  6.2 1.0 fusion.13
  7.2 0.0 copy-start.3
  7.2 46.3 %shard_map.102 = f32[32,32,128]{2,1,0:T(8,128)} custom-call(f32[1]{0:T(128)} %bitcast.1.flag_ref, f32[32,32,128]{2,1,0:T(8,128)} %bitcast.59), custom_call_target="tpu_custom_call" | custom-call | tf_op jit(solution)/shard_map/pallas_call | solution.py:165
  53.6 0.0 copy-done.3
  53.6 0.2 copy.19
  53.9 0.0 copy-start
  53.9 0.5 fusion.4
  54.4 0.5 copy-done
  54.9 0.3 fusion.27
  55.2 0.4 fusion.9
  55.6 0.0 copy-start.5
  55.6 0.0 copy-start.6
  55.6 0.2 copy.24
  55.8 0.7 copy-done.5
  56.5 0.0 copy-done.6
  56.5 0.2 fusion.6
  56.7 0.7 maximum_maximum_fusion.parts_ref
  57.3 8.0 %shard_map.103 = f32[8,128]{1,0:T(8,128)} custom-call(f32[8,128]{1,0:T(8,128)} %maximum_maximum_fusion.parts_ref), custom_call_target="tpu_custom_call" | custom-call | tf_op jit(solution)/shard_map/pallas_call | solution.py:226
  65.4 0.8 fusion.33
  66.2 0.7 rsqrt_bitcast_fusion
  66.8 0.9 fusion.8
  67.8 0.0 copy-start.2
  67.8 1.0 fusion.10
  68.8 0.0 copy-done.2
  68.8 39.0 %shard_map.104 = (f32[32,32,128]{2,1,0:T(8,128)}, f32[128,1024]{1,0:T(8,128)}, f32[128,1024]{1,0:T(8,128)}, f32[128,1024]{1,0:T(8,128)}) custom-call(f32[1]{0:T(128)} %bitcast.14.flag_ref, f32[32,32,128]{2,1,0:T(8,128)} %bitcast.60, bf16[128,1024]{1,0:T(8,128)(2,1)} %query_ref.1, bf16[128,1024]{1,0:T(8,128)(2,1)} %key_ref.1, bf16[128,1024]{1,0:T(8,128)(2,1)} %value_ref.1, ...), custom_call_target="tpu_custom_call" | custom-call | tf_op jit(solution)/shard_map/pallas_call | solution.py:165
  107.8 3.9 %shard_map.105 = (bf16[128,1024]{1,0:T(8,128)(2,1)}, bf16[128,1024]{1,0:T(8,128)(2,1)}, bf16[128,1024]{1,0:T(8,128)(2,1)}) custom-call(bf16[128,1024]{1,0:T(8,128)(2,1)} %query_ref.1, bf16[128,1024]{1,0:T(8,128)(2,1)} %key_ref.1, bf16[128,1024]{1,0:T(8,128)(2,1)} %value_ref.1, bf16[128,1024]{1,0:T(8,128)(2,1)} %copy-done.2, s32[1,128]{1,0:T(1,128)} %bitcast.65, ...), custom_call_target="tpu_custom_call" | custom-call | tf_op jit(solution)/shard_map/pallas_call | solution.py:282
  (5 shorter events, 0.1 us)
Async XLA Ops:
  0.6 0.7 copy-start.7
  2.5 0.7 copy-start.8
  4.1 1.1 copy-start.4
  5.2 1.0 copy-start.1
  7.2 46.4 %copy-start.3 = (bf16[128,1024]{1,0:T(8,128)(2,1)S(1)}, bf16[128,1024]{1,0:T(8,128)(2,1)}, u32[]{:S(2)}) copy-start(bf16[128,1024]{1,0:T(8,128)(2,1)} %query_ref.1) | copy-start | bytes 786436
  53.9 1.0 copy-start
  55.6 1.0 copy-start.5
  55.6 1.0 copy-start.6
  67.8 1.0 copy-start.2

commit v16 on v15

--- a/solution.py
+++ b/solution.py
@@ -31,11 +31,19 @@
     return (reach >= 1).astype(jnp.float32) * total
 
 
-def chain_kernel(count, step, side_work, extra_in, flag_ref, element_ref, *refs):
+def chain_kernel(count, step, side_work, extra_in, prologue, pro_in, flag_ref, *refs):
+    if prologue is None:
+        element_ref, refs = refs[0], refs[1:]
+    pro_refs = refs[:pro_in]
+    refs = refs[pro_in:]
     side_in = refs[:extra_in]
     out_ref = refs[extra_in]
-    link_slot, state_slot, sent_slot, send_sems, recv_sems = refs[-5:]
-    side_out = refs[extra_in + 1:-5]
+    if prologue is None:
+        link_slot, state_slot, sent_slot, send_sems, recv_sems = refs[-5:]
+        side_out = refs[extra_in + 1:-5]
+    else:
+        link_slot, state_slot, sent_slot, send_sems, recv_sems, element_ref = refs[-6:]
+        side_out = refs[extra_in + 1:-6]
     me = lax.axis_index("seq")
     head = lax.axis_index("head")
     heads = element_ref.shape[0]
@@ -48,6 +56,8 @@
         ring_peer = (lax.rem(me + offset + count, count), head)
         pl.semaphore_signal(barrier, inc=1, device_id=ring_peer, device_id_type=pl.DeviceIdType.MESH)
     pl.semaphore_wait(barrier, 2)
+    if prologue is not None:
+        prologue(pro_refs, element_ref)
 
     def describe(kind, part, source, landing):
         return pltpu.make_async_remote_copy(
@@ -156,26 +166,49 @@
         value_out[:, cols] = jnp.dot(scaled.T.astype(jnp.bfloat16), grad_h, preferred_element_type=jnp.float32)
 
 
-def scan_window(element, flag, step, ident, side_work=no_side_work, side_inputs=(), side_shapes=()):
+def forward_element(cut_ref, key_ref, value_ref, element_ref):
+    rows = key_ref.shape[0]
+    keep = lax.broadcasted_iota(jnp.int32, (rows, HD), 0) >= cut_ref[0]
+    size = HD // PIECES
+    for part in range(key_ref.shape[1] // HD):
+        cols = pl.ds(part * HD, HD)
+        kept = jnp.where(keep, key_ref[:, cols].astype(jnp.float32), 0.0).T.astype(jnp.bfloat16)
+        block = jnp.dot(kept, value_ref[:, cols], preferred_element_type=jnp.float32)
+        for piece in range(PIECES):
+            element_ref[part * PIECES + piece] = block[piece * size:(piece + 1) * size, :]
+
+
+def scan_window(element, flag, step, ident, side_work=no_side_work, side_inputs=(), side_shapes=(),
+                prologue=None, prologue_inputs=(), shape=None):
     count = lax.axis_size("seq")
-    shape = element.shape
-    element = element.reshape(shape[0] * PIECES, shape[1] // PIECES, shape[2])
-    heads = element.shape[0]
+    shape = element.shape if element is not None else shape
+    chunked = (shape[0] * PIECES, shape[1] // PIECES, shape[2])
+    heads = chunked[0]
     vmem = pl.BlockSpec(memory_space=pltpu.VMEM)
+    smem = pl.BlockSpec(memory_space=pltpu.SMEM)
+    scratch = [
+        pltpu.VMEM(chunked, jnp.float32),
+        pltpu.VMEM(chunked, jnp.float32),
+        pltpu.VMEM(chunked, jnp.float32),
+        pltpu.SemaphoreType.DMA((2, heads)),
+        pltpu.SemaphoreType.DMA((2, heads)),
+    ]
+    if prologue is None:
+        leading = (element.reshape(chunked),)
+        leading_specs = [vmem]
+    else:
+        leading = ()
+        leading_specs = []
+        scratch.append(pltpu.VMEM(chunked, jnp.float32))
+    pro_specs = [smem] + [vmem] * (len(prologue_inputs) - 1) if prologue_inputs else []
     outs = pl.pallas_call(
-        functools.partial(chain_kernel, count, step, side_work, len(side_inputs)),
-        out_shape=(jax.ShapeDtypeStruct(element.shape, jnp.float32),) + tuple(side_shapes),
-        in_specs=[pl.BlockSpec(memory_space=pltpu.SMEM)] + [vmem] * (1 + len(side_inputs)),
+        functools.partial(chain_kernel, count, step, side_work, len(side_inputs), prologue, len(prologue_inputs)),
+        out_shape=(jax.ShapeDtypeStruct(chunked, jnp.float32),) + tuple(side_shapes),
+        in_specs=[smem] + leading_specs + pro_specs + [vmem] * len(side_inputs),
         out_specs=(vmem,) * (1 + len(side_shapes)),
-        scratch_shapes=[
-            pltpu.VMEM(element.shape, jnp.float32),
-            pltpu.VMEM(element.shape, jnp.float32),
-            pltpu.VMEM(element.shape, jnp.float32),
-            pltpu.SemaphoreType.DMA((2, heads)),
-            pltpu.SemaphoreType.DMA((2, heads)),
-        ],
+        scratch_shapes=scratch,
         compiler_params=pltpu.CompilerParams(collective_id=ident, has_side_effects=True),
-    )(flag.astype(jnp.float32).reshape(1), element, *side_inputs)
+    )(flag.astype(jnp.float32).reshape(1), *leading, *prologue_inputs, *side_inputs)
     return (outs[0].reshape(shape),) + tuple(outs[1:])
 
 def head_sum_kernel(count, parts_ref, out_ref, slots, send_sems, recv_sems):
@@ -317,14 +350,12 @@
     key_h = key_rows.reshape(token_count, head_count, HD)
     value_h = value_rows.reshape(token_count, head_count, HD)
     last_start = dial_start[token_count - 1]
-    keep_last = position >= last_start
-    element = jnp.einsum(
-        "shd,she->hde",
-        jnp.where(keep_last[:, None, None], key_h, jnp.zeros((), jnp.bfloat16)),
-        value_h,
-        preferred_element_type=jnp.float32,
-    )
-    carried = scan_window(element, last_start < block_begin, 1, 0)[0]
+    carried = scan_window(
+        None, last_start < block_begin, 1, 0,
+        prologue=lambda refs, out: forward_element(*refs, out),
+        prologue_inputs=((last_start - block_begin).reshape(1), key_rows, value_rows),
+        shape=(head_count, HD, HD),
+    )[0]
     carried, query_h, key_h, value_h = lax.optimization_barrier((carried, query_h, key_h, value_h))
     inside = (position[None, :] >= dial_start[:, None]) & (local_pos[None, :] <= local_pos[:, None])
     scores = jnp.einsum("thd,shd->hts", query_h, key_h, preferred_element_type=jnp.float32)

time: 112 us -> 111 us (level)
    unnamed x21 -> x19, local copies, waits for them, and re-layouts: 4.41 us -> 4.58 us
where the time goes in v16:
time: 111 us
  Pallas kernels  97.3 us (88%)
  local copies, waits for them, and re-layouts  5.67 us (5%)
  other arithmetic  3.3 us (3%)
  matrix products  2.18 us (2%)
  between operations  2.16 us (2%)
    pallas_call x2, Pallas kernels, scan_window(): pl.pallas_call(functools.partial(chain_kernel, count, step, side_work, le...  85.4 us
    pallas_call x1, Pallas kernels, head_sum(): pl.pallas_call(functools.partial(head_sum_kernel, count), out_shape=jax.S...  8.04 us
    unnamed x19, local copies, waits for them, and re-layouts  4.58 us
    pallas_call x1, Pallas kernels, gradients(): pl.pallas_call(functools.partial(gradient_kernel, scale), out_shape=(flat...  3.86 us

profile of v16, /device:TPU:16, one launch (start us, length us, event | category | flops | bytes accessed | tf_op | source)
XLA Modules:
  0.0 110.7 jit_solution(7808026105633969272)
XLA Ops:
  0.6 0.0 copy-start.6
  0.7 0.6 copy-done.6
  1.3 0.6 slice.12
  3.2 0.0 copy-start.7
  3.2 0.6 copy-done.7
  4.0 0.1 pad.2.clone
  4.0 0.1 fusion.25
  4.1 0.0 copy-start.1
  4.1 1.0 copy.26
  5.2 0.0 copy-done.1
  5.2 0.0 copy-start.3
  5.3 0.9 copy-done.3
  6.2 46.5 %shard_map.102 = f32[32,32,128]{2,1,0:T(8,128)} custom-call(f32[1]{0:T(128)} %bitcast.1.flag_ref, s32[1]{0:T(128)} %bitcast.2.refs_0_, bf16[128,1024]{1,0:T(8,128)(2,1)} %key_ref.1, bf16[128,1024]{1,0:T(8,128)(2,1)} %value_ref.1), custom_call_target="tpu_custom_call" | custom-call | tf_op jit(solution)/shard_map/pallas_call | solution.py:204
  52.7 0.2 copy.17
  52.9 0.0 copy-start
  52.9 0.5 fusion.4
  53.5 0.5 copy-done
  54.0 0.3 fusion.23
  54.3 0.4 fusion.9
  54.6 0.0 copy-start.4
  54.6 0.0 copy-start.5
  54.6 0.2 copy.22
  54.8 0.7 copy-done.4
  55.6 0.0 copy-done.5
  55.6 0.2 fusion.6
  55.7 0.7 maximum_maximum_fusion.parts_ref
  56.4 8.0 %shard_map.103 = f32[8,128]{1,0:T(8,128)} custom-call(f32[8,128]{1,0:T(8,128)} %maximum_maximum_fusion.parts_ref), custom_call_target="tpu_custom_call" | custom-call | tf_op jit(solution)/shard_map/pallas_call | solution.py:259
  64.4 0.8 fusion.27
  65.2 0.7 rsqrt_bitcast_fusion
  65.9 0.9 fusion.8
  66.8 0.0 copy-start.2
  66.8 1.0 fusion.10
  67.8 0.0 copy-done.2
  67.8 38.9 %shard_map.104 = (f32[32,32,128]{2,1,0:T(8,128)}, f32[128,1024]{1,0:T(8,128)}, f32[128,1024]{1,0:T(8,128)}, f32[128,1024]{1,0:T(8,128)}) custom-call(f32[1]{0:T(128)} %bitcast.14.flag_ref, f32[32,32,128]{2,1,0:T(8,128)} %bitcast.50, bf16[128,1024]{1,0:T(8,128)(2,1)} %query_ref.1, bf16[128,1024]{1,0:T(8,128)(2,1)} %key_ref.1, bf16[128,1024]{1,0:T(8,128)(2,1)} %value_ref.1, ...), custom_call_target="tpu_custom_call" | custom-call | tf_op jit(solution)/shard_map/pallas_call | solution.py:204
  106.8 3.9 %shard_map.105 = (bf16[128,1024]{1,0:T(8,128)(2,1)}, bf16[128,1024]{1,0:T(8,128)(2,1)}, bf16[128,1024]{1,0:T(8,128)(2,1)}) custom-call(bf16[128,1024]{1,0:T(8,128)(2,1)} %query_ref.1, bf16[128,1024]{1,0:T(8,128)(2,1)} %key_ref.1, bf16[128,1024]{1,0:T(8,128)(2,1)} %value_ref.1, bf16[128,1024]{1,0:T(8,128)(2,1)} %copy-done.2, s32[1,128]{1,0:T(1,128)} %bitcast.56, ...), custom_call_target="tpu_custom_call" | custom-call | tf_op jit(solution)/shard_map/pallas_call | solution.py:315
  (6 shorter events, 0.1 us)
Async XLA Ops:
  0.6 0.7 copy-start.6
  3.2 0.7 copy-start.7
  4.1 1.1 copy-start.1
  5.2 1.0 copy-start.3
  52.9 1.0 copy-start
  54.6 1.0 copy-start.4
  54.6 1.0 copy-start.5
  66.8 1.0 copy-start.2

commit v17 on v16

--- a/solution.py
+++ b/solution.py
@@ -166,9 +166,10 @@
         value_out[:, cols] = jnp.dot(scaled.T.astype(jnp.bfloat16), grad_h, preferred_element_type=jnp.float32)
 
 
-def forward_element(cut_ref, key_ref, value_ref, element_ref):
+def forward_element(cut_ref, key_ref, value_ref, element_ref, below=False):
     rows = key_ref.shape[0]
-    keep = lax.broadcasted_iota(jnp.int32, (rows, HD), 0) >= cut_ref[0]
+    index = lax.broadcasted_iota(jnp.int32, (rows, HD), 0)
+    keep = index < cut_ref[0] if below else index >= cut_ref[0]
     size = HD // PIECES
     for part in range(key_ref.shape[1] // HD):
         cols = pl.ds(part * HD, HD)
@@ -377,19 +378,16 @@
     grad_weight = grad_attn.astype(jnp.bfloat16).reshape(token_count, head_count, HD)
     first_end = dial_end[0]
     keep_first = position < first_end
-    back_element = jnp.einsum(
-        "thd,the->hde",
-        jnp.where(keep_first[:, None, None], query_h, jnp.zeros((), jnp.bfloat16)),
-        grad_weight,
-        preferred_element_type=jnp.float32,
-    )
     wide_shape = jax.ShapeDtypeStruct(queries.shape, jnp.float32)
     grad_flat = grad_weight.reshape(queries.shape)
     returned, *local = scan_window(
-        back_element, first_end > block_begin + token_count, -1, 1,
+        None, first_end > block_begin + token_count, -1, 1,
         functools.partial(backward_local, score_scale),
         (queries, key_rows, value_rows, grad_flat, dial_start.reshape(1, token_count)),
         (wide_shape,) * 3,
+        prologue=lambda refs, out: forward_element(*refs, out, below=True),
+        prologue_inputs=((first_end - block_begin).reshape(1), queries, grad_flat),
+        shape=(head_count, HD, HD),
     )
     query_grad, key_grad, value_grad = gradients(
         score_scale, queries, key_rows, value_rows, grad_flat,

time: 111 us -> 110 us (level)
    unnamed x19 -> x17, local copies, waits for them, and re-layouts: 4.58 us -> 4.59 us
where the time goes in v17:
time: 110 us
  Pallas kernels  97.7 us (89%)
  local copies, waits for them, and re-layouts  5.45 us (5%)
  other arithmetic  3.34 us (3%)
  between operations  2.18 us (2%)
  matrix products  1.18 us (1%)
    pallas_call x2, Pallas kernels, scan_window(): pl.pallas_call(functools.partial(chain_kernel, count, step, side_work, le...  85.8 us
    pallas_call x1, Pallas kernels, head_sum(): pl.pallas_call(functools.partial(head_sum_kernel, count), out_shape=jax.S...  8.03 us
    unnamed x17, local copies, waits for them, and re-layouts  4.59 us
    pallas_call x1, Pallas kernels, gradients(): pl.pallas_call(functools.partial(gradient_kernel, scale), out_shape=(flat...  3.86 us

profile of v17, /device:TPU:16, one launch (start us, length us, event | category | flops | bytes accessed | tf_op | source)
XLA Modules:
  0.0 109.8 jit_solution(5998184010006835568)
XLA Ops:
  0.6 0.0 copy-start.5
  0.7 0.6 copy-done.5
  1.3 0.6 slice.12
  3.2 0.0 copy-start.6
  3.2 0.6 copy-done.6
  3.9 0.1 pad.2.clone
  4.0 0.1 fusion.23
  4.1 0.0 copy-start.1
  4.1 1.0 copy.23
  5.2 0.0 copy-done.1
  5.2 0.0 copy-start.2
  5.2 0.9 copy-done.2
  6.2 46.5 %shard_map.102 = f32[32,32,128]{2,1,0:T(8,128)} custom-call(f32[1]{0:T(128)} %bitcast.1.flag_ref, s32[1]{0:T(128)} %bitcast.2.refs_0_, bf16[128,1024]{1,0:T(8,128)(2,1)} %key_ref.1, bf16[128,1024]{1,0:T(8,128)(2,1)} %value_ref.1), custom_call_target="tpu_custom_call" | custom-call | tf_op jit(solution)/shard_map/pallas_call | solution.py:205
  52.7 0.0 copy-start
  52.7 0.5 fusion.4
  53.2 0.5 copy-done
  53.7 0.3 fusion.19
  54.1 0.4 fusion.9
  54.4 0.0 copy-start.3
  54.4 0.0 copy-start.4
  54.4 0.2 copy.20
  54.6 0.7 copy-done.3
  55.4 0.0 copy-done.4
  55.4 0.2 fusion.6
  55.5 0.7 maximum_maximum_fusion.parts_ref
  56.2 8.0 %shard_map.103 = f32[8,128]{1,0:T(8,128)} custom-call(f32[8,128]{1,0:T(8,128)} %maximum_maximum_fusion.parts_ref), custom_call_target="tpu_custom_call" | custom-call | tf_op jit(solution)/shard_map/pallas_call | solution.py:260
  64.2 0.8 fusion.25
  65.0 0.7 rsqrt_bitcast_fusion
  65.6 1.0 fusion.8
  66.7 39.3 %shard_map.104 = (f32[32,32,128]{2,1,0:T(8,128)}, f32[128,1024]{1,0:T(8,128)}, f32[128,1024]{1,0:T(8,128)}, f32[128,1024]{1,0:T(8,128)}) custom-call(f32[1]{0:T(128)} %bitcast.14.flag_ref, s32[1]{0:T(128)} %bitcast.15.refs_0_, bf16[128,1024]{1,0:T(8,128)(2,1)} %query_ref.1, bf16[128,1024]{1,0:T(8,128)(2,1)} %get-tuple-element.26.refs_2_.refs_6_.grad_ref, ...), custom_call_target="tpu_custom_call" | custom-call | tf_op jit(solution)/shard_map/pallas_call | solution.py:205
  105.9 3.9 %shard_map.105 = (bf16[128,1024]{1,0:T(8,128)(2,1)}, bf16[128,1024]{1,0:T(8,128)(2,1)}, bf16[128,1024]{1,0:T(8,128)(2,1)}) custom-call(bf16[128,1024]{1,0:T(8,128)(2,1)} %query_ref.1, bf16[128,1024]{1,0:T(8,128)(2,1)} %key_ref.1, bf16[128,1024]{1,0:T(8,128)(2,1)} %value_ref.1, bf16[128,1024]{1,0:T(8,128)(2,1)} %get-tuple-element.26.refs_2_.refs_6_.grad_ref, ...), custom_call_target="tpu_custom_call" | custom-call | tf_op jit(solution)/shard_map/pallas_call | solution.py:316
  (5 shorter events, 0.1 us)
Async XLA Ops:
  0.6 0.7 copy-start.5
  3.2 0.7 copy-start.6
  4.1 1.1 copy-start.1
  5.2 1.0 copy-start.2
  52.7 1.0 copy-start
  54.4 1.0 copy-start.3
  54.4 1.0 copy-start.4

commit v18 on v17

--- a/solution.py
+++ b/solution.py
@@ -141,13 +141,14 @@
 
 
 def backward_local(scale, side_in, side_out):
-    query_ref, key_ref, value_ref, grad_ref, starts_ref = side_in
+    query_ref, key_ref, value_ref, grad_ref, starts_ref, carried_ref = side_in
     query_out, key_out, value_out = side_out
     rows = query_ref.shape[0]
     row = lax.broadcasted_iota(jnp.int32, (rows, rows), 0)
     col = lax.broadcasted_iota(jnp.int32, (rows, rows), 1)
     begin = lax.axis_index("seq") * rows
     starts = jnp.broadcast_to(starts_ref[...], (rows, rows)).T
+    before = (starts < begin).astype(jnp.float32)
     inside = (begin + col >= starts) & (col <= row)
     contract_last = (((1,), (1,)), ((), ()))
     for part in range(query_ref.shape[1] // HD):
@@ -161,7 +162,13 @@
             grad_h, value_ref[:, cols], contract_last, preferred_element_type=jnp.float32
         )
         mixed = jnp.where(inside, scale * grad_scores, 0.0)
-        query_out[:, cols] = jnp.dot(mixed.astype(jnp.bfloat16), key_h, preferred_element_type=jnp.float32)
+        upper = carried_ref[part].astype(jnp.bfloat16)
+        lower = (carried_ref[part] - upper.astype(jnp.float32)).astype(jnp.bfloat16)
+        across = lax.dot_general(grad_h, upper, contract_last, preferred_element_type=jnp.float32)
+        across = across + lax.dot_general(grad_h, lower, contract_last, preferred_element_type=jnp.float32)
+        query_out[:, cols] = jnp.dot(
+            mixed.astype(jnp.bfloat16), key_h, preferred_element_type=jnp.float32
+        ) + before * scale * across
         key_out[:, cols] = jnp.dot(mixed.T.astype(jnp.bfloat16), query_h, preferred_element_type=jnp.float32)
         value_out[:, cols] = jnp.dot(scaled.T.astype(jnp.bfloat16), grad_h, preferred_element_type=jnp.float32)
 
@@ -297,9 +304,7 @@
         cols = pl.ds(part * HD, HD)
         carried = carried_ref[part]
         returned = returned_ref[part]
-        query_out[:, cols] = (
-            query_local[:, cols] + before * scale * across(grad_ref[:, cols], carried, "nt")
-        ).astype(jnp.bfloat16)
+        query_out[:, cols] = query_local[:, cols].astype(jnp.bfloat16)
         key_out[:, cols] = (
             key_local[:, cols] + after * scale * across(value_ref[:, cols], returned, "nt")
         ).astype(jnp.bfloat16)
@@ -383,7 +388,7 @@
     returned, *local = scan_window(
         None, first_end > block_begin + token_count, -1, 1,
         functools.partial(backward_local, score_scale),
-        (queries, key_rows, value_rows, grad_flat, dial_start.reshape(1, token_count)),
+        (queries, key_rows, value_rows, grad_flat, dial_start.reshape(1, token_count), carried),
         (wide_shape,) * 3,
         prologue=lambda refs, out: forward_element(*refs, out, below=True),
         prologue_inputs=((first_end - block_begin).reshape(1), queries, grad_flat),

time: 110 us -> 110 us (level)
  no operation moved by 1% of the time
where the time goes in v18:
time: 110 us
  Pallas kernels  97.4 us (89%)
  local copies, waits for them, and re-layouts  5.45 us (5%)
  other arithmetic  3.34 us (3%)
  between operations  2.18 us (2%)
  matrix products  1.18 us (1%)
    pallas_call x2, Pallas kernels, scan_window(): pl.pallas_call(functools.partial(chain_kernel, count, step, side_work, le...  85.9 us
    pallas_call x1, Pallas kernels, head_sum(): pl.pallas_call(functools.partial(head_sum_kernel, count), out_shape=jax.S...  8.03 us
    unnamed x17, local copies, waits for them, and re-layouts  4.59 us
    pallas_call x1, Pallas kernels, gradients(): pl.pallas_call(functools.partial(gradient_kernel, scale), out_shape=(flat...  3.51 us

profile of v18, /device:TPU:16, one launch (start us, length us, event | category | flops | bytes accessed | tf_op | source)
XLA Modules:
  0.0 109.6 jit_solution(6026300297250003585)
XLA Ops:
  0.6 0.0 copy-start.5
  0.7 0.6 copy-done.5
  1.3 0.6 slice.12
  3.2 0.0 copy-start.6
  3.2 0.6 copy-done.6
  3.9 0.1 pad.2.clone
  4.0 0.1 fusion.23
  4.1 0.0 copy-start.1
  4.1 1.0 copy.23
  5.2 0.0 copy-done.1
  5.2 0.0 copy-start.2
  5.2 0.9 copy-done.2
  6.2 46.5 %shard_map.102 = f32[32,32,128]{2,1,0:T(8,128)} custom-call(f32[1]{0:T(128)} %bitcast.1.flag_ref, s32[1]{0:T(128)} %bitcast.2.refs_0_, bf16[128,1024]{1,0:T(8,128)(2,1)} %key_ref.1, bf16[128,1024]{1,0:T(8,128)(2,1)} %value_ref.1), custom_call_target="tpu_custom_call" | custom-call | tf_op jit(solution)/shard_map/pallas_call | solution.py:212
  52.7 0.0 copy-start
  52.7 0.5 fusion.4
  53.2 0.5 copy-done
  53.7 0.3 fusion.19
  54.1 0.4 fusion.9
  54.4 0.0 copy-start.3
  54.4 0.0 copy-start.4
  54.4 0.2 copy.20
  54.6 0.7 copy-done.3
  55.4 0.0 copy-done.4
  55.4 0.2 fusion.6
  55.5 0.7 maximum_maximum_fusion.parts_ref
  56.2 8.0 %shard_map.103 = f32[8,128]{1,0:T(8,128)} custom-call(f32[8,128]{1,0:T(8,128)} %maximum_maximum_fusion.parts_ref), custom_call_target="tpu_custom_call" | custom-call | tf_op jit(solution)/shard_map/pallas_call | solution.py:267
  64.2 0.8 fusion.25
  65.0 0.7 rsqrt_bitcast_fusion
  65.6 1.0 fusion.8
  66.7 39.4 %shard_map.104 = (f32[32,32,128]{2,1,0:T(8,128)}, f32[128,1024]{1,0:T(8,128)}, f32[128,1024]{1,0:T(8,128)}, f32[128,1024]{1,0:T(8,128)}) custom-call(f32[1]{0:T(128)} %bitcast.14.flag_ref, s32[1]{0:T(128)} %bitcast.15.refs_0_, bf16[128,1024]{1,0:T(8,128)(2,1)} %query_ref.1, bf16[128,1024]{1,0:T(8,128)(2,1)} %get-tuple-element.26.refs_2_.refs_6_.grad_ref, ...), custom_call_target="tpu_custom_call" | custom-call | tf_op jit(solution)/shard_map/pallas_call | solution.py:212
  106.1 3.5 %shard_map.105 = (bf16[128,1024]{1,0:T(8,128)(2,1)}, bf16[128,1024]{1,0:T(8,128)(2,1)}, bf16[128,1024]{1,0:T(8,128)(2,1)}) custom-call(bf16[128,1024]{1,0:T(8,128)(2,1)} %query_ref.1, bf16[128,1024]{1,0:T(8,128)(2,1)} %key_ref.1, bf16[128,1024]{1,0:T(8,128)(2,1)} %value_ref.1, bf16[128,1024]{1,0:T(8,128)(2,1)} %get-tuple-element.26.refs_2_.refs_6_.grad_ref, ...), custom_call_target="tpu_custom_call" | custom-call | tf_op jit(solution)/shard_map/pallas_call | solution.py:321
  (5 shorter events, 0.1 us)
Async XLA Ops:
  0.6 0.7 copy-start.5
  3.2 0.7 copy-start.6
  4.1 1.1 copy-start.1
  5.2 1.0 copy-start.2
  52.7 1.0 copy-start
  54.4 1.0 copy-start.3
  54.4 1.0 copy-start.4
